TPU v7x, 32 devices: a whole 2x2x4 slice. The times are simulated.
32 devices in a mesh: dp: 8 (over z, core), group: 4 (over y, x).
Axes of the slice: x: 2, y: 2, z: 4, core: 2. Of those that a mesh axis runs over, the one named last changes fastest.
Arguments:
- tokens: bfloat16 [32768, 1024], P(('dp', 'group')), may hold values from -6 to 6
- cotangent: bfloat16 [32768, 1024], P(('dp', 'group')), may hold values from -6 to 6
- doc_ids: int32 [32768], P(('dp', 'group')), may hold values from -1 to 3, as said below
- master: float32 [12587008], P('group')
- moment_one: float32 [12587008], P('group'), may hold values from -2 to 2
- moment_two: float32 [12587008], P('group'), may hold values from 0.001 to 1
Outputs:
- mixed: bfloat16 [32768, 1024], P(('dp', 'group'))
- input_grad: bfloat16 [32768, 1024], P(('dp', 'group'))
- weight_grad: float32 [12587008], P('group')
- master_step: float32 [12587008], P('group')
- new_moment_one: float32 [12587008], P('group')
Inputs may be any that keep to these rules, and one draw needn't show every extreme that they name: `doc_ids`: each device's block of 1024 slots holds one to four sequences numbered 0, 1, ... in order, each of 16 tokens or more, followed by padding slots of -1 at its end; some device holds a single sequence of 1024 tokens and some device holds four.
All inputs are finite; a program needn't handle non-finite values.
Results may differ from a plain program's by a relative error of at most 0.012.
Values may be sent and summed in bfloat16 or wider, within the bound.
A program may use at most 384 MiB of HBM per device.

v0:
```python
import jax
import jax.numpy as jnp
from jax import lax
from jax.sharding import PartitionSpec as P

H = 16
FF = 4096


norm_eps = 1e-05
mask_fill = -1e30
beta_first = 0.9
beta_second = 0.999
learn_rate = 0.001
adam_eps = 1e-08
adam_steps = 100.0


def layer_norm(values, gain, bias):
    centre = values - jnp.mean(values, axis=-1, keepdims=True)
    spread = jnp.mean(centre * centre, axis=-1, keepdims=True)
    return centre * lax.rsqrt(spread + norm_eps) * gain + bias


def exact_gelu(values):
    return jax.nn.gelu(values, approximate=False)


def param_shapes(model_width, hidden_width):
    return [
        (model_width, 3 * model_width),
        (model_width, model_width),
        (model_width, hidden_width),
        (hidden_width, model_width),
        (4, model_width),
    ]


def shard_pieces(shard, shapes, group_count):
    pieces = []
    offset = 0
    for shape in shapes:
        length = shape[0] * shape[1] // group_count
        pieces.append(lax.slice_in_dim(shard, offset, offset + length))
        offset = offset + length
    return pieces


def split_heads(packed):
    token_count, model_width = packed.shape
    return packed.reshape(token_count, H, model_width // H)


def block_mask(doc_ids, start, block):
    key_pos = jnp.arange(doc_ids.shape[0], dtype=jnp.int32)
    query_pos = start + jnp.arange(block, dtype=jnp.int32)
    query_doc = lax.dynamic_slice_in_dim(doc_ids, start, block, 0)
    return (query_doc[:, None] == doc_ids[None, :]) & (key_pos[None, :] <= query_pos[:, None])


def attention_forward(qkv, doc_ids):
    token_count = qkv.shape[0]
    model_width = qkv.shape[1] // 3
    queries = split_heads(qkv[:, :model_width])
    keys_all = split_heads(qkv[:, model_width : 2 * model_width])
    values_all = split_heads(qkv[:, 2 * model_width :])
    factor = (model_width // H) ** (-0.5)
    block = min(512, token_count)

    def one_block(blk_index):
        start = blk_index * block
        query_blk = lax.dynamic_slice_in_dim(queries, start, block, 0)
        allowed = block_mask(doc_ids, start, block)
        scores = (
            jnp.einsum("qhd,khd->hqk", query_blk, keys_all, preferred_element_type=jnp.float32)
            * factor
        )
        scores = jnp.where(allowed[None], scores, mask_fill)
        top_score = jnp.max(scores, axis=-1, keepdims=True)
        exp_scores = jnp.exp(scores - top_score)
        totals = jnp.sum(exp_scores, axis=-1, keepdims=True)
        prob_low = (exp_scores / totals).astype(jnp.bfloat16)
        head_out = jnp.einsum(
            "hqk,khd->qhd", prob_low, values_all, preferred_element_type=jnp.float32
        )
        return (head_out.astype(jnp.bfloat16), (top_score + jnp.log(totals))[..., 0])

    outputs, log_totals = lax.map(one_block, jnp.arange(token_count // block, dtype=jnp.int32))
    return (outputs.reshape(token_count, model_width), log_totals)


def attention_backward(qkv, d_att, log_totals, doc_ids):
    token_count = qkv.shape[0]
    model_width = qkv.shape[1] // 3
    queries = split_heads(qkv[:, :model_width])
    keys_all = split_heads(qkv[:, model_width : 2 * model_width])
    values_all = split_heads(qkv[:, 2 * model_width :])
    out_grads = split_heads(d_att)
    factor = (model_width // H) ** (-0.5)
    block = min(512, token_count)

    def one_block(carry, blk_index):
        key_grad, value_grad = carry
        start = blk_index * block
        query_blk = lax.dynamic_slice_in_dim(queries, start, block, 0)
        outgrad_blk = lax.dynamic_slice_in_dim(out_grads, start, block, 0)
        allowed = block_mask(doc_ids, start, block)
        scores = (
            jnp.einsum("qhd,khd->hqk", query_blk, keys_all, preferred_element_type=jnp.float32)
            * factor
        )
        scores = jnp.where(allowed[None], scores, mask_fill)
        lse_blk = lax.dynamic_index_in_dim(log_totals, blk_index, 0, keepdims=False)
        prob_full = jnp.exp(scores - lse_blk[..., None])
        prob_low = prob_full.astype(jnp.bfloat16)
        prob_grad = jnp.einsum(
            "qhd,khd->hqk", outgrad_blk, values_all, preferred_element_type=jnp.float32
        )
        inner = jnp.sum(prob_full * prob_grad, axis=-1, keepdims=True)
        score_grad = (prob_full * (prob_grad - inner)).astype(jnp.bfloat16)
        query_grad = (
            jnp.einsum("hqk,khd->qhd", score_grad, keys_all, preferred_element_type=jnp.float32)
            * factor
        )
        key_grad = (
            key_grad
            + jnp.einsum("hqk,qhd->khd", score_grad, query_blk, preferred_element_type=jnp.float32)
            * factor
        )
        value_grad = value_grad + jnp.einsum(
            "hqk,qhd->khd", prob_low, outgrad_blk, preferred_element_type=jnp.float32
        )
        return ((key_grad, value_grad), query_grad)

    empty = jnp.zeros(queries.shape, jnp.float32)
    (key_grad, value_grad), query_grads = lax.scan(
        one_block, (empty, empty), jnp.arange(token_count // block, dtype=jnp.int32)
    )
    return jnp.concatenate(
        [
            query_grads.reshape(token_count, model_width),
            key_grad.reshape(token_count, model_width),
            value_grad.reshape(token_count, model_width),
        ],
        axis=1,
    )


def body(tokens, cotangent, doc_ids, master, moment_one, moment_two):
    group_count = lax.axis_size("group")
    replica_count = lax.axis_size("dp")
    token_count, model_width = tokens.shape
    shapes = param_shapes(model_width, FF)
    pieces = shard_pieces(master.astype(jnp.bfloat16), shapes, group_count)
    gathered = (
        lax.all_gather(pieces[0], "group", axis=0, tiled=True),
        lax.all_gather(pieces[1], "group", axis=0, tiled=True),
        lax.all_gather(pieces[2], "group", axis=0, tiled=True),
        lax.all_gather(pieces[3], "group", axis=0, tiled=True),
        lax.all_gather(pieces[4], "group", axis=0, tiled=True),
    )
    w_qkv, w_out, w_in, w_back, norm_low = [
        tensor.reshape(shape) for tensor, shape in zip(gathered, shapes)
    ]
    norm_params = norm_low.astype(jnp.float32)
    token_full = tokens.astype(jnp.float32)
    valid = (doc_ids >= 0)[:, None]
    a_one = layer_norm(token_full, norm_params[0], norm_params[1]).astype(jnp.bfloat16)
    qkv = jnp.dot(a_one, w_qkv, preferred_element_type=jnp.float32).astype(jnp.bfloat16)
    att, log_totals = attention_forward(qkv, doc_ids)
    resid = token_full + jnp.dot(att, w_out, preferred_element_type=jnp.float32)
    a_two = layer_norm(resid, norm_params[2], norm_params[3]).astype(jnp.bfloat16)
    pre_act = jnp.dot(a_two, w_in, preferred_element_type=jnp.float32)
    hidden = exact_gelu(pre_act).astype(jnp.bfloat16)
    output = resid + jnp.dot(hidden, w_back, preferred_element_type=jnp.float32)
    mixed = jnp.where(valid, output, 0.0).astype(jnp.bfloat16)
    regathered = (
        lax.all_gather(pieces[0], "group", axis=0, tiled=True),
        lax.all_gather(pieces[1], "group", axis=0, tiled=True),
        lax.all_gather(pieces[2], "group", axis=0, tiled=True),
        lax.all_gather(pieces[3], "group", axis=0, tiled=True),
        lax.all_gather(pieces[4], "group", axis=0, tiled=True),
    )
    w_qkv, w_out, w_in, w_back, norm_low = [
        tensor.reshape(shape) for tensor, shape in zip(regathered, shapes)
    ]
    norm_params = norm_low.astype(jnp.float32)
    d_out = jnp.where(valid, cotangent.astype(jnp.float32), 0.0)
    d_out_low = d_out.astype(jnp.bfloat16)
    grad_back = jnp.einsum("tf,td->fd", hidden, d_out_low, preferred_element_type=jnp.float32)
    d_hidden = jnp.einsum("td,fd->tf", d_out_low, w_back, preferred_element_type=jnp.float32)
    gelu_pull = jax.vjp(exact_gelu, pre_act)[1]
    d_pre = gelu_pull(d_hidden)[0].astype(jnp.bfloat16)
    grad_in = jnp.einsum("td,tf->df", a_two, d_pre, preferred_element_type=jnp.float32)
    d_two = jnp.einsum("tf,df->td", d_pre, w_in, preferred_element_type=jnp.float32)
    second_pull = jax.vjp(layer_norm, resid, norm_params[2], norm_params[3])[1]
    resid_part, gain_two, bias_two = second_pull(d_two)
    d_resid = d_out + resid_part
    d_resid_low = d_resid.astype(jnp.bfloat16)
    grad_out = jnp.einsum("td,te->de", att, d_resid_low, preferred_element_type=jnp.float32)
    d_att = jnp.einsum("te,de->td", d_resid_low, w_out, preferred_element_type=jnp.float32).astype(
        jnp.bfloat16
    )
    d_qkv = attention_backward(qkv, d_att, log_totals, doc_ids).astype(jnp.bfloat16)
    grad_qkv = jnp.einsum("td,te->de", a_one, d_qkv, preferred_element_type=jnp.float32)
    d_one = jnp.einsum("te,de->td", d_qkv, w_qkv, preferred_element_type=jnp.float32)
    first_pull = jax.vjp(layer_norm, token_full, norm_params[0], norm_params[1])[1]
    input_part, gain_one, bias_one = first_pull(d_one)
    input_grad = (d_resid + input_part).astype(jnp.bfloat16)
    grad_norms = jnp.stack([gain_one, bias_one, gain_two, bias_two])
    inv_root = float(token_count * group_count * replica_count) ** (-0.5)
    flat_grads = [
        (tensor * inv_root).reshape(-1)
        for tensor in (grad_qkv, grad_out, grad_in, grad_back, grad_norms)
    ]
    owned = (
        lax.psum_scatter(flat_grads[0], "group", scatter_dimension=0, tiled=True),
        lax.psum_scatter(flat_grads[1], "group", scatter_dimension=0, tiled=True),
        lax.psum_scatter(flat_grads[2], "group", scatter_dimension=0, tiled=True),
        lax.psum_scatter(flat_grads[3], "group", scatter_dimension=0, tiled=True),
        lax.psum_scatter(flat_grads[4], "group", scatter_dimension=0, tiled=True),
    )
    summed = lax.psum((owned[0], owned[1], owned[2], owned[3], owned[4]), "dp")
    grad_shard = jnp.concatenate([tensor for tensor in summed])
    first_new = beta_first * moment_one + (1.0 - beta_first) * grad_shard
    second_new = beta_second * moment_two + (1.0 - beta_second) * grad_shard * grad_shard
    first_hat = first_new / (1.0 - beta_first**adam_steps)
    second_hat = second_new / (1.0 - beta_second**adam_steps)
    step_taken = -learn_rate * first_hat / (jnp.sqrt(second_hat) + adam_eps)
    return (mixed, input_grad, grad_shard, step_taken, first_new)


def solution(mesh):
    in_specs = (
        P(("dp", "group"), None),
        P(("dp", "group"), None),
        P(("dp", "group")),
        P("group"),
        P("group"),
        P("group"),
    )
    out_specs = (
        P(("dp", "group"), None),
        P(("dp", "group"), None),
        P("group"),
        P("group"),
        P("group"),
    )
    return jax.shard_map(body, mesh=mesh, in_specs=in_specs, out_specs=out_specs, check_vma=False)
```

profile of v0, /device:TPU:0, one launch (start us, length us, event | category | flops | bytes accessed | tf_op | source)
XLA Modules:
  0.0 1886.6 jit_solution(3403308118956380638)
XLA Ops:
  7.2 5.3 convert_element_type.61
  27.0 9.6 all_gather.20
  43.3 10.9 all-gather.7.cloned.1.call-done
  58.4 68.5 %all-gather.5.cloned.1.call-done = bf16[3145728]{0:T(1024)(128)(2,1)} async-done(((bf16[786432]{0:T(1024)(128)(2,1)}), bf16[3145728]{0:T(1024)(128)(2,1)}) %all-gather.5.cloned.1.call-update) | async-done | bytes 6291472 | tf_op jit(solution)/shard_map/all_gather | solution.py:156
  126.8 10.4 reshape.282
  137.3 11.1 convolution_convert_fusion
  160.7 100.6 %while.27 = (s32[]{:T(128)}, bf16[2,512,16,64]{1,3,2,0:T(8,128)(2,1)}, f32[2,16,512]{2,1,0:T(8,128)S(1)}, s32[2]{0:T(128)S(1)}, s32[1024]{0:T(1024)S(1)}, /*inde...) while((s32[]{:T(128)}, ...), condition=%wide.region_5.6_spmd, body=%wide.region_2.5_spmd.sunk | while | flops 2250236416 | bytes 134494480 | solution.py:88
  162.8 16.5 fusion.125
  179.3 15.3 fusion.126
  194.7 14.6 fusion.127
  212.5 16.6 fusion.125
  229.2 15.9 fusion.126
  245.1 14.6 fusion.127
  271.8 13.3 reshape.288
  285.1 47.6 %multiply_convert_fusion.1 = (bf16[1024,4096]{1,0:T(8,128)(2,1)}, f32[1024,4096]{1,0:T(8,128)}, f32[1024,4096]{1,0:T(8,128)}) fusion(bf16[1024,4096]{1,0:T(8,128)(2,1)} %reshape.288, bf16[1024,1024]{0,1:T(8,128)(2,1)S(1)} %add_convert_fusion.4.clone.4), kind=kOutput, calls=%fused_computation.49 | convolution fusion | flops 8862564352 | bytes 52428800 | tf_op jit(solution)/shard_map/dot_general | solution.py:173
  332.7 13.4 reshape.289
  346.1 22.8 %add_convert_fusion = bf16[1024,4096]{1,0:T(8,128)(2,1)} fusion(f32[1024,4096]{1,0:T(8,128)} %get-tuple-element.237, f32[1024,4096]{1,0:T(8,128)} %get-tuple-element.253, bf16[4096,1024]{1,0:T(8,128)(2,1)} %reshape.289, bf16[1024,1024]{0,1:T(8,128)(2,1)S(1)} %copy-done.15, pred[1024]{0:T(1024)(128)(4,1)S(1)} %copy-done.56), kind=kOutput, calls=%fused_computation.48 | convolution fusion | flops 8651800576 | bytes 52429824 | tf_op jit(solution)/shard_map/td,fd->tf/dot_general | solution.py:191
  369.0 15.9 fusion.78
  384.8 5.4 copy.47
  390.2 5.4 multiply_reduce_fusion.1
  408.4 12.7 multiply_bitcast_fusion.1
  421.2 224.2 %while.28 = (s32[]{:T(128)}, f32[1024,16,64]{0,2,1:T(8,128)}, f32[1024,16,64]{0,2,1:T(8,128)}, bf16[2,512,16,64]{1,3,2,0:T(8,128)(2,1)}, s32[2]{0:T(128)S(1)}, /...) while((s32[]{:T(128)}, f32[1024,16,64]{0,2,1:T(8,128)}, ...), condition=%wide.region_12.13_spmd.clone, body=%wide.region_10.12_spmd.clone.sunk | while | flops 5501870592 | bytes 283359520 | solution.py:136
  422.8 14.4 fusion.137
  439.9 26.0 %multiply_reduce_fusion.5 = (f32[16,512]{1,0:T(8,128)S(1)}, f32[16,512,1024]{2,1,0:T(8,128)}) fusion(f32[16,512,1024]{2,1,0:T(8,128)} %fusion.137, f32[16,512]{1,0:T(8,128)S(1)} %dynamic-slice_bitcast_fusion.2, pred[512,1024]{1,0:T(8,128)(4,1)S(1)} %fusion.138, bf16[1024,16,64]{0,2,1:T(8,128)(2,1)} %get-tuple-element.460, ...), kind=kOutput, calls=%fused_computation.19.clone.1 | convolution fusion | flops 1115676672 | bytes 70844416 | tf_op jit(solution)/shard_map/while/body/eval_jaxpr/qhd,khd->hqk/dot_general | solution.py:116
  465.9 27.8 %multiply_convert_fusion.3 = bf16[16,512,1024]{2,1,0:T(8,128)(2,1)} fusion(f32[16,512,1024]{2,1,0:T(8,128)} %get-tuple-element.380, f32[16,512,1024]{2,1,0:T(8,128)} %fusion.137, f32[16,512]{1,0:T(8,128)S(1)} %get-tuple-element.381, f32[16,512]{1,0:T(8,128)S(1)} %dynamic-slice_bitcast_fusion.2, pred[512,1024]{1,0:T(8,128)(4,1)S(1)} %fusion.138), kind=kLoop, calls=%fused_computation.18.clone.1 | loop fusion | flops 50331648 | bytes 84475904 | tf_op jit(solution)/shard_map/while/body/eval_jaxpr/convert_element_type | solution.py:120
  493.7 11.2 bitcast_add_fusion.4
  504.8 17.6 bitcast_add_fusion.5
  522.4 9.8 bitcast_dynamic-update-slice_fusion.5
  533.4 14.4 fusion.137
  550.5 26.0 %multiply_reduce_fusion.5 = (f32[16,512]{1,0:T(8,128)S(1)}, f32[16,512,1024]{2,1,0:T(8,128)}) fusion(f32[16,512,1024]{2,1,0:T(8,128)} %fusion.137, f32[16,512]{1,0:T(8,128)S(1)} %dynamic-slice_bitcast_fusion.2, pred[512,1024]{1,0:T(8,128)(4,1)S(1)} %fusion.138, bf16[1024,16,64]{0,2,1:T(8,128)(2,1)} %get-tuple-element.460, ...), kind=kOutput, calls=%fused_computation.19.clone.1 | convolution fusion | flops 1115676672 | bytes 70844416 | tf_op jit(solution)/shard_map/while/body/eval_jaxpr/qhd,khd->hqk/dot_general | solution.py:116
  576.5 27.8 %multiply_convert_fusion.3 = bf16[16,512,1024]{2,1,0:T(8,128)(2,1)} fusion(f32[16,512,1024]{2,1,0:T(8,128)} %get-tuple-element.380, f32[16,512,1024]{2,1,0:T(8,128)} %fusion.137, f32[16,512]{1,0:T(8,128)S(1)} %get-tuple-element.381, f32[16,512]{1,0:T(8,128)S(1)} %dynamic-slice_bitcast_fusion.2, pred[512,1024]{1,0:T(8,128)(4,1)S(1)} %fusion.138), kind=kLoop, calls=%fused_computation.18.clone.1 | loop fusion | flops 50331648 | bytes 84475904 | tf_op jit(solution)/shard_map/while/body/eval_jaxpr/convert_element_type | solution.py:120
  604.3 12.3 bitcast_add_fusion.4
  616.6 18.8 bitcast_add_fusion.5
  635.4 9.8 bitcast_dynamic-update-slice_fusion.5
  655.4 11.7 multiply_bitcast_fusion.2
  667.0 12.3 copy.57
  679.4 5.4 copy.58
  684.8 14.3 copy.59
  699.1 11.4 multiply_bitcast_fusion
  710.5 8.1 copy.60
  721.8 855.2 %all-reduce.12.cloned.1.call-done = (f32[3145728]{0:T(1024)}, f32[1048576]{0:T(1024)}, f32[4194304]{0:T(1024)}, f32[4194304]{0:T(1024)}) async-done(((f32[3145728]{0:T(1024)}, f32[1048576]{0:T(1024)}, f32[4194304]{0:T(1024)}, f32[4194304]{0:T(1024)}), (f32[3145728]{0:T(1024)}, f32[1048576]{0:T(1024)}, f32[4194304]{0:T(1024)}, f32[4194304]{0:T(1024)})) %all-reduce.12.cloned.1.call-update) | async-done | bytes 50331664
  1592.5 15.8 select_convert_fusion
  1612.2 12.0 fusion.79
  1624.2 5.4 copy.49
  1643.3 17.5 all-reduce.4
  1660.8 14.6 psum.39
  1675.4 175.0 %all-reduce.10.cloned.1.call-done = (f32[786432]{0:T(1024)}, f32[262144]{0:T(1024)}, f32[1048576]{0:T(1024)}, f32[1048576]{0:T(1024)}) async-done(((f32[786432]{0:T(1024)}, f32[262144]{0:T(1024)}, f32[1048576]{0:T(1024)}, f32[1048576]{0:T(1024)}), (f32[786432]{0:T(1024)}, f32[262144]{0:T(1024)}, f32[1048576]{0:T(1024)}, f32[1048576]{0:T(1024)})) %all-reduce.10.cloned.1.call-update) | async-done | bytes 12582928 | tf_op jit(solution)/shard_map/psum | solution.py:223
  1856.3 23.3 %fusion.41 = (f32[3146752]{0:T(1024)}, f32[3146752]{0:T(1024)}) fusion(f32[3146752]{0:T(1024)S(1)} %constant_dynamic-update-slice_fusion, f32[3146752]{0:T(1024)} %param.15, f32[3146752]{0:T(1024)} %param.14), kind=kLoop, calls=%fused_computation.67 | loop fusion | flops 34614272 | bytes 62935040 | tf_op jit(solution)/shard_map/div | solution.py:229
  (231 shorter events, 117.8 us)
Async XLA Ops:
  7.2 47.1 %all-gather.7.cloned.1.call-start = ((), (), s32[]{:S(2)}) async-start(), calls=%async_computation.1 | async-start | bytes 2621440 | tf_op jit(solution)/shard_map/all_gather | solution.py:157
  16.0 110.8 %all-gather.5.cloned.1.call-start = ((), (), s32[]{:S(2)}) async-start(), calls=%async_computation | async-start | bytes 7864320 | tf_op jit(solution)/shard_map/all_gather | solution.py:156
  18.8 253.0 %all-gather.9.cloned.1.call-start = ((), (), s32[]{:S(2)}) async-start(), calls=%async_computation.2 | async-start | bytes 10485760 | tf_op jit(solution)/shard_map/all_gather | solution.py:158
  23.3 3.6 slice-start
  23.3 309.4 %all-gather.11.cloned.1.call-start = ((), (), s32[]{:S(2)}) async-start(), calls=%async_computation.3 | async-start | bytes 10485760 | tf_op jit(solution)/shard_map/all_gather | solution.py:159
  23.9 1553.0 %all-reduce.12.cloned.1.call-start = ((), (), s32[]{:S(2)}) async-start(), calls=%async_computation.5 | async-start | bytes 100663296
  24.0 14.7 copy-start.30
  27.0 110.3 %copy-start.4 = (bf16[1024,1024]{0,1:T(8,128)(2,1)}, bf16[1024,1024]{0,1:T(8,128)(2,1)S(1)}, u32[]{:S(2)}) copy-start(bf16[1024,1024]{0,1:T(8,128)(2,1)S(1)} %copy.40) | copy-start | bytes 6291460
  37.2 100.1 %copy-start.43 = (f32[1024]{0:T(1024)}, f32[1024]{0:T(1024)S(1)}, u32[]{:S(2)}) copy-start(f32[1024]{0:T(1024)S(1)} %get-tuple-element.249) | copy-start | bytes 12292
  37.2 100.1 %copy-start.58 = (f32[1024]{0:T(1024)}, f32[1024]{0:T(1024)S(1)}, u32[]{:S(2)}) copy-start(f32[1024]{0:T(1024)S(1)} %get-tuple-element.250) | copy-start | bytes 12292
  37.6 99.7 %copy-start.37 = (f32[1024]{0:T(1024)}, f32[1024]{0:T(1024)S(1)}, u32[]{:S(2)}) copy-start(f32[1024]{0:T(1024)S(1)} %broadcast_multiply_fusion.1) | copy-start | bytes 12292
  38.8 98.5 %copy-start.49 = (f32[1024]{0:T(1024)}, f32[1024]{0:T(1024)S(1)}, u32[]{:S(2)}) copy-start(f32[1024]{0:T(1024)S(1)} %fusion.63) | copy-start | bytes 12292
  179.3 15.3 copy-start.3
  179.3 15.3 copy-start.26
  229.2 15.9 copy-start.3
  229.2 15.9 copy-start.26
  261.3 5.2 copy-start
  261.3 5.2 copy-start.33
  261.4 5.2 copy-start.5
  261.4 5.2 copy-start.23
  332.7 13.5 copy-start.15
  332.7 13.5 copy-start.56
  384.8 5.4 copy-start.36
  384.8 5.4 copy-start.40
  384.8 5.4 copy-start.42
  390.2 5.4 copy-start.48
  390.2 5.4 copy-start.8
  390.2 5.9 copy-start.10
  400.3 3.7 copy-start.29
  400.3 8.1 slice-start.1
  404.0 4.4 copy-start.55
  404.0 4.4 slice-start.2
  408.4 12.8 copy-start.1
  408.4 12.8 copy-start.31
  408.4 12.8 copy-start.34
  648.0 6.0 copy-start.20
  649.1 4.9 copy-start.21
  651.2 4.1 copy-start.6
  651.2 4.1 copy-start.38
  651.2 4.1 copy-start.44
  651.2 4.1 copy-start.50
  651.2 4.1 copy-start.59
  684.8 14.3 copy-start.16
  684.8 14.3 copy-start.57
  718.6 1131.8 %all-reduce.10.cloned.1.call-start = ((), (), s32[]{:S(2)}) async-start(), calls=%async_computation.4 | async-start | bytes 25165824 | tf_op jit(solution)/shard_map/psum | solution.py:223
  1639.1 4.1 copy-start.53
  1639.1 4.1 copy-start.60
  1856.3 23.3 %copy-start.14 = (f32[3146752]{0:T(1024)}, f32[3146752]{0:T(1024)S(1)}, u32[]{:S(2)}) copy-start(f32[3146752]{0:T(1024)S(1)} %constant_dynamic-update-slice_fusion) | copy-start | bytes 37761028
  (26 other events, 57.5 us)
Sparse Core Ops, SparseCore 0:
  16.2 38.0 all-gather.6
  56.6 70.1 all-gather.4
  129.3 87.6 all-gather.8
  219.2 87.6 all-gather.10
  718.7 858.2 all-reduce.11
  1592.0 258.3 all-reduce.9
where the time goes:
time: 1900 us; the launch traced here: 1890 us
  waiting for transfers between devices  1110 us (58%)
  matrix products  394 us (21%)
  local copies, waits for them, and re-layouts  176 us (9%)
  other arithmetic  139 us (7%)
  blocking collectives  41.7 us (2%)
    unnamed x7, waiting for transfers between devices  856 us
    psum x1, waiting for transfers between devices, body(): summed = lax.psum((owned[0], owned[1], owned[2], owned[3], owned[4]), 'dp')  175 us
    unnamed x143, local copies, waits for them, and re-layouts  90.5 us
    all_gather x1, waiting for transfers between devices, body(): lax.all_gather(pieces[0], 'group', axis=0, tiled=True)  68.5 us
    dot_general x4, matrix products, one_block(): jnp.einsum('qhd,khd->hqk', query_blk, keys_all, preferred_element_type=jn...  62 us
    convert_element_type x2, other arithmetic, one_block(): score_grad = (prob_full * (prob_grad - inner)).astype(jnp.bfloat16)  55.6 us
    dot_general x2, matrix products, one_block(): jnp.einsum('qhd,khd->hqk', outgrad_blk, values_all, preferred_element_typ...  52 us
    dot_general x1, matrix products, body(): pre_act = jnp.dot(a_two, w_in, preferred_element_type=jnp.float32)  47.6 us
  transfers between devices with their start and end apart: 6, of which 4 were waited for; matrix products, arithmetic and copies ran while one was open for 14% of the time, Pallas kernels for 0%

commit v1 on v0

v1 whole, which is shorter than its diff:
```python
import functools

import jax
import jax.numpy as jnp
from jax import lax
from jax.experimental import pallas as pl
from jax.experimental.pallas import tpu as pltpu
from jax.sharding import Mesh
from jax.sharding import PartitionSpec as P

HEADS = 16
EPS = 1e-05
FILL = -1e30
BETA_ONE = 0.9
BETA_TWO = 0.999
RATE = 0.001
ADAM_EPS = 1e-08
STEPS = 100.0
VMEM_MB = 60

f32 = jnp.float32
bf16 = jnp.bfloat16
ANY = pl.BlockSpec(memory_space=pl.ANY)


def params(limit=VMEM_MB):
    return pltpu.CompilerParams(vmem_limit_bytes=limit << 20)


def cost(flops, nbytes, trans=0):
    return pl.CostEstimate(flops=int(flops), bytes_accessed=int(nbytes), transcendentals=int(trans))


def sds(shape, dtype):
    return jax.ShapeDtypeStruct(shape, dtype)


def dot_nn(a, b):
    return jnp.dot(a, b, preferred_element_type=f32)


def dot_nt(a, b):
    return lax.dot_general(a, b, (((1,), (1,)), ((), ())), preferred_element_type=f32)


def dot_tn(a, b):
    return lax.dot_general(a, b, (((0,), (0,)), ((), ())), preferred_element_type=f32)


def pick(flag, a, b):
    return jnp.where(flag, a, b)


def unpack_kernel(dims, ids, m_qkv, m_out, m_in, m_back, own_qkv, oth_qkv, own_oi, oth_oi, own_bk, oth_bk):
    n, d, ff = dims
    c = ids[1]
    first = c == 0
    rows = d // n
    nb = d // 128

    def put(ref, own, oth, dst, lo, hi, stride, count):
        a = ref[pl.ds(lo, count, stride=stride), :].astype(bf16)
        b = ref[pl.ds(hi, count, stride=stride), :].astype(bf16)
        own[:, dst : dst + 128] = pick(first, a, b)
        oth[:, dst : dst + 128] = pick(first, b, a)

    half = nb // 2
    for part in range(3):
        for w in range(half):
            lo = part * nb + w
            put(m_qkv, own_qkv, oth_qkv, (part * half + w) * 128, lo, lo + half, 3 * nb, rows)
    for w in range(half):
        put(m_out, own_oi, oth_oi, w * 128, w, w + half, nb, rows)
    share = ff // n
    hs = share // 2
    for j in range(n):
        for q in range(hs // 128):
            lo = (share * j) // 128 + q
            put(m_in, own_oi, oth_oi, d // 2 + hs * j + q * 128, lo, lo + hs // 128, ff // 128, rows)
    for w in range(nb):
        put(m_back, own_bk, oth_bk, w * 128, w, hs * nb + w, nb, hs)


def unpack(ids, flat, n, d, ff):
    rows = d // n
    hs = ff // n // 2
    lanes = flat.reshape(-1, 128)
    r1, r2, r3, r4 = rows * 3 * d // 128, rows * d // 128, rows * ff // 128, ff // n * d // 128
    assert r1 % r2 == 0 and (r1 + r2) % r3 == 0 and (r1 + r2 + r3) % r4 == 0
    spec = lambda r, i: pl.BlockSpec((r, 128), lambda g, ids: (i, 0))
    full = lambda s: pl.BlockSpec(s, lambda g, ids: (0, 0))
    s1, s2, s3 = (rows, 3 * d // 2), (rows, d // 2 + ff // 2), (hs, d)
    shapes = [s1, s1, s2, s2, s3, s3]
    return pl.pallas_call(
        functools.partial(unpack_kernel, (n, d, ff)),
        out_shape=[sds(s, bf16) for s in shapes],
        grid_spec=pltpu.PrefetchScalarGridSpec(
            num_scalar_prefetch=1,
            grid=(1,),
            in_specs=[spec(r1, 0), spec(r2, r1 // r2), spec(r3, (r1 + r2) // r3), spec(r4, (r1 + r2 + r3) // r4)],
            out_specs=[full(s) for s in shapes],
        ),
        compiler_params=params(),
        name="unpack",
    )(ids, lanes, lanes, lanes, lanes)


def gather_halves(h, n):
    rows = h.shape[0]
    if n == 4:
        hx = lax.ppermute(h, "x", [(0, 1), (1, 0)])
        hy = lax.ppermute(h, "y", [(0, 1), (1, 0)])
        da = lax.ppermute(hx[: rows // 2], "y", [(0, 1), (1, 0)])
        db = lax.ppermute(hy[rows // 2 :], "x", [(0, 1), (1, 0)])
        return [(0, 0, h), (1, 0, hx), (2, 0, hy), (3, 0, da), (3, rows // 2, db)]
    full = lax.all_gather(h, ("y", "x"), axis=0)
    me = lax.axis_index(("y", "x"))
    return [(k, 0, lax.dynamic_index_in_dim(full, me ^ k, 0, keepdims=False)) for k in range(n)]


def swap_core(v):
    return lax.ppermute(v, "core", [(0, 1), (1, 0)])


def piece_layout(pieces):
    return tuple((k, off, p.shape[0]) for k, off, p in pieces)


def start_pieces(layout, refs, dst, rows, base, cols, me, sems, first_sem, src_cols=None):
    copies = []
    for s, ((k, off, count), ref) in enumerate(zip(layout, refs)):
        start = pl.multiple_of(base + (me ^ k) * rows + off, 8)
        src = ref if src_cols is None else ref.at[:, src_cols]
        copies.append(pltpu.make_async_copy(src, dst.at[pl.ds(start, count), cols], sems.at[first_sem + s]))
    for cp in copies:
        cp.start()
    return copies


def layer_norm_parts(v):
    centre = v - jnp.mean(v, axis=-1, keepdims=True)
    r = lax.rsqrt(jnp.mean(centre * centre, axis=-1, keepdims=True) + EPS)
    return centre * r, r


def layer_norm_back(v, gain, dz):
    xhat, r = layer_norm_parts(v)
    dg = jnp.sum(dz * xhat, axis=0, keepdims=True)
    db = jnp.sum(dz, axis=0, keepdims=True)
    t = dz * gain
    dv = r * (t - jnp.mean(t, axis=-1, keepdims=True) - xhat * jnp.mean(t * xhat, axis=-1, keepdims=True))
    return dv, dg, db


def qkv_kernel(lay, ids, tok, norms, *refs):
    pieces, (a_out, own_out, oth_out, w, sems) = refs[: 2 * len(lay)], refs[2 * len(lay) :]
    d = tok.shape[1]
    rows = d // ids_n(lay)
    half = 3 * d // 2

    @pl.when(pl.program_id(0) == 0)
    def _():
        me = ids[0]
        cps = start_pieces(lay, pieces[: len(lay)], w, rows, 0, pl.ds(0, half), me, sems, 0)
        cps += start_pieces(lay, pieces[len(lay) :], w, rows, 0, pl.ds(half, half), me, sems, len(lay))
        for cp in cps:
            cp.wait()

    xhat, _ = layer_norm_parts(tok[...].astype(f32))
    a = (xhat * norms[0:1, :] + norms[1:2, :]).astype(bf16)
    a_out[...] = a
    acc = dot_nn(a, w[...])
    scale = (d // HEADS) ** (-0.5)
    q = d // 2
    own_out[:, :q] = (acc[:, :q].astype(bf16).astype(f32) * scale).astype(bf16)
    own_out[:, q:] = acc[:, q:half].astype(bf16)
    oth_out[:, :q] = (acc[:, half : half + q].astype(bf16).astype(f32) * scale).astype(bf16)
    oth_out[:, q:] = acc[:, half + q :].astype(bf16)


def ids_n(lay):
    return max(k for k, _, _ in lay) + 1


def project_qkv(ids, tok, norms, own, oth, tm=256):
    lay = piece_layout(own)
    t, d = tok.shape
    blk = lambda w: pl.BlockSpec((tm, w), lambda i, ids: (i, 0))
    return pl.pallas_call(
        functools.partial(qkv_kernel, lay),
        out_shape=[sds((t, d), bf16), sds((t, 3 * d // 2), bf16), sds((t, 3 * d // 2), bf16)],
        grid_spec=pltpu.PrefetchScalarGridSpec(
            num_scalar_prefetch=1,
            grid=(t // tm,),
            in_specs=[blk(d), pl.BlockSpec((4, d), lambda i, ids: (0, 0))] + [ANY] * (2 * len(lay)),
            out_specs=[blk(d), blk(3 * d // 2), blk(3 * d // 2)],
            scratch_shapes=[pltpu.VMEM((d, 3 * d), bf16), pltpu.SemaphoreType.DMA((2 * len(lay),))],
        ),
        compiler_params=params(),
        cost_estimate=cost(2 * t * d * 3 * d, 16e6),
        name="qkv",
    )(ids, tok, norms, *[p for _, _, p in own], *[p for _, _, p in oth])


QB = 256


def fill_bias(bias, doc_row, doc_col):
    t = bias.shape[0]
    for r in range(0, t, QB):
        key = r + lax.broadcasted_iota(jnp.int32, (QB, t), 0)
        query = lax.broadcasted_iota(jnp.int32, (QB, t), 1)
        ok = (doc_col[r : r + QB, :] == doc_row[...]) & (key <= query)
        bias[r : r + QB, :] = jnp.where(ok, 0.0, FILL)


def head_lanes(v, h, hd):
    lane = lax.broadcasted_iota(jnp.int32, v.shape, 1)
    return jnp.where((lane >= h * hd) & (lane < (h + 1) * hd), v, jnp.zeros_like(v))


def attend_kernel(hd, q, k, v, doc_row, doc_col, out, lse, bias):
    @pl.when(pl.program_id(0) == 0)
    def _():
        fill_bias(bias, doc_row, doc_col)

    t = q.shape[0]
    vt = v[...].T
    per = 128 // hd
    qs = [head_lanes(q[...], h, hd) for h in range(per)]
    for i in range(t // QB):
        n = (i + 1) * QB
        cols = slice(i * QB, n)
        outs = []
        for h in range(per):
            s = dot_nt(k[:n, :], qs[h][cols, :]) + bias[:n, cols]
            top = jnp.max(s, axis=0, keepdims=True)
            e = jnp.exp(s - top)
            total = jnp.sum(e, axis=0, keepdims=True)
            lse[0, h : h + 1, cols] = top + jnp.log(total)
            o = dot_nn(vt[h * hd : (h + 1) * hd, :n], e.astype(bf16))
            outs.append(o / total)
        out[cols, :] = jnp.concatenate(outs, axis=0).T.astype(bf16)


def attend(qkv, doc_row, doc_col, d):
    t = qkv.shape[0]
    half = d // 2
    pairs = half // 128
    hd = d // HEADS
    per = 128 // hd
    col = lambda part: pl.BlockSpec((t, 128), lambda p: (0, part * pairs + p))
    return pl.pallas_call(
        functools.partial(attend_kernel, hd),
        grid=(pairs,),
        out_shape=[sds((t, half), bf16), sds((pairs, per, t), f32)],
        in_specs=[col(0), col(1), col(2), pl.BlockSpec((1, t), lambda p: (0, 0)), pl.BlockSpec((t, 1), lambda p: (0, 0))],
        out_specs=[pl.BlockSpec((t, 128), lambda p: (0, p)), pl.BlockSpec((1, per, t), lambda p: (p, 0, 0))],
        scratch_shapes=[pltpu.VMEM((t, t), f32)],
        compiler_params=params(),
        cost_estimate=cost(8 * t * t * half, 5e6, t * t * half // hd),
        name="attend",
    )(qkv, qkv, qkv, doc_row, doc_col)


def attend_back_kernel(hd, q, k, v, dout, att, lse, doc_row, doc_col, dq, dk, dv, bias, dk_acc, dv_acc):
    @pl.when(pl.program_id(0) == 0)
    def _():
        fill_bias(bias, doc_row, doc_col)

    t = q.shape[0]
    per = 128 // hd
    scale = hd ** (-0.5)
    kt = k[...].T
    prod = (dout[...].astype(f32) * att[...].astype(f32)).T
    inner = [jnp.sum(prod[h * hd : (h + 1) * hd, :], axis=0, keepdims=True) for h in range(per)]
    qs = [head_lanes(q[...], h, hd) for h in range(per)]
    ds_ = [head_lanes(dout[...], h, hd) for h in range(per)]
    dk_acc[...] = jnp.zeros_like(dk_acc)
    dv_acc[...] = jnp.zeros_like(dv_acc)
    for i in range(t // QB):
        n = (i + 1) * QB
        cols = slice(i * QB, n)
        dqs = []
        for h in range(per):
            qh, dh = qs[h][cols, :], ds_[h][cols, :]
            s = dot_nt(k[:n, :], qh) + bias[:n, cols]
            p = jnp.exp(s - lse[0, h : h + 1, cols])
            dp = dot_nt(v[:n, :], dh)
            g = (p * (dp - inner[h][:, cols])).astype(bf16)
            dv_acc[:n, :] += dot_nn(p.astype(bf16), dh)
            dk_acc[:n, :] += dot_nn(g, qh)
            dqs.append(dot_nn(kt[h * hd : (h + 1) * hd, :n], g))
        dq[cols, :] = (jnp.concatenate(dqs, axis=0).T * scale).astype(bf16)
    dk[...] = dk_acc[...].astype(bf16)
    dv[...] = dv_acc[...].astype(bf16)


def attend_back(qkv, dout, att, lse, doc_row, doc_col, d):
    t = qkv.shape[0]
    half = d // 2
    pairs = half // 128
    hd = d // HEADS
    per = 128 // hd
    col = lambda part: pl.BlockSpec((t, 128), lambda p: (0, part * pairs + p))
    one = pl.BlockSpec((t, 128), lambda p: (0, p))
    return pl.pallas_call(
        functools.partial(attend_back_kernel, hd),
        grid=(pairs,),
        out_shape=[sds((t, half), bf16)] * 3,
        in_specs=[col(0), col(1), col(2), one, one, pl.BlockSpec((1, per, t), lambda p: (p, 0, 0)),
                  pl.BlockSpec((1, t), lambda p: (0, 0)), pl.BlockSpec((t, 1), lambda p: (0, 0))],
        out_specs=[one, one, one],
        scratch_shapes=[pltpu.VMEM((t, t), f32), pltpu.VMEM((t, 128), f32), pltpu.VMEM((t, 128), f32)],
        compiler_params=params(),
        cost_estimate=cost(20 * t * t * half, 8e6, t * t * half // hd),
        name="attend_back",
    )(qkv, qkv, qkv, dout, att, lse, doc_row, doc_col)


def out_proj_kernel(lay, ids, att_own, att_oth, tok, norms, *refs):
    pieces, (resid, a_two, w, sems) = refs[: 2 * len(lay)], refs[2 * len(lay) :]
    d = tok.shape[1]
    half = d // 2
    c = ids[1]

    @pl.when(pl.program_id(0) == 0)
    def _():
        load_out(lay, ids, pieces, w, sems)

    lo = pl.multiple_of(c * half, half)
    hi = pl.multiple_of((1 - c) * half, half)
    y = dot_nn(att_own[...], w[pl.ds(lo, half), :]) + dot_nn(att_oth[...], w[pl.ds(hi, half), :])
    r = tok[...].astype(f32) + y
    resid[...] = r
    xhat, _ = layer_norm_parts(r)
    a_two[...] = (xhat * norms[2:3, :] + norms[3:4, :]).astype(bf16)


def load_out(lay, ids, pieces, w, sems):
    d = w.shape[1]
    half = d // 2
    rows = d // ids_n(lay)
    me, c = ids[0], ids[1]
    cols = pl.ds(0, half)
    lo = pl.multiple_of(c * half, half)
    hi = pl.multiple_of((1 - c) * half, half)
    cps = start_pieces(lay, pieces[: len(lay)], w, rows, 0, pl.ds(lo, half), me, sems, 0, cols)
    cps += start_pieces(lay, pieces[len(lay) :], w, rows, 0, pl.ds(hi, half), me, sems, len(lay), cols)
    for cp in cps:
        cp.wait()


def out_proj(ids, att_own, att_oth, tok, norms, own, oth, tm=256):
    lay = piece_layout(own)
    t, d = tok.shape
    blk = lambda w: pl.BlockSpec((tm, w), lambda i, ids: (i, 0))
    return pl.pallas_call(
        functools.partial(out_proj_kernel, lay),
        out_shape=[sds((t, d), f32), sds((t, d), bf16)],
        grid_spec=pltpu.PrefetchScalarGridSpec(
            num_scalar_prefetch=1,
            grid=(t // tm,),
            in_specs=[blk(d // 2), blk(d // 2), blk(d), pl.BlockSpec((4, d), lambda i, ids: (0, 0))] + [ANY] * (2 * len(lay)),
            out_specs=[blk(d), blk(d)],
            scratch_shapes=[pltpu.VMEM((d, d), bf16), pltpu.SemaphoreType.DMA((2 * len(lay),))],
        ),
        compiler_params=params(),
        cost_estimate=cost(2 * t * d * d, 14e6),
        name="out_proj",
    )(ids, att_own, att_oth, tok, norms, *[p for _, _, p in own], *[p for _, _, p in oth])


def ffn_in_kernel(lay, ids, a_two, *refs):
    pieces, (hidden, slope, w, sems) = refs[: len(lay)], refs[len(lay) :]
    d = a_two.shape[1]
    wide = w.shape[1]
    blk = hidden.shape[1]

    @pl.when(pl.program_id(0) == 0)
    def _():
        cps = start_pieces(lay, pieces, w, d // ids_n(lay), 0, pl.ds(0, wide), ids[0], sems, 0, pl.ds(d // 2, wide))
        for cp in cps:
            cp.wait()

    cols = pl.ds(pl.multiple_of(pl.program_id(0) * blk, blk), blk)
    pre = dot_nn(a_two[...], w[:, cols])
    cdf = 0.5 + 0.5 * lax.erf(pre * (0.5**0.5))
    pdf = jnp.exp(-0.5 * pre * pre) * 0.3989422804014327
    hidden[...] = (pre * cdf).astype(bf16)
    slope[...] = (cdf + pre * pdf).astype(bf16)


def ffn_in(ids, a_two, pieces, ff, blk=512):
    lay = piece_layout(pieces)
    t, d = a_two.shape
    wide = ff // 2
    out = pl.BlockSpec((t, blk), lambda j, ids: (0, j))
    return pl.pallas_call(
        functools.partial(ffn_in_kernel, lay),
        out_shape=[sds((t, wide), bf16)] * 2,
        grid_spec=pltpu.PrefetchScalarGridSpec(
            num_scalar_prefetch=1,
            grid=(wide // blk,),
            in_specs=[pl.BlockSpec((t, d), lambda j, ids: (0, 0))] + [ANY] * len(lay),
            out_specs=[out, out],
            scratch_shapes=[pltpu.VMEM((d, wide), bf16), pltpu.SemaphoreType.DMA((len(lay),))],
        ),
        compiler_params=params(),
        cost_estimate=cost(2 * t * d * wide, 14e6, 2 * t * wide),
        name="ffn_in",
    )(ids, a_two, *[p for _, _, p in pieces])


def ffn_out_kernel(lay, ids, h_own, h_oth, resid, doc, *refs):
    pieces, (mixed, w, sems) = refs[: 2 * len(lay)], refs[2 * len(lay) :]
    half = h_own.shape[1]
    d = resid.shape[1]

    @pl.when(pl.program_id(0) == 0)
    def _():
        rows = half // ids_n(lay)
        cps = start_pieces(lay, pieces[: len(lay)], w, rows, 0, pl.ds(0, d), ids[0], sems, 0)
        cps += start_pieces(lay, pieces[len(lay) :], w, rows, half, pl.ds(0, d), ids[0], sems, len(lay))
        for cp in cps:
            cp.wait()

    y = dot_nn(h_own[...], w[:half, :]) + dot_nn(h_oth[...], w[half:, :]) + resid[...]
    mixed[...] = jnp.where(doc[...] >= 0, y, 0.0).astype(bf16)


def ffn_out(ids, h_own, h_oth, resid, doc_col, own, oth, tm=256):
    lay = piece_layout(own)
    t, half = h_own.shape
    d = resid.shape[1]
    blk = lambda w: pl.BlockSpec((tm, w), lambda i, ids: (i, 0))
    return pl.pallas_call(
        functools.partial(ffn_out_kernel, lay),
        out_shape=sds((t, d), bf16),
        grid_spec=pltpu.PrefetchScalarGridSpec(
            num_scalar_prefetch=1,
            grid=(t // tm,),
            in_specs=[blk(half), blk(half), blk(d), blk(1)] + [ANY] * (2 * len(lay)),
            out_specs=blk(d),
            scratch_shapes=[pltpu.VMEM((2 * half, d), bf16), pltpu.SemaphoreType.DMA((2 * len(lay),))],
        ),
        compiler_params=params(),
        cost_estimate=cost(4 * t * d * half, 23e6),
        name="ffn_out",
    )(ids, h_own, h_oth, resid, doc_col, *[p for _, _, p in own], *[p for _, _, p in oth])


def d_pre_kernel(lay, ids, d_out, slope, *refs):
    pieces, (d_pre, w, sems) = refs[: len(lay)], refs[len(lay) :]
    d = d_out.shape[1]
    blk = slope.shape[1]
    half = w.shape[0]

    @pl.when(pl.program_id(0) == 0)
    def _():
        cps = start_pieces(lay, pieces, w, half // ids_n(lay), 0, pl.ds(0, d), ids[0], sems, 0)
        for cp in cps:
            cp.wait()

    rows = pl.ds(pl.multiple_of(pl.program_id(0) * blk, blk), blk)
    d_pre[...] = (dot_nt(d_out[...], w[rows, :]) * slope[...].astype(f32)).astype(bf16)


def pre_grad(ids, d_out, slope, pieces, blk=512):
    lay = piece_layout(pieces)
    t, d = d_out.shape
    half = slope.shape[1]
    col = pl.BlockSpec((t, blk), lambda j, ids: (0, j))
    return pl.pallas_call(
        functools.partial(d_pre_kernel, lay),
        out_shape=sds((t, half), bf16),
        grid_spec=pltpu.PrefetchScalarGridSpec(
            num_scalar_prefetch=1,
            grid=(half // blk,),
            in_specs=[pl.BlockSpec((t, d), lambda j, ids: (0, 0)), col] + [ANY] * len(lay),
            out_specs=col,
            scratch_shapes=[pltpu.VMEM((half, d), bf16), pltpu.SemaphoreType.DMA((len(lay),))],
        ),
        compiler_params=params(),
        cost_estimate=cost(2 * t * d * half, 14e6),
        name="pre_grad",
    )(ids, d_out, slope, *[p for _, _, p in pieces])


def d_two_kernel(lay, ids, p_own, p_oth, resid, d_out, norms, *refs):
    pieces = refs[: 2 * len(lay)]
    d_resid, low, low_oth, dg, db, w, sems = refs[2 * len(lay) :]
    half = p_own.shape[1]
    d = resid.shape[1]

    @pl.when(pl.program_id(0) == 0)
    def _():
        rows = d // ids_n(lay)
        cols = pl.ds(d // 2, half)
        cps = start_pieces(lay, pieces[: len(lay)], w, rows, 0, pl.ds(0, half), ids[0], sems, 0, cols)
        cps += start_pieces(lay, pieces[len(lay) :], w, rows, 0, pl.ds(half, half), ids[0], sems, len(lay), cols)
        for cp in cps:
            cp.wait()
        dg[...] = jnp.zeros_like(dg)
        db[...] = jnp.zeros_like(db)

    dz = dot_nt(p_own[...], w[:, :half]) + dot_nt(p_oth[...], w[:, half:])
    dv, g, b = layer_norm_back(resid[...], norms[2:3, :], dz)
    dg[...] += g
    db[...] += b
    dr = d_out[...].astype(f32) + dv
    d_resid[...] = dr
    dl = dr.astype(bf16)
    low[...] = dl
    low_oth[...] = pick(ids[1] == 0, dl[:, d // 2 :], dl[:, : d // 2])


def two_grad(ids, p_own, p_oth, resid, d_out, norms, own, oth, tm=256):
    lay = piece_layout(own)
    t, half = p_own.shape
    d = resid.shape[1]
    blk = lambda w: pl.BlockSpec((tm, w), lambda i, ids: (i, 0))
    row = pl.BlockSpec((1, d), lambda i, ids: (0, 0))
    return pl.pallas_call(
        functools.partial(d_two_kernel, lay),
        out_shape=[sds((t, d), f32), sds((t, d), bf16), sds((t, d // 2), bf16), sds((1, d), f32), sds((1, d), f32)],
        grid_spec=pltpu.PrefetchScalarGridSpec(
            num_scalar_prefetch=1,
            grid=(t // tm,),
            in_specs=[blk(half), blk(half), blk(d), blk(d), pl.BlockSpec((4, d), lambda i, ids: (0, 0))] + [ANY] * (2 * len(lay)),
            out_specs=[blk(d), blk(d), blk(d // 2), row, row],
            scratch_shapes=[pltpu.VMEM((d, 2 * half), bf16), pltpu.SemaphoreType.DMA((2 * len(lay),))],
        ),
        compiler_params=params(),
        cost_estimate=cost(4 * t * d * half, 30e6),
        name="two_grad",
    )(ids, p_own, p_oth, resid, d_out, norms, *[p for _, _, p in own], *[p for _, _, p in oth])


def d_att_kernel(lay, ids, low, *refs):
    pieces, (own, oth, w, sems) = refs[: 2 * len(lay)], refs[2 * len(lay) :]
    half = own.shape[1]

    @pl.when(pl.program_id(0) == 0)
    def _():
        load_out(lay, ids, pieces, w, sems)

    lo = pl.multiple_of(ids[1] * half, half)
    hi = pl.multiple_of((1 - ids[1]) * half, half)
    own[...] = dot_nt(low[...], w[pl.ds(lo, half), :]).astype(bf16)
    oth[...] = dot_nt(low[...], w[pl.ds(hi, half), :]).astype(bf16)


def att_grad(ids, low, own, oth, tm=512):
    lay = piece_layout(own)
    t, d = low.shape
    blk = lambda w: pl.BlockSpec((tm, w), lambda i, ids: (i, 0))
    return pl.pallas_call(
        functools.partial(d_att_kernel, lay),
        out_shape=[sds((t, d // 2), bf16)] * 2,
        grid_spec=pltpu.PrefetchScalarGridSpec(
            num_scalar_prefetch=1,
            grid=(t // tm,),
            in_specs=[blk(d)] + [ANY] * (2 * len(lay)),
            out_specs=[blk(d // 2), blk(d // 2)],
            scratch_shapes=[pltpu.VMEM((d, d), bf16), pltpu.SemaphoreType.DMA((2 * len(lay),))],
        ),
        compiler_params=params(),
        cost_estimate=cost(2 * t * d * d, 6e6),
        name="att_grad",
    )(ids, low, *[p for _, _, p in own], *[p for _, _, p in oth])


def d_one_kernel(lay, ids, *refs):
    grads, (tok, d_resid, norms), refs = refs[:6], refs[6:9], refs[9:]
    pieces, (out, dg, db, w, sems) = refs[: 2 * len(lay)], refs[2 * len(lay) :]
    d = tok.shape[1]
    half = 3 * d // 2

    @pl.when(pl.program_id(0) == 0)
    def _():
        rows = d // ids_n(lay)
        cps = start_pieces(lay, pieces[: len(lay)], w, rows, 0, pl.ds(0, half), ids[0], sems, 0)
        cps += start_pieces(lay, pieces[len(lay) :], w, rows, 0, pl.ds(half, half), ids[0], sems, len(lay))
        for cp in cps:
            cp.wait()
        dg[...] = jnp.zeros_like(dg)
        db[...] = jnp.zeros_like(db)

    both = jnp.concatenate([g[...] for g in grads], axis=1)
    dz = dot_nt(both, w[...])
    dv, g, b = layer_norm_back(tok[...].astype(f32), norms[0:1, :], dz)
    dg[...] += g
    db[...] += b
    out[...] = (d_resid[...] + dv).astype(bf16)


def one_grad(ids, g_own, g_oth, tok, d_resid, norms, own, oth, tm=256):
    lay = piece_layout(own)
    t, d = tok.shape
    blk = lambda w: pl.BlockSpec((tm, w), lambda i, ids: (i, 0))
    row = pl.BlockSpec((1, d), lambda i, ids: (0, 0))
    return pl.pallas_call(
        functools.partial(d_one_kernel, lay),
        out_shape=[sds((t, d), bf16), sds((1, d), f32), sds((1, d), f32)],
        grid_spec=pltpu.PrefetchScalarGridSpec(
            num_scalar_prefetch=1,
            grid=(t // tm,),
            in_specs=[blk(d // 2)] * 6 + [blk(d), blk(d), pl.BlockSpec((4, d), lambda i, ids: (0, 0))] + [ANY] * (2 * len(lay)),
            out_specs=[blk(d), row, row],
            scratch_shapes=[pltpu.VMEM((d, 3 * d), bf16), pltpu.SemaphoreType.DMA((2 * len(lay),))],
        ),
        compiler_params=params(),
        cost_estimate=cost(6 * t * d * d, 22e6),
        name="one_grad",
    )(ids, *g_own, *g_oth, tok, d_resid, norms, *[p for _, _, p in own], *[p for _, _, p in oth])


def pair_kernel(nb, a_mine, a_theirs, *refs):
    mine, theirs, out = refs[:nb], refs[nb : 2 * nb], refs[2 * nb]
    wide = mine[0].shape[1]
    for j in range(nb):
        acc = dot_tn(a_mine[...], mine[j][...]) + dot_tn(a_theirs[...], theirs[j][...])
        out[:, j * wide : (j + 1) * wide] = acc.astype(bf16)


def pair_grad(a_mine, a_theirs, mine, theirs, name, tm=256):
    t, m = a_mine.shape
    wide = mine[0].shape[1]
    nb = len(mine)
    a_spec = pl.BlockSpec((t, tm), lambda i: (0, i))
    b_spec = pl.BlockSpec((t, wide), lambda i: (0, 0))
    return pl.pallas_call(
        functools.partial(pair_kernel, nb),
        grid=(m // tm,),
        out_shape=sds((m, nb * wide), bf16),
        in_specs=[a_spec, a_spec] + [b_spec] * (2 * nb),
        out_specs=pl.BlockSpec((tm, nb * wide), lambda i: (i, 0)),
        compiler_params=params(),
        cost_estimate=cost(4 * t * m * wide * nb, 14e6),
        name=name,
    )(a_mine, a_theirs, *mine, *theirs)


def out_grad_kernel(ids, a_own, a_oth, t_own, t_oth, low, theirs, out):
    half = a_own.shape[1]
    c = ids[1]
    lo = pl.multiple_of(c * half, half)
    hi = pl.multiple_of((1 - c) * half, half)
    out[pl.ds(lo, half), :] = (dot_tn(a_own[...], low[...]) + dot_tn(t_oth[...], theirs[...])).astype(bf16)
    out[pl.ds(hi, half), :] = (dot_tn(a_oth[...], low[...]) + dot_tn(t_own[...], theirs[...])).astype(bf16)


def out_grad(ids, att_own, att_oth, their_own, their_oth, low, theirs):
    t, half = att_own.shape
    full = pl.BlockSpec((t, half), lambda i, ids: (0, 0))
    return pl.pallas_call(
        out_grad_kernel,
        out_shape=sds((2 * half, half), bf16),
        grid_spec=pltpu.PrefetchScalarGridSpec(
            num_scalar_prefetch=1,
            grid=(1,),
            in_specs=[full] * 4 + [pl.BlockSpec((t, half), lambda i, ids: (0, ids[1])), full],
            out_specs=pl.BlockSpec((2 * half, half), lambda i, ids: (0, 0)),
        ),
        compiler_params=params(),
        cost_estimate=cost(8 * t * half * half, 8e6),
        name="out_grad",
    )(ids, att_own, att_oth, their_own, their_oth, low, theirs)


def reduce_depth(v, nz):
    if nz != 4:
        return lax.psum(v.astype(f32), "z").astype(bf16)
    z = lax.axis_index("z")
    near = [(0, 1), (1, 0), (2, 3), (3, 2)]
    far = [(0, 2), (2, 0), (1, 3), (3, 1)]

    def split(u, bit):
        h = u.shape[0] // 2
        a, b = u[:h], u[h:]
        return jnp.where(bit == 0, a, b), jnp.where(bit == 0, b, a)

    def join(mine, theirs, bit):
        return jnp.where(bit == 0, jnp.concatenate([mine, theirs]), jnp.concatenate([theirs, mine]))

    b0, b1 = z % 2, z // 2
    keep, send = split(v, b0)
    keep = keep + lax.ppermute(send, "z", near)
    keep, send = split(keep, b1)
    keep = keep + lax.ppermute(send, "z", far)
    keep = join(keep, lax.ppermute(keep, "z", far), b1)
    return join(keep, lax.ppermute(keep, "z", near), b0)


def adam_rows(g, m1, m2):
    first = BETA_ONE * m1 + (1.0 - BETA_ONE) * g
    second = BETA_TWO * m2 + (1.0 - BETA_TWO) * g * g
    first_hat = first / (1.0 - BETA_ONE**STEPS)
    second_hat = second / (1.0 - BETA_TWO**STEPS)
    return -RATE * first_hat / (jnp.sqrt(second_hat) + ADAM_EPS), first


def adam_kernel(plan, inv_root, ids, own, oth, m1, m2, *refs):
    wg, st, mn = refs[-3:]
    rows, stride, places = plan
    first = ids[1] == 0
    for col, lo, hi in places:
        a = own[:, col : col + 128].astype(f32)
        b = oth[:, col : col + 128].astype(f32)
        for at, g in ((lo, pick(first, a, b)), (hi, pick(first, b, a))):
            where = pl.ds(at, rows, stride=stride)
            g = g * inv_root
            step, moment = adam_rows(g, m1[where, :], m2[where, :])
            wg[where, :] = g
            st[where, :] = step
            mn[where, :] = moment


def adam_columns(ids, own, oth, m1, m2, prev, inv_root, first_row, rows, places, width):
    count = own.shape[0]
    nb = width // 128
    blk = rows * nb
    assert first_row % blk == 0
    base = first_row // blk
    half = pl.BlockSpec((rows, own.shape[1]), lambda i, ids: (i, 0))
    flat = pl.BlockSpec((blk, 128), lambda i, ids: (base + i, 0))
    plan = (rows, nb, places)
    return adam_call(plan, ids, own, oth, m1, m2, prev, inv_root, count // rows, half, flat)


def adam_call(plan, ids, own, oth, m1, m2, prev, inv_root, steps, half, flat):
    return pl.pallas_call(
        functools.partial(adam_kernel, plan, inv_root),
        out_shape=[sds(m1.shape, f32)] * 3,
        grid_spec=pltpu.PrefetchScalarGridSpec(
            num_scalar_prefetch=1,
            grid=(steps,),
            in_specs=[half, half, flat, flat] + [ANY] * len(prev),
            out_specs=[flat] * 3,
        ),
        input_output_aliases={5 + i: i for i in range(len(prev))},
        compiler_params=params(),
        cost_estimate=cost(0, own.size * 2 * 22),
        name="adam",
    )(ids, own, oth, m1, m2, *prev)


def adam_back_kernel(inv_root, ids, own, oth, m1, m2, *refs):
    wg, st, mn = refs[-3:]
    g = pick(pl.program_id(0) == ids[1], own[...], oth[...]).astype(f32) * inv_root
    rows, width = g.shape
    nb = width // 128
    for w in range(nb):
        where = pl.ds(w, rows, stride=nb)
        gw = g[:, w * 128 : (w + 1) * 128]
        step, moment = adam_rows(gw, m1[where, :], m2[where, :])
        wg[where, :] = gw
        st[where, :] = step
        mn[where, :] = moment


def adam_back(ids, own, oth, m1, m2, prev, inv_root, first_row):
    count, width = own.shape
    rows = count // 4
    blk = rows * width // 128
    base = first_row // blk
    half = pl.BlockSpec((rows, width), lambda h, i, ids: (i, 0))
    flat = pl.BlockSpec((blk, 128), lambda h, i, ids: (base + h * 4 + i, 0))
    return pl.pallas_call(
        functools.partial(adam_back_kernel, inv_root),
        out_shape=[sds(m1.shape, f32)] * 3,
        grid_spec=pltpu.PrefetchScalarGridSpec(
            num_scalar_prefetch=1,
            grid=(2, 4),
            in_specs=[half, half, flat, flat] + [ANY] * len(prev),
            out_specs=[flat] * 3,
        ),
        input_output_aliases={5 + i: i for i in range(len(prev))},
        compiler_params=params(),
        cost_estimate=cost(0, own.size * 2 * 22),
        name="adam_back",
    )(ids, own, oth, m1, m2, *prev)


def adam_tail_kernel(g, m1, m2, p1, p2, p3, wg, st, mn):
    step, moment = adam_rows(g[...], m1[...], m2[...])
    wg[...] = g[...]
    st[...] = step
    mn[...] = moment


def adam_tail(g, m1, m2, prev, first_row):
    rows = 8
    assert first_row % rows == 0 and g.shape[0] <= rows
    g = jnp.pad(g, ((0, rows - g.shape[0]), (0, 0)))
    flat = pl.BlockSpec((rows, 128), lambda i: (first_row // rows, 0))
    return pl.pallas_call(
        adam_tail_kernel,
        grid=(1,),
        out_shape=[sds(m1.shape, f32)] * 3,
        in_specs=[pl.BlockSpec((rows, 128), lambda i: (0, 0)), flat, flat] + [ANY] * 3,
        out_specs=[flat] * 3,
        input_output_aliases={3: 0, 4: 1, 5: 2},
        name="adam_norms",
    )(g, m1, m2, *prev)


def body(n, nz, tokens, cotangent, doc_ids, master, moment_one, moment_two):
    t, d = tokens.shape
    ff = (master.shape[0] * n - 4 * d) // (2 * d) - 2 * d
    me = lax.axis_index(("y", "x"))
    core = lax.axis_index("core")
    ids = jnp.stack([me, core]).astype(jnp.int32)
    rows = d // n

    own_qkv, oth_qkv, own_oi, oth_oi, own_bk, oth_bk = unpack(ids, master, n, d, ff)
    norm_share = master[-(4 * d // n) :].astype(bf16)
    norms = lax.all_gather(norm_share, ("y", "x"), axis=0, tiled=True).reshape(4, d).astype(f32)

    def fetch(own, oth):
        pieces = gather_halves(own, n)
        others = [(0, 0, oth)] + [(k, off, swap_core(p)) for k, off, p in pieces[1:]]
        return pieces, others

    w_qkv = fetch(own_qkv, oth_qkv)
    own_oi, _ = lax.optimization_barrier((own_oi, w_qkv[0][-1][2]))
    w_oi = fetch(own_oi, oth_oi)
    own_bk, _ = lax.optimization_barrier((own_bk, w_oi[0][-1][2]))
    w_bk = fetch(own_bk, oth_bk)

    doc_row = doc_ids.reshape(1, t)
    doc_col = doc_ids.reshape(t, 1)
    d_out = jnp.where(doc_col >= 0, cotangent, jnp.zeros((), bf16))

    a_one, qkv_own, qkv_oth = project_qkv(ids, tokens, norms, *w_qkv)
    att_own, lse_own = attend(qkv_own, doc_row, doc_col, d)
    att_oth, lse_oth = attend(qkv_oth, doc_row, doc_col, d)
    resid, a_two = out_proj(ids, att_own, att_oth, tokens, norms, *w_oi)
    hid_oth, slope_oth = ffn_in(ids, a_two, w_oi[1], ff)
    hid_own, slope_own = ffn_in(ids, a_two, w_oi[0], ff)

    d_out_p = swap_core(d_out)
    a_one_p = swap_core(a_one)
    a_two_p = swap_core(a_two)
    att_own_p, att_oth_p = swap_core(att_own), swap_core(att_oth)
    hid_p = swap_core(hid_oth)

    scatter = lambda g: lax.psum_scatter(g, ("y", "x"), scatter_dimension=0, tiled=True)

    grad_back = scatter(pair_grad(hid_own, hid_p, [d_out], [d_out_p], "grad_back"))
    mixed = ffn_out(ids, hid_own, hid_oth, resid, doc_col, *w_bk)
    dp_oth = pre_grad(ids, d_out, slope_oth, w_bk[1])
    dp_p = swap_core(dp_oth)
    dp_own = pre_grad(ids, d_out, slope_own, w_bk[0])
    grad_in = scatter(pair_grad(a_two, a_two_p, [dp_own], [dp_p], "grad_in"))
    d_resid, low, low_oth, gain_two, bias_two = two_grad(ids, dp_own, dp_oth, resid, d_out, norms, *w_oi)
    low_p = swap_core(low_oth)
    datt_own, datt_oth = att_grad(ids, low, *w_oi)
    grad_out = scatter(out_grad(ids, att_own, att_oth, att_own_p, att_oth_p, low, low_p))
    dqkv_oth = attend_back(qkv_oth, datt_oth, att_oth, lse_oth, doc_row, doc_col, d)
    dqkv_p = [swap_core(g) for g in dqkv_oth]
    dqkv_own = attend_back(qkv_own, datt_own, att_own, lse_own, doc_row, doc_col, d)
    grad_qkv = scatter(pair_grad(a_one, a_one_p, dqkv_own, dqkv_p, "grad_qkv"))
    input_grad, gain_one, bias_one = one_grad(ids, dqkv_own, dqkv_oth, tokens, d_resid, norms, *w_qkv)

    norm_grads = lax.psum(jnp.concatenate([gain_one, bias_one, gain_two, bias_two]), ("z", "core", "y", "x"))
    inv_root = float(t * n * nz * 2) ** (-0.5)
    share = 4 * d // n
    norm_share = lax.dynamic_slice_in_dim(norm_grads.reshape(-1), me * share, share, 0) * inv_root

    m1, m2 = moment_one.reshape(-1, 128), moment_two.reshape(-1, 128)

    def finish(g):
        g = reduce_depth(g, nz)
        return g, swap_core(g)

    nb = d // 128
    half = nb // 2
    hs = ff // n // 2
    r_qkv, r_out, r_in = rows * 3 * nb, rows * nb, rows * ff // 128
    back_at = r_qkv + r_out + r_in
    outs = adam_back(ids, *finish(grad_back), m1, m2, [], inv_root, back_at)
    places = [(hs * j + q * 128, (2 * hs * j) // 128 + q, (2 * hs * j + hs) // 128 + q) for j in range(n) for q in range(hs // 128)]
    outs = adam_columns(ids, *finish(grad_in), m1, m2, outs, inv_root, r_qkv + r_out, rows // 8, places, ff)
    places = [(w * 128, w, w + half) for w in range(half)]
    outs = adam_columns(ids, *finish(grad_out), m1, m2, outs, inv_root, r_qkv, rows // 2, places, d)
    places = [((p * half + w) * 128, p * nb + w, p * nb + w + half) for p in range(3) for w in range(half)]
    outs = adam_columns(ids, *finish(grad_qkv), m1, m2, outs, inv_root, 0, rows // 8, places, 3 * d)
    outs = adam_tail(norm_share.reshape(-1, 128), m1, m2, outs, back_at + ff // n * nb)
    weight_grad, step, moment = [o.reshape(-1) for o in outs]
    return mixed, input_grad, weight_grad, step, moment


def solution(mesh):
    dp, n = mesh.shape["dp"], mesh.shape["group"]
    fine = Mesh(mesh.devices.reshape(dp // 2, 2, n // 2, 2), ("z", "core", "y", "x"))
    tok = ("z", "core", "y", "x")
    flat = P(("y", "x"))
    in_specs = (P(tok, None), P(tok, None), P(tok), flat, flat, flat)
    out_specs = (P(tok, None), P(tok, None), flat, flat, flat)
    return jax.shard_map(
        functools.partial(body, n, dp // 2), mesh=fine, in_specs=in_specs, out_specs=out_specs, check_vma=False
    )
```

time: 1900 us -> 748 us (0.39)
  waiting for transfers between devices: 1110 us -> 264 us
  matrix products: 394 us -> 0 us
  Pallas kernels: 0 us -> 315 us
  local copies, waits for them, and re-layouts: 176 us -> 19.7 us
  other arithmetic: 139 us -> 11.8 us
  starting transfers between devices: 0.24 us -> 40.3 us
  blocking collectives: 41.7 us -> 75.1 us
    unnamed x7 -> x4, waiting for transfers between devices: 856 us -> 0.07 us
    dot_general x26 -> x0, matrix products: 394 us -> none  [the longest x4 62 us: one_block(): jnp.einsum('qhd,khd->hqk', query_blk, keys_all, preferred_element_type=jn...]
    pallas_call x0 -> x24, Pallas kernels: none -> 315 us  [the longest x3 40.6 us: pair_grad(): pl.pallas_call(functools.partial(pair_kernel, nb), grid=(m // tm,), out_s...]
    ppermute x0 -> x55, waiting for transfers between devices: none -> 194 us  [the longest x3 43.7 us: gather_halves(): hy = lax.ppermute(h, 'y', [(0, 1), (1, 0)])]
    psum x1 -> x0, waiting for transfers between devices: 175 us -> none  [body(): summed = lax.psum((owned[0], owned[1], owned[2], owned[3], owned[4]), 'dp')]
    all_gather x4 -> x0, waiting for transfers between devices: 79.4 us -> none  [the longest x1 68.5 us: body(): lax.all_gather(pieces[0], 'group', axis=0, tiled=True)]
    unnamed x143 -> x59, local copies, waits for them, and re-layouts: 90.5 us -> 11.5 us
    reduce_scatter x0 -> x4, waiting for transfers between devices: none -> 70.1 us  [body(): lax.psum_scatter(g, ('y', 'x'), scatter_dimension=0, tiled=True)]
  transfers between devices with their start and end apart: 6 -> 59, of which waited for: 4 -> 18; matrix products, arithmetic and copies ran while one was open for 14% -> 2% of each run, Pallas kernels for 0% -> 39%
where the time goes in v1:
time: 748 us; the launch traced here: 741 us
  Pallas kernels  315 us (42%)
  waiting for transfers between devices  264 us (35%)
  blocking collectives  75.1 us (10%)
  starting transfers between devices  40.3 us (5%)
  local copies, waits for them, and re-layouts  19.7 us (3%)
  between operations  15 us (2%)
  other arithmetic  11.8 us (2%)
    reduce_scatter x4, waiting for transfers between devices, body(): lax.psum_scatter(g, ('y', 'x'), scatter_dimension=0, tiled=True)  70.1 us
    ppermute x3, waiting for transfers between devices, gather_halves(): hy = lax.ppermute(h, 'y', [(0, 1), (1, 0)])  43.7 us
    pallas_call x3, Pallas kernels, pair_grad(): pl.pallas_call(functools.partial(pair_kernel, nb), grid=(m // tm,), out_s...  40.6 us
    pallas_call x2, Pallas kernels, attend(): pl.pallas_call(functools.partial(attend_kernel, hd), grid=(pairs,), out_s...  38.3 us
    psum x1, blocking collectives, body(): lax.psum(jnp.concatenate([gain_one, bias_one, gain_two, bias_two]), ('z',...  38.1 us
    all_gather x1, blocking collectives, body(): lax.all_gather(norm_share, ('y', 'x'), axis=0, tiled=True).reshape(4, d)  37.1 us
    pallas_call x3, Pallas kernels, adam_call(): pl.pallas_call(functools.partial(adam_kernel, plan, inv_root), out_shape=...  35.7 us
    pallas_call x2, Pallas kernels, attend_back(): pl.pallas_call(functools.partial(attend_back_kernel, hd), grid=(pairs,),...  35 us
  transfers between devices with their start and end apart: 59, of which 18 were waited for; matrix products, arithmetic and copies ran while one was open for 2% of the time, Pallas kernels for 39%

profile of v1, /device:TPU:0, one launch (start us, length us, event | category | flops | bytes accessed | tf_op | source)
XLA Modules:
  0.0 741.3 jit_solution(3890194217770124462)
XLA Ops:
  7.9 11.2 %unpack.1 = (bf16[256,1536]{1,0:T(8,128)(2,1)}, bf16[256,1536]{1,0:T(8,128)(2,1)}, bf16[256,2560]{1,0:T(8,128)(2,1)}, bf16[256,2560]{1,0:T(8,128)(2,1)}, bf16[51...) custom-call(s32[2]{0:T(128)} %pad_add_fusion.ids, f32[24584,128]{1,0:T(8,128)} %bitcast.27, f32[24584,128]{1,0:T(8,128)} %bitcast.28, ...), custom_call_target="tpu_custom_call" | custom-call | tf_op jit(solution)/shard_map/unpack/pallas_call | solution.py:94
  19.1 3.0 collective-permute-start.1
  22.1 17.9 %collective-permute-done.1.refs_2_.refs_11_ = bf16[256,1536]{1,0:T(8,128)(2,1)} collective-permute-done((bf16[256,1536]{1,0:T(8,128)(2,1)}, bf16[256,1536]{1,0:T(8,128)(2,1)}, u32[]{:S(2)}, u32[]{:S(2)}) %collective-permute-start.1) | collective-permute-done | bytes 786464 | tf_op jit(solution)/shard_map/ppermute | solution.py:112
  42.7 8.6 %collective-permute-done.3.refs_4_.refs_13_ = bf16[128,1536]{1,0:T(8,128)(2,1)S(1)} collective-permute-done((bf16[128,1536]{1,0:T(8,128)(2,1)S(1)}, bf16[128,1536]{1,0:T(8,128)(2,1)S(1)}, u32[]{:S(2)}, u32[]{:S(2)}) %collective-permute-start.3) | collective-permute-done | bytes 393248 | tf_op jit(solution)/shard_map/ppermute | solution.py:114
  54.8 25.8 %collective-permute-done.9.refs_2_ = bf16[256,2560]{1,0:T(8,128)(2,1)S(1)} collective-permute-done((bf16[256,2560]{1,0:T(8,128)(2,1)}, bf16[256,2560]{1,0:T(8,128)(2,1)S(1)}, u32[]{:S(2)}, u32[]{:S(2)}) %collective-permute-start.9) | collective-permute-done | bytes 1310752 | tf_op jit(solution)/shard_map/ppermute | solution.py:112
  84.9 5.9 collective-permute-done.2.refs_3_.refs_12_
  90.8 21.5 %collective-permute-done.11.refs_4_ = bf16[128,2560]{1,0:T(8,128)(2,1)S(1)} collective-permute-done((bf16[128,2560]{1,0:T(8,128)(2,1)S(1)}, bf16[128,2560]{1,0:T(8,128)(2,1)S(1)}, u32[]{:S(2)}, u32[]{:S(2)}) %collective-permute-start.11) | collective-permute-done | bytes 655392 | tf_op jit(solution)/shard_map/ppermute | solution.py:114
  118.4 37.1 %all_gather.3 = bf16[4096]{0:T(1024)(128)(2,1)S(1)} all-gather(bf16[1024]{0:T(1024)(128)(2,1)S(1)} %slice.149), channel_id=1, replica_groups=mesh['z'=4,'core'=2,'y'=2,'x'=2] {'y','x'}, dimensions={0}, use_global_device_ids=true | all-gather | bytes 10240 | tf_op jit(solution)/shard_map/all_gather | solution.py:819
  158.1 14.0 %qkv.1 = (bf16[1024,1024]{1,0:T(8,128)(2,1)}, bf16[1024,1536]{1,0:T(8,128)(2,1)}, bf16[1024,1536]{1,0:T(8,128)(2,1)}) custom-call(s32[2]{0:T(128)} %pad_add_fusion.ids, bf16[1024,1024]{1,0:T(8,128)(2,1)} %refs_6_.1, f32[4,1024]{1,0:T(4,128)} %reshape.55.norms.refs_8_, bf16[256,1536]{1,0:T(8,128)(2,1)} %get-tuple-element.57.refs_0_.refs_9_, ...), custom_call_target="tpu_custom_call" | custom-call | flops 6442450944 | bytes 16000000 | tf_op jit(solution)/shard_map/qkv/pallas_call | solution.py:189
  172.7 19.1 %attend.2 = (bf16[1024,512]{1,0:T(8,128)(2,1)}, f32[4,2,1024]{2,1,0:T(2,128)}) custom-call(bf16[1024,1536]{1,0:T(8,128)(2,1)} %get-tuple-element.59.q.k.v, bf16[1024,1536]{1,0:T(8,128)(2,1)} %get-tuple-element.59.q.k.v, bf16[1024,1536]{1,0:T(8,128)(2,1)} %get-tuple-element.59.q.k.v, s32[1,1024]{1,0:T(1,128)} %bitcast.35, s32[1024,1]{1,0:T(8,128)} %copy.28.doc_col.doc), custom_call_target="tpu_custom_call" | custom-call | flops 4294967296 | bytes 5000000 | tf_op jit(solution)/shard_map/attend/pallas_call | solution.py:253
  191.9 19.2 %attend.3 = (bf16[1024,512]{1,0:T(8,128)(2,1)}, f32[4,2,1024]{2,1,0:T(2,128)}) custom-call(bf16[1024,1536]{1,0:T(8,128)(2,1)} %get-tuple-element.61.q.k.v, bf16[1024,1536]{1,0:T(8,128)(2,1)} %get-tuple-element.61.q.k.v, bf16[1024,1536]{1,0:T(8,128)(2,1)} %get-tuple-element.61.q.k.v, s32[1,1024]{1,0:T(1,128)} %bitcast.36, s32[1024,1]{1,0:T(8,128)} %copy.28.doc_col.doc), custom_call_target="tpu_custom_call" | custom-call | flops 4294967296 | bytes 5000000 | tf_op jit(solution)/shard_map/attend/pallas_call | solution.py:253
  212.3 1.9 slice.98
  216.2 9.0 %out_proj.1 = (f32[1024,1024]{1,0:T(8,128)}, bf16[1024,1024]{1,0:T(8,128)(2,1)}) custom-call(s32[2]{0:T(128)} %pad_add_fusion.ids, bf16[1024,512]{1,0:T(8,128)(2,1)} %get-tuple-element.60.att_own.att.a_own, bf16[1024,512]{1,0:T(8,128)(2,1)} %get-tuple-element.62.att_oth.att.a_oth, bf16[1024,1024]{1,0:T(8,128)(2,1)} %refs_6_.1, ...), custom_call_target="tpu_custom_call" | custom-call | flops 2147483648 | bytes 14000000 | tf_op jit(solution)/shard_map/out_proj/pallas_call | solution.py:358
  225.8 13.6 %ffn_in.3 = (bf16[1024,2048]{1,0:T(8,128)(2,1)}, bf16[1024,2048]{1,0:T(8,128)(2,1)}) custom-call(s32[2]{0:T(128)} %pad_add_fusion.ids, bf16[1024,1024]{1,0:T(8,128)(2,1)} %get-tuple-element.66.a_two.a_mine, bf16[256,2560]{1,0:T(8,128)(2,1)} %get-tuple-element.65.refs_5_.refs_0_, bf16[256,2560]{1,0:T(8,128)(2,1)} %collective-permute-done.12.refs_6_.refs_1_, ...), custom_call_target="tpu_custom_call" | custom-call | flops 4294967296 | bytes 14000000 | tf_op jit(solution)/shard_map/ffn_in/pallas_call | solution.py:399
  240.0 13.6 %ffn_in.2 = (bf16[1024,2048]{1,0:T(8,128)(2,1)}, bf16[1024,2048]{1,0:T(8,128)(2,1)}) custom-call(s32[2]{0:T(128)} %pad_add_fusion.ids, bf16[1024,1024]{1,0:T(8,128)(2,1)} %get-tuple-element.66.a_two.a_mine, bf16[256,2560]{1,0:T(8,128)(2,1)} %get-tuple-element.64.refs_0_, bf16[256,2560]{1,0:T(8,128)(2,1)} %copy-done.1, bf16[256,2560]{1,0:T(8,128)(2,1)} %copy-done, ...), custom_call_target="tpu_custom_call" | custom-call | flops 4294967296 | bytes 14000000 | tf_op jit(solution)/shard_map/ffn_in/pallas_call | solution.py:399
  253.6 11.6 %pre_grad.2.p_own.refs_0_ = bf16[1024,2048]{1,0:T(8,128)(2,1)} custom-call(s32[2]{0:T(128)} %pad_add_fusion.ids, bf16[1024,1024]{1,0:T(8,128)(2,1)} %broadcast_select_fusion.d_out.refs_0_, bf16[1024,2048]{1,0:T(8,128)(2,1)} %get-tuple-element.73.slope, bf16[512,1024]{1,0:T(8,128)(2,1)} %get-tuple-element.71.refs_0_, ...), custom_call_target="tpu_custom_call" | custom-call | flops 4294967296 | bytes 14000000 | tf_op jit(solution)/shard_map/pre_grad/pallas_call | solution.py:474
  266.4 11.4 %pre_grad.3.p_oth = bf16[1024,2048]{1,0:T(8,128)(2,1)} custom-call(s32[2]{0:T(128)} %pad_add_fusion.ids, bf16[1024,1024]{1,0:T(8,128)(2,1)} %broadcast_select_fusion.d_out.refs_0_, bf16[1024,2048]{1,0:T(8,128)(2,1)} %get-tuple-element.74.slope, bf16[512,1024]{1,0:T(8,128)(2,1)} %get-tuple-element.72.refs_5_.refs_0_, ...), custom_call_target="tpu_custom_call" | custom-call | flops 4294967296 | bytes 14000000 | tf_op jit(solution)/shard_map/pre_grad/pallas_call | solution.py:474
  277.9 19.6 %two_grad.1 = (f32[1024,1024]{1,0:T(8,128)}, bf16[1024,1024]{1,0:T(8,128)(2,1)}, bf16[1024,512]{1,0:T(8,128)(2,1)}, f32[1,1024]{1,0:T(1,128)}, f32[1,1024]{1,0:T(1,128)}) custom-call(s32[2]{0:T(128)} %pad_add_fusion.ids, bf16[1024,2048]{1,0:T(8,128)(2,1)} %pre_grad.2.p_own.refs_0_, bf16[1024,2048]{1,0:T(8,128)(2,1)} %pre_grad.3.p_oth, ...), custom_call_target="tpu_custom_call" | custom-call | flops 8589934592 | bytes 30000000 | tf_op jit(solution)/shard_map/two_grad/pallas_call | solution.py:524
  298.1 7.0 att_grad.1
  307.1 6.8 out_grad.1
  314.0 17.6 %attend_back.3 = (bf16[1024,512]{1,0:T(8,128)(2,1)}, bf16[1024,512]{1,0:T(8,128)(2,1)}, bf16[1024,512]{1,0:T(8,128)(2,1)}) custom-call(bf16[1024,1536]{1,0:T(8,128)(2,1)} %get-tuple-element.61.q.k.v, bf16[1024,1536]{1,0:T(8,128)(2,1)} %get-tuple-element.61.q.k.v, bf16[1024,1536]{1,0:T(8,128)(2,1)} %get-tuple-element.61.q.k.v, ...), custom_call_target="tpu_custom_call" | custom-call | flops 10737418240 | bytes 8000000 | tf_op jit(solution)/shard_map/attend_back/pallas_call | solution.py:307
  332.5 17.4 %attend_back.2 = (bf16[1024,512]{1,0:T(8,128)(2,1)}, bf16[1024,512]{1,0:T(8,128)(2,1)}, bf16[1024,512]{1,0:T(8,128)(2,1)}) custom-call(bf16[1024,1536]{1,0:T(8,128)(2,1)} %get-tuple-element.59.q.k.v, bf16[1024,1536]{1,0:T(8,128)(2,1)} %get-tuple-element.59.q.k.v, bf16[1024,1536]{1,0:T(8,128)(2,1)} %get-tuple-element.59.q.k.v, ...), custom_call_target="tpu_custom_call" | custom-call | flops 10737418240 | bytes 8000000 | tf_op jit(solution)/shard_map/attend_back/pallas_call | solution.py:307
  351.6 11.5 %grad_qkv.1 = bf16[1024,1536]{1,0:T(8,128)(2,1)} custom-call(bf16[1024,1024]{1,0:T(8,128)(2,1)} %get-tuple-element.92.a_mine, bf16[1024,1024]{1,0:T(8,128)(2,1)} %collective-permute-done.24.a_theirs, bf16[1024,512]{1,0:T(8,128)(2,1)} %get-tuple-element.78.refs_0_, bf16[1024,512]{1,0:T(8,128)(2,1)} %get-tuple-element.79.refs_1_, ...), custom_call_target="tpu_custom_call" | custom-call | flops 6442450944 | bytes 14000000 | tf_op jit(solution)/shard_map/grad_qkv/pallas_call | solution.py:633
  364.7 8.6 %collective-permute-done.49.refs_1_ = bf16[1024,1024]{1,0:T(8,128)(2,1)S(1)} collective-permute-done((bf16[1024,1024]{1,0:T(8,128)(2,1)S(1)}, bf16[1024,1024]{1,0:T(8,128)(2,1)S(1)}, u32[]{:S(2)}, u32[]{:S(2)}) %collective-permute-start.49) | collective-permute-done | bytes 2097184 | tf_op jit(solution)/shard_map/ppermute | solution.py:122
  374.7 14.5 %grad_back.1 = bf16[2048,1024]{1,0:T(8,128)(2,1)} custom-call(bf16[1024,2048]{1,0:T(8,128)(2,1)} %get-tuple-element.67.h_own.a_mine, bf16[1024,2048]{1,0:T(8,128)(2,1)} %collective-permute-done.48.a_theirs, bf16[1024,1024]{1,0:T(8,128)(2,1)} %broadcast_select_fusion.d_out.refs_0_, bf16[1024,1024]{1,0:T(8,128)(2,1)} %copy-done.21), custom_call_target="tpu_custom_call" | custom-call | flops 8589934592 | bytes 14000000 | tf_op jit(solution)/shard_map/grad_back/pallas_call | solution.py:633
  390.8 8.6 %collective-permute-done.41.a_theirs = bf16[1024,1024]{1,0:T(8,128)(2,1)S(1)} collective-permute-done((bf16[1024,1024]{1,0:T(8,128)(2,1)S(1)}, bf16[1024,1024]{1,0:T(8,128)(2,1)S(1)}, u32[]{:S(2)}, u32[]{:S(2)}) %collective-permute-start.41) | collective-permute-done | bytes 2097184 | tf_op jit(solution)/shard_map/ppermute | solution.py:122
  400.7 14.6 %grad_in.1 = bf16[1024,2048]{1,0:T(8,128)(2,1)} custom-call(bf16[1024,1024]{1,0:T(8,128)(2,1)} %get-tuple-element.66.a_two.a_mine, bf16[1024,1024]{1,0:T(8,128)(2,1)} %copy-done.20, bf16[1024,2048]{1,0:T(8,128)(2,1)} %pre_grad.2.p_own.refs_0_, bf16[1024,2048]{1,0:T(8,128)(2,1)} %collective-permute-done.42.refs_1_), custom_call_target="tpu_custom_call" | custom-call | flops 8589934592 | bytes 14000000 | tf_op jit(solution)/shard_map/grad_in/pallas_call | solution.py:633
  418.0 4.0 collective-permute-done.36
  423.0 2.6 collective-permute-start.37
  425.7 16.9 %ffn_out.1 = bf16[1024,1024]{1,0:T(8,128)(2,1)} custom-call(s32[2]{0:T(128)} %pad_add_fusion.ids, bf16[1024,2048]{1,0:T(8,128)(2,1)} %get-tuple-element.67.h_own.a_mine, bf16[1024,2048]{1,0:T(8,128)(2,1)} %get-tuple-element.68.h_oth, f32[1024,1024]{1,0:T(8,128)} %get-tuple-element.69.resid, s32[1024,1]{1,0:T(8,128)} %copy.28.doc_col.doc, ...), custom_call_target="tpu_custom_call" | custom-call | flops 8589934592 | bytes 23000000 | tf_op jit(solution)/shard_map/ffn_out/pallas_call | solution.py:437
  443.1 2.0 broadcast_select_fusion.3
  446.6 16.9 %reduce-scatter.11.cloned.1.call-done = bf16[512,1024]{1,0:T(8,128)(2,1)} async-done(((bf16[2048,1024]{1,0:T(8,128)(2,1)}), bf16[512,1024]{1,0:T(8,128)(2,1)}) %reduce-scatter.11.cloned.1.call-update) | async-done | bytes 1048592 | tf_op jit(solution)/shard_map/reduce_scatter | solution.py:849
  466.4 53.2 %reduce-scatter.9.cloned.1.call-done = bf16[256,2048]{1,0:T(8,128)(2,1)} async-done(((bf16[1024,2048]{1,0:T(8,128)(2,1)}), bf16[256,2048]{1,0:T(8,128)(2,1)}) %reduce-scatter.9.cloned.1.call-update) | async-done | bytes 1048592 | tf_op jit(solution)/shard_map/reduce_scatter | solution.py:849
  522.6 2.5 collective-permute-start.51
  525.1 15.1 %collective-permute-done.43 = bf16[128,2048]{1,0:T(8,128)(2,1)S(1)} collective-permute-done((bf16[128,2048]{1,0:T(8,128)(2,1)S(1)}, bf16[128,2048]{1,0:T(8,128)(2,1)S(1)}, u32[]{:S(2)}, u32[]{:S(2)}) %collective-permute-start.43) | collective-permute-done | bytes 524320 | tf_op jit(solution)/shard_map/ppermute | solution.py:689
  544.9 19.8 %collective-permute-done.44 = bf16[64,2048]{1,0:T(8,128)(2,1)S(1)} collective-permute-done((bf16[64,2048]{1,0:T(8,128)(2,1)S(1)}, bf16[64,2048]{1,0:T(8,128)(2,1)S(1)}, u32[]{:S(2)}, u32[]{:S(2)}) %collective-permute-start.44) | collective-permute-done | bytes 262176 | tf_op jit(solution)/shard_map/ppermute | solution.py:691
  564.9 9.7 %collective-permute-done.29 = bf16[64,1536]{1,0:T(8,128)(2,1)S(1)} collective-permute-done((bf16[64,1536]{1,0:T(8,128)(2,1)S(1)}, bf16[64,1536]{1,0:T(8,128)(2,1)S(1)}, u32[]{:S(2)}, u32[]{:S(2)}) %collective-permute-start.29) | collective-permute-done | bytes 196640 | tf_op jit(solution)/shard_map/ppermute | solution.py:691
  574.7 9.7 %collective-permute-done.52 = bf16[128,1024]{1,0:T(8,128)(2,1)S(1)} collective-permute-done((bf16[128,1024]{1,0:T(8,128)(2,1)S(1)}, bf16[128,1024]{1,0:T(8,128)(2,1)S(1)}, u32[]{:S(2)}, u32[]{:S(2)}) %collective-permute-start.52) | collective-permute-done | bytes 262176 | tf_op jit(solution)/shard_map/ppermute | solution.py:692
  584.7 5.5 collective-permute-done.45
  590.4 2.1 collective-permute-start.39
  593.6 25.1 %collective-permute-done.39 = bf16[128,512]{1,0:T(8,128)(2,1)S(1)} collective-permute-done((bf16[128,512]{1,0:T(8,128)(2,1)S(1)}, bf16[128,512]{1,0:T(8,128)(2,1)S(1)}, u32[]{:S(2)}, u32[]{:S(2)}) %collective-permute-start.39) | collective-permute-done | bytes 131104 | tf_op jit(solution)/shard_map/ppermute | solution.py:693
  620.3 6.7 collective-permute-done.31
  627.4 15.6 %one_grad.1 = (bf16[1024,1024]{1,0:T(8,128)(2,1)}, f32[1,1024]{1,0:T(1,128)}, f32[1,1024]{1,0:T(1,128)}) custom-call(s32[2]{0:T(128)} %pad_add_fusion.ids, bf16[1024,512]{1,0:T(8,128)(2,1)} %get-tuple-element.78.refs_0_, bf16[1024,512]{1,0:T(8,128)(2,1)} %get-tuple-element.79.refs_1_, bf16[1024,512]{1,0:T(8,128)(2,1)} %get-tuple-element.80.refs_2_, ...), custom_call_target="tpu_custom_call" | custom-call | flops 6442450944 | bytes 22000000 | tf_op jit(solution)/shard_map/one_grad/pallas_call | solution.py:603
  643.8 38.1 %psum.7 = f32[4096]{0:T(1024)S(1)} all-reduce(f32[4096]{0:T(1024)S(1)} %bitcast.34), channel_id=1, replica_groups=mesh['z'=4,'core'=2,'y'=2,'x'=2] {'z','core','y','x'}, use_global_device_ids=true, to_apply=%region_0.1 | all-reduce | flops 4096 | bytes 32768 | tf_op jit(solution)/shard_map/psum | solution.py:867
  682.5 14.1 %adam_back.1 = (f32[24584,128]{1,0:T(8,128)}, f32[24584,128]{1,0:T(8,128)}, f32[24584,128]{1,0:T(8,128)}) custom-call(s32[2]{0:T(128)} %pad_add_fusion.ids, bf16[512,1024]{1,0:T(8,128)(2,1)} %copy-done.4, bf16[512,1024]{1,0:T(8,128)(2,1)} %collective-permute-done.54.oth, f32[24584,128]{1,0:T(8,128)} %bitcast.17, f32[24584,128]{1,0:T(8,128)} %bitcast.22), custom_call_target="tpu_custom_call" | custom-call | bytes 23068672 | tf_op jit(solution)/shard_map/adam_back/pallas_call | solution.py:770
  696.6 19.7 %adam.3 = (f32[24584,128]{1,0:T(8,128)}, f32[24584,128]{1,0:T(8,128)}, f32[24584,128]{1,0:T(8,128)}) custom-call(s32[2]{0:T(128)} %pad_add_fusion.ids, bf16[256,2048]{1,0:T(8,128)(2,1)} %copy-done.2, bf16[256,2048]{1,0:T(8,128)(2,1)} %collective-permute-done.47.oth, ...), custom_call_target="tpu_custom_call", output_to_operand_aliasing={{0}: (5, {}), {1}: (6, {}), {2}: (7, {})} | custom-call | bytes 23068672 | tf_op jit(solution)/shard_map/adam/pallas_call | solution.py:733
  716.9 4.6 adam.4
  721.5 11.4 %adam.5 = (f32[24584,128]{1,0:T(8,128)}, f32[24584,128]{1,0:T(8,128)}, f32[24584,128]{1,0:T(8,128)}) custom-call(s32[2]{0:T(128)} %pad_add_fusion.ids, bf16[256,1536]{1,0:T(8,128)(2,1)} %copy-done.7, bf16[256,1536]{1,0:T(8,128)(2,1)} %collective-permute-done.32.oth, ...), custom_call_target="tpu_custom_call", output_to_operand_aliasing={{0}: (5, {}), {1}: (6, {}), {2}: (7, {})} | custom-call | bytes 17301504 | tf_op jit(solution)/shard_map/adam/pallas_call | solution.py:733
  (197 shorter events, 60.4 us)
Async XLA Ops:
  7.2 408.3 %reduce-scatter.7.cloned.1.call-start = ((), (), s32[]{:S(2)}) async-start(), calls=%async_computation.5 | async-start | bytes 1310720 | tf_op jit(solution)/shard_map/reduce_scatter | solution.py:849
  19.1 20.8 %collective-permute-start.1 = (bf16[256,1536]{1,0:T(8,128)(2,1)}, bf16[256,1536]{1,0:T(8,128)(2,1)}, u32[]{:S(2)}, u32[]{:S(2)}) collective-permute-start(bf16[256,1536]{1,0:T(8,128)(2,1)} %get-tuple-element.57.refs_0_.refs_9_), channel_id=1, source_target_pairs={{0,2},{2,0},{1,3},{3,1},{4,6},{6,4},{5,7},{7,5},{8,10},{10,8},{9,1... | collective-permute-start | bytes 2359304 | tf_op jit(solution)/shard_map/ppermute | solution.py:112
  51.3 29.3 %collective-permute-start.9 = (bf16[256,2560]{1,0:T(8,128)(2,1)}, bf16[256,2560]{1,0:T(8,128)(2,1)S(1)}, u32[]{:S(2)}, u32[]{:S(2)}) collective-permute-start(bf16[256,2560]{1,0:T(8,128)(2,1)} %get-tuple-element.64.refs_0_), channel_id=1, source_target_pairs={{0,2},{2,0},{1,3},{3,1},{4,6},{6,4},{5,7},{7,5},{8,10},{10,8},{9,1... | collective-permute-start | bytes 3932168 | tf_op jit(solution)/shard_map/ppermute | solution.py:112
  52.8 29.0 %collective-permute-start = (bf16[256,1536]{1,0:T(8,128)(2,1)}, bf16[256,1536]{1,0:T(8,128)(2,1)}, u32[]{:S(2)}, u32[]{:S(2)}) collective-permute-start(bf16[256,1536]{1,0:T(8,128)(2,1)} %get-tuple-element.57.refs_0_.refs_9_), channel_id=1, source_target_pairs={{0,1},{1,0},{2,3},{3,2},{4,5},{5,4},{6,7},{7,6},{8,9},{9,8},{10,11... | collective-permute-start | bytes 2359304 | tf_op jit(solution)/shard_map/ppermute | solution.py:111
  54.2 58.1 %collective-permute-start.8 = (bf16[256,2560]{1,0:T(8,128)(2,1)}, bf16[256,2560]{1,0:T(8,128)(2,1)S(1)}, u32[]{:S(2)}, u32[]{:S(2)}) collective-permute-start(bf16[256,2560]{1,0:T(8,128)(2,1)} %get-tuple-element.64.refs_0_), channel_id=1, source_target_pairs={{0,1},{1,0},{2,3},{3,2},{4,5},{5,4},{6,7},{7,6},{8,9},{9,8},{10,11... | collective-permute-start | bytes 3932168 | tf_op jit(solution)/shard_map/ppermute | solution.py:111
  80.6 31.7 %collective-permute-start.11 = (bf16[128,2560]{1,0:T(8,128)(2,1)S(1)}, bf16[128,2560]{1,0:T(8,128)(2,1)S(1)}, u32[]{:S(2)}, u32[]{:S(2)}) collective-permute-start(bf16[128,2560]{1,0:T(8,128)(2,1)S(1)} %slice.97), channel_id=1, source_target_pairs={{0,1},{1,0},{2,3},{3,2},{4,5},{5,4},{6,7},{7,6},{8,9},{9,8},{10,11... | collective-permute-start | bytes 1966088 | tf_op jit(solution)/shard_map/ppermute | solution.py:114
  84.4 72.7 %collective-permute-start.5 = (bf16[256,1536]{1,0:T(8,128)(2,1)}, bf16[256,1536]{1,0:T(8,128)(2,1)}, u32[]{:S(2)}, u32[]{:S(2)}) collective-permute-start(bf16[256,1536]{1,0:T(8,128)(2,1)} %collective-permute-done.1.refs_2_.refs_11_), channel_id=1, source_target_pairs={{0,4},{4,0},{1,5},{5,1},{2,6},{6,2},{3,7},{7,3},{8,12},{12,8},{9,1... | collective-permute-start | bytes 2359304 | tf_op jit(solution)/shard_map/ppermute | solution.py:122
  84.4 73.2 %collective-permute-start.4 = (bf16[256,1536]{1,0:T(8,128)(2,1)}, bf16[256,1536]{1,0:T(8,128)(2,1)}, u32[]{:S(2)}, u32[]{:S(2)}) collective-permute-start(bf16[256,1536]{1,0:T(8,128)(2,1)} %collective-permute-done.refs_1_.refs_10_), channel_id=1, source_target_pairs={{0,4},{4,0},{1,5},{5,1},{2,6},{6,2},{3,7},{7,3},{8,12},{12,8},{9,1... | collective-permute-start | bytes 2359304 | tf_op jit(solution)/shard_map/ppermute | solution.py:122
  90.8 23.4 %collective-permute-start.7 = (bf16[128,1536]{1,0:T(8,128)(2,1)S(1)}, bf16[128,1536]{1,0:T(8,128)(2,1)S(1)}, u32[]{:S(2)}, u32[]{:S(2)}) collective-permute-start(bf16[128,1536]{1,0:T(8,128)(2,1)S(1)} %collective-permute-done.3.refs_4_.refs_13_), channel_id=1, source_target_pairs={{0,4},{4,0},{1,5},{5,1},{2,6},{6,2},{3,7},{7,3},{8,12},{12,8},{9,1... | collective-permute-start | bytes 1179656 | tf_op jit(solution)/shard_map/ppermute | solution.py:122
  112.3 44.8 %collective-permute-start.6 = (bf16[128,1536]{1,0:T(8,128)(2,1)}, bf16[128,1536]{1,0:T(8,128)(2,1)}, u32[]{:S(2)}, u32[]{:S(2)}) collective-permute-start(bf16[128,1536]{1,0:T(8,128)(2,1)} %collective-permute-done.2.refs_3_.refs_12_), channel_id=1, source_target_pairs={{0,4},{4,0},{1,5},{5,1},{2,6},{6,2},{3,7},{7,3},{8,12},{12,8},{9,1... | collective-permute-start | bytes 1179656 | tf_op jit(solution)/shard_map/ppermute | solution.py:122
  112.3 59.9 %collective-permute-start.17 = (bf16[512,1024]{1,0:T(8,128)(2,1)}, bf16[512,1024]{1,0:T(8,128)(2,1)}, u32[]{:S(2)}, u32[]{:S(2)}) collective-permute-start(bf16[512,1024]{1,0:T(8,128)(2,1)} %get-tuple-element.71.refs_0_), channel_id=1, source_target_pairs={{0,2},{2,0},{1,3},{3,1},{4,6},{6,4},{5,7},{7,5},{8,10},{10,8},{9,1... | collective-permute-start | bytes 3145736 | tf_op jit(solution)/shard_map/ppermute | solution.py:112
  115.0 57.2 %collective-permute-start.10 = (bf16[128,2560]{1,0:T(8,128)(2,1)}, bf16[128,2560]{1,0:T(8,128)(2,1)}, u32[]{:S(2)}, u32[]{:S(2)}) collective-permute-start(bf16[128,2560]{1,0:T(8,128)(2,1)} %slice.96), channel_id=1, source_target_pairs={{0,2},{2,0},{1,3},{3,1},{4,6},{6,4},{5,7},{7,5},{8,10},{10,8},{9,1... | collective-permute-start | bytes 1966088 | tf_op jit(solution)/shard_map/ppermute | solution.py:113
  157.1 59.1 %collective-permute-start.13 = (bf16[256,2560]{1,0:T(8,128)(2,1)S(1)}, bf16[256,2560]{1,0:T(8,128)(2,1)}, u32[]{:S(2)}, u32[]{:S(2)}) collective-permute-start(bf16[256,2560]{1,0:T(8,128)(2,1)S(1)} %collective-permute-done.9.refs_2_), channel_id=1, source_target_pairs={{0,4},{4,0},{1,5},{5,1},{2,6},{6,2},{3,7},{7,3},{8,12},{12,8},{9,1... | collective-permute-start | bytes 3932168 | tf_op jit(solution)/shard_map/ppermute | solution.py:122
  157.1 59.1 %collective-permute-start.12 = (bf16[256,2560]{1,0:T(8,128)(2,1)S(1)}, bf16[256,2560]{1,0:T(8,128)(2,1)}, u32[]{:S(2)}, u32[]{:S(2)}) collective-permute-start(bf16[256,2560]{1,0:T(8,128)(2,1)S(1)} %collective-permute-done.8.refs_1_), channel_id=1, source_target_pairs={{0,4},{4,0},{1,5},{5,1},{2,6},{6,2},{3,7},{7,3},{8,12},{12,8},{9,1... | collective-permute-start | bytes 3932168 | tf_op jit(solution)/shard_map/ppermute | solution.py:122
  157.6 54.5 %collective-permute-start.16 = (bf16[512,1024]{1,0:T(8,128)(2,1)}, bf16[512,1024]{1,0:T(8,128)(2,1)}, u32[]{:S(2)}, u32[]{:S(2)}) collective-permute-start(bf16[512,1024]{1,0:T(8,128)(2,1)} %get-tuple-element.71.refs_0_), channel_id=1, source_target_pairs={{0,1},{1,0},{2,3},{3,2},{4,5},{5,4},{6,7},{7,6},{8,9},{9,8},{10,11... | collective-permute-start | bytes 3145736 | tf_op jit(solution)/shard_map/ppermute | solution.py:111
  172.2 42.0 %collective-permute-start.15 = (bf16[128,2560]{1,0:T(8,128)(2,1)S(1)}, bf16[128,2560]{1,0:T(8,128)(2,1)}, u32[]{:S(2)}, u32[]{:S(2)}) collective-permute-start(bf16[128,2560]{1,0:T(8,128)(2,1)S(1)} %collective-permute-done.11.refs_4_), channel_id=1, source_target_pairs={{0,4},{4,0},{1,5},{5,1},{2,6},{6,2},{3,7},{7,3},{8,12},{12,8},{9,1... | collective-permute-start | bytes 1966088 | tf_op jit(solution)/shard_map/ppermute | solution.py:122
  172.3 43.4 %collective-permute-start.14 = (bf16[128,2560]{1,0:T(8,128)(2,1)}, bf16[128,2560]{1,0:T(8,128)(2,1)}, u32[]{:S(2)}, u32[]{:S(2)}) collective-permute-start(bf16[128,2560]{1,0:T(8,128)(2,1)} %collective-permute-done.10.refs_3_), channel_id=1, source_target_pairs={{0,4},{4,0},{1,5},{5,1},{2,6},{6,2},{3,7},{7,3},{8,12},{12,8},{9,1... | collective-permute-start | bytes 1966088 | tf_op jit(solution)/shard_map/ppermute | solution.py:122
  212.1 93.0 %collective-permute-start.33 = (bf16[1024,512]{1,0:T(8,128)(2,1)}, bf16[1024,512]{1,0:T(8,128)(2,1)}, u32[]{:S(2)}, u32[]{:S(2)}) collective-permute-start(bf16[1024,512]{1,0:T(8,128)(2,1)} %get-tuple-element.60.att_own.att.a_own), channel_id=1, source_target_pairs={{0,4},{4,0},{1,5},{5,1},{2,6},{6,2},{3,7},{7,3},{8,12},{12,8},{9,1... | collective-permute-start | bytes 3145736 | tf_op jit(solution)/shard_map/ppermute | solution.py:122
  214.1 25.3 %collective-permute-start.19 = (bf16[256,1024]{1,0:T(8,128)(2,1)S(1)}, bf16[256,1024]{1,0:T(8,128)(2,1)S(1)}, u32[]{:S(2)}, u32[]{:S(2)}) collective-permute-start(bf16[256,1024]{1,0:T(8,128)(2,1)S(1)} %slice.99), channel_id=1, source_target_pairs={{0,1},{1,0},{2,3},{3,2},{4,5},{5,4},{6,7},{7,6},{8,9},{9,8},{10,11... | collective-permute-start | bytes 1572872 | tf_op jit(solution)/shard_map/ppermute | solution.py:114
  215.6 24.0 %collective-permute-start.18 = (bf16[256,1024]{1,0:T(8,128)(2,1)}, bf16[256,1024]{1,0:T(8,128)(2,1)}, u32[]{:S(2)}, u32[]{:S(2)}) collective-permute-start(bf16[256,1024]{1,0:T(8,128)(2,1)} %slice.98), channel_id=1, source_target_pairs={{0,2},{2,0},{1,3},{3,1},{4,6},{6,4},{5,7},{7,5},{8,10},{10,8},{9,1... | collective-permute-start | bytes 1572872 | tf_op jit(solution)/shard_map/ppermute | solution.py:113
  225.2 40.2 %collective-permute-start.21 = (bf16[512,1024]{1,0:T(8,128)(2,1)}, bf16[512,1024]{1,0:T(8,128)(2,1)S(1)}, u32[]{:S(2)}, u32[]{:S(2)}) collective-permute-start(bf16[512,1024]{1,0:T(8,128)(2,1)} %collective-permute-done.17.refs_2_), channel_id=1, source_target_pairs={{0,4},{4,0},{1,5},{5,1},{2,6},{6,2},{3,7},{7,3},{8,12},{12,8},{9,1... | collective-permute-start | bytes 3145736 | tf_op jit(solution)/shard_map/ppermute | solution.py:122
  225.3 40.2 %collective-permute-start.20 = (bf16[512,1024]{1,0:T(8,128)(2,1)}, bf16[512,1024]{1,0:T(8,128)(2,1)}, u32[]{:S(2)}, u32[]{:S(2)}) collective-permute-start(bf16[512,1024]{1,0:T(8,128)(2,1)} %collective-permute-done.16.refs_1_), channel_id=1, source_target_pairs={{0,4},{4,0},{1,5},{5,1},{2,6},{6,2},{3,7},{7,3},{8,12},{12,8},{9,1... | collective-permute-start | bytes 3145736 | tf_op jit(solution)/shard_map/ppermute | solution.py:122
  239.4 25.8 %collective-permute-start.23 = (bf16[256,1024]{1,0:T(8,128)(2,1)S(1)}, bf16[256,1024]{1,0:T(8,128)(2,1)}, u32[]{:S(2)}, u32[]{:S(2)}) collective-permute-start(bf16[256,1024]{1,0:T(8,128)(2,1)S(1)} %collective-permute-done.19.refs_4_), channel_id=1, source_target_pairs={{0,4},{4,0},{1,5},{5,1},{2,6},{6,2},{3,7},{7,3},{8,12},{12,8},{9,1... | collective-permute-start | bytes 1572872 | tf_op jit(solution)/shard_map/ppermute | solution.py:122
  239.6 25.9 %collective-permute-start.22 = (bf16[256,1024]{1,0:T(8,128)(2,1)}, bf16[256,1024]{1,0:T(8,128)(2,1)}, u32[]{:S(2)}, u32[]{:S(2)}) collective-permute-start(bf16[256,1024]{1,0:T(8,128)(2,1)} %collective-permute-done.18.refs_3_), channel_id=1, source_target_pairs={{0,4},{4,0},{1,5},{5,1},{2,6},{6,2},{3,7},{7,3},{8,12},{12,8},{9,1... | collective-permute-start | bytes 1572872 | tf_op jit(solution)/shard_map/ppermute | solution.py:122
  265.3 39.9 %collective-permute-start.34 = (bf16[1024,512]{1,0:T(8,128)(2,1)S(1)}, bf16[1024,512]{1,0:T(8,128)(2,1)S(1)}, u32[]{:S(2)}, u32[]{:S(2)}) collective-permute-start(bf16[1024,512]{1,0:T(8,128)(2,1)S(1)} %copy-done.3), channel_id=1, source_target_pairs={{0,4},{4,0},{1,5},{5,1},{2,6},{6,2},{3,7},{7,3},{8,12},{12,8},{9,1... | collective-permute-start | bytes 3145736 | tf_op jit(solution)/shard_map/ppermute | solution.py:122
  298.0 51.9 %collective-permute-start.24 = (bf16[1024,1024]{1,0:T(8,128)(2,1)}, bf16[1024,1024]{1,0:T(8,128)(2,1)}, u32[]{:S(2)}, u32[]{:S(2)}) collective-permute-start(bf16[1024,1024]{1,0:T(8,128)(2,1)} %get-tuple-element.92.a_mine), channel_id=1, source_target_pairs={{0,4},{4,0},{1,5},{5,1},{2,6},{6,2},{3,7},{7,3},{8,12},{12,8},{9,1... | collective-permute-start | bytes 6291464 | tf_op jit(solution)/shard_map/ppermute | solution.py:122
  313.9 129.1 %reduce-scatter.5.cloned.1.call-start = ((), (), s32[]{:S(2)}) async-start(), calls=%async_computation.4 | async-start | bytes 3932160 | tf_op jit(solution)/shard_map/reduce_scatter | solution.py:849
  363.1 100.4 %reduce-scatter.11.cloned.1.call-start = ((), (), s32[]{:S(2)}) async-start(), calls=%async_computation.7 | async-start | bytes 5242880 | tf_op jit(solution)/shard_map/reduce_scatter | solution.py:849
  389.1 130.5 %reduce-scatter.9.cloned.1.call-start = ((), (), s32[]{:S(2)}) async-start(), calls=%async_computation.6 | async-start | bytes 5242880 | tf_op jit(solution)/shard_map/reduce_scatter | solution.py:849
  423.0 19.6 %collective-permute-start.37 = (bf16[64,512]{1,0:T(8,128)(2,1)S(1)}, bf16[64,512]{1,0:T(8,128)(2,1)S(1)}, u32[]{:S(2)}, u32[]{:S(2)}) collective-permute-start(bf16[64,512]{1,0:T(8,128)(2,1)S(1)} %broadcast_select_fusion.8), channel_id=1, source_target_pairs={{0,16},{16,0},{8,24},{24,8},{1,17},{17,1},{9,25},{25,9},{2,18},{18... | collective-permute-start | bytes 196616 | tf_op jit(solution)/shard_map/ppermute | solution.py:691
  442.6 147.7 %collective-permute-start.38 = (bf16[64,512]{1,0:T(8,128)(2,1)S(1)}, bf16[64,512]{1,0:T(8,128)(2,1)S(1)}, u32[]{:S(2)}, u32[]{:S(2)}) collective-permute-start(bf16[64,512]{1,0:T(8,128)(2,1)S(1)} %select_add_fusion.7), channel_id=1, source_target_pairs={{0,16},{16,0},{8,24},{24,8},{1,17},{17,1},{9,25},{25,9},{2,18},{18... | collective-permute-start | bytes 196616 | tf_op jit(solution)/shard_map/ppermute | solution.py:692
  445.0 77.4 %collective-permute-start.28 = (bf16[128,1536]{1,0:T(8,128)(2,1)}, bf16[128,1536]{1,0:T(8,128)(2,1)S(1)}, u32[]{:S(2)}, u32[]{:S(2)}) collective-permute-start(bf16[128,1536]{1,0:T(8,128)(2,1)} %broadcast_select_fusion.3), channel_id=1, source_target_pairs={{0,8},{8,0},{16,24},{24,16},{1,9},{9,1},{17,25},{25,17},{2,10},{10... | collective-permute-start | bytes 1179656 | tf_op jit(solution)/shard_map/ppermute | solution.py:689
  464.8 57.7 %collective-permute-start.50 = (bf16[256,1024]{1,0:T(8,128)(2,1)S(1)}, bf16[256,1024]{1,0:T(8,128)(2,1)S(1)}, u32[]{:S(2)}, u32[]{:S(2)}) collective-permute-start(bf16[256,1024]{1,0:T(8,128)(2,1)S(1)} %broadcast_select_fusion.1), channel_id=1, source_target_pairs={{0,8},{8,0},{16,24},{24,16},{1,9},{9,1},{17,25},{25,17},{2,10},{10... | collective-permute-start | bytes 1572872 | tf_op jit(solution)/shard_map/ppermute | solution.py:689
  520.9 19.3 %collective-permute-start.43 = (bf16[128,2048]{1,0:T(8,128)(2,1)S(1)}, bf16[128,2048]{1,0:T(8,128)(2,1)S(1)}, u32[]{:S(2)}, u32[]{:S(2)}) collective-permute-start(bf16[128,2048]{1,0:T(8,128)(2,1)S(1)} %broadcast_select_fusion.2), channel_id=1, source_target_pairs={{0,8},{8,0},{16,24},{24,16},{1,9},{9,1},{17,25},{25,17},{2,10},{10... | collective-permute-start | bytes 1572872 | tf_op jit(solution)/shard_map/ppermute | solution.py:689
  522.6 20.8 %collective-permute-start.51 = (bf16[128,1024]{1,0:T(8,128)(2,1)S(1)}, bf16[128,1024]{1,0:T(8,128)(2,1)S(1)}, u32[]{:S(2)}, u32[]{:S(2)}) collective-permute-start(bf16[128,1024]{1,0:T(8,128)(2,1)S(1)} %broadcast_select_fusion.4), channel_id=1, source_target_pairs={{0,16},{16,0},{8,24},{24,8},{1,17},{17,1},{9,25},{25,9},{2,18},{18... | collective-permute-start | bytes 786440 | tf_op jit(solution)/shard_map/ppermute | solution.py:691
  540.3 24.4 %collective-permute-start.44 = (bf16[64,2048]{1,0:T(8,128)(2,1)S(1)}, bf16[64,2048]{1,0:T(8,128)(2,1)S(1)}, u32[]{:S(2)}, u32[]{:S(2)}) collective-permute-start(bf16[64,2048]{1,0:T(8,128)(2,1)S(1)} %broadcast_select_fusion.5), channel_id=1, source_target_pairs={{0,16},{16,0},{8,24},{24,8},{1,17},{17,1},{9,25},{25,9},{2,18},{18... | collective-permute-start | bytes 786440 | tf_op jit(solution)/shard_map/ppermute | solution.py:691
  541.8 32.8 %collective-permute-start.29 = (bf16[64,1536]{1,0:T(8,128)(2,1)S(1)}, bf16[64,1536]{1,0:T(8,128)(2,1)S(1)}, u32[]{:S(2)}, u32[]{:S(2)}) collective-permute-start(bf16[64,1536]{1,0:T(8,128)(2,1)S(1)} %broadcast_select_fusion.6), channel_id=1, source_target_pairs={{0,16},{16,0},{8,24},{24,8},{1,17},{17,1},{9,25},{25,9},{2,18},{18... | collective-permute-start | bytes 589832 | tf_op jit(solution)/shard_map/ppermute | solution.py:691
  543.4 41.0 %collective-permute-start.52 = (bf16[128,1024]{1,0:T(8,128)(2,1)S(1)}, bf16[128,1024]{1,0:T(8,128)(2,1)S(1)}, u32[]{:S(2)}, u32[]{:S(2)}) collective-permute-start(bf16[128,1024]{1,0:T(8,128)(2,1)S(1)} %select_add_fusion.3), channel_id=1, source_target_pairs={{0,16},{16,0},{8,24},{24,8},{1,17},{17,1},{9,25},{25,9},{2,18},{18... | collective-permute-start | bytes 786440 | tf_op jit(solution)/shard_map/ppermute | solution.py:692
  564.8 25.3 %collective-permute-start.45 = (bf16[64,2048]{1,0:T(8,128)(2,1)S(1)}, bf16[64,2048]{1,0:T(8,128)(2,1)S(1)}, u32[]{:S(2)}, u32[]{:S(2)}) collective-permute-start(bf16[64,2048]{1,0:T(8,128)(2,1)S(1)} %select_add_fusion.4), channel_id=1, source_target_pairs={{0,16},{16,0},{8,24},{24,8},{1,17},{17,1},{9,25},{25,9},{2,18},{18... | collective-permute-start | bytes 786440 | tf_op jit(solution)/shard_map/ppermute | solution.py:692
  574.6 18.8 %collective-permute-start.30 = (bf16[64,1536]{1,0:T(8,128)(2,1)S(1)}, bf16[64,1536]{1,0:T(8,128)(2,1)S(1)}, u32[]{:S(2)}, u32[]{:S(2)}) collective-permute-start(bf16[64,1536]{1,0:T(8,128)(2,1)S(1)} %select_add_fusion.5), channel_id=1, source_target_pairs={{0,16},{16,0},{8,24},{24,8},{1,17},{17,1},{9,25},{25,9},{2,18},{18... | collective-permute-start | bytes 589832 | tf_op jit(solution)/shard_map/ppermute | solution.py:692
  584.6 34.3 %collective-permute-start.53 = (bf16[256,1024]{1,0:T(8,128)(2,1)S(1)}, bf16[256,1024]{1,0:T(8,128)(2,1)S(1)}, u32[]{:S(2)}, u32[]{:S(2)}) collective-permute-start(bf16[256,1024]{1,0:T(8,128)(2,1)S(1)} %maximum_select_fusion.4), channel_id=1, source_target_pairs={{0,8},{8,0},{16,24},{24,16},{1,9},{9,1},{17,25},{25,17},{2,10},{10... | collective-permute-start | bytes 1572872 | tf_op jit(solution)/shard_map/ppermute | solution.py:693
  590.2 29.7 %collective-permute-start.46 = (bf16[128,2048]{1,0:T(8,128)(2,1)S(1)}, bf16[128,2048]{1,0:T(8,128)(2,1)S(1)}, u32[]{:S(2)}, u32[]{:S(2)}) collective-permute-start(bf16[128,2048]{1,0:T(8,128)(2,1)S(1)} %maximum_select_fusion.3), channel_id=1, source_target_pairs={{0,8},{8,0},{16,24},{24,16},{1,9},{9,1},{17,25},{25,17},{2,10},{10... | collective-permute-start | bytes 1572872 | tf_op jit(solution)/shard_map/ppermute | solution.py:693
  590.4 28.4 %collective-permute-start.39 = (bf16[128,512]{1,0:T(8,128)(2,1)S(1)}, bf16[128,512]{1,0:T(8,128)(2,1)S(1)}, u32[]{:S(2)}, u32[]{:S(2)}) collective-permute-start(bf16[128,512]{1,0:T(8,128)(2,1)S(1)} %maximum_select_fusion.7), channel_id=1, source_target_pairs={{0,8},{8,0},{16,24},{24,16},{1,9},{9,1},{17,25},{25,17},{2,10},{10... | collective-permute-start | bytes 393224 | tf_op jit(solution)/shard_map/ppermute | solution.py:693
  593.5 33.5 %collective-permute-start.31 = (bf16[128,1536]{1,0:T(8,128)(2,1)S(1)}, bf16[128,1536]{1,0:T(8,128)(2,1)S(1)}, u32[]{:S(2)}, u32[]{:S(2)}) collective-permute-start(bf16[128,1536]{1,0:T(8,128)(2,1)S(1)} %maximum_select_fusion.5), channel_id=1, source_target_pairs={{0,8},{8,0},{16,24},{24,16},{1,9},{9,1},{17,25},{25,17},{2,10},{10... | collective-permute-start | bytes 1179656 | tf_op jit(solution)/shard_map/ppermute | solution.py:693
  618.8 97.4 %collective-permute-start.40 = (bf16[256,512]{1,0:T(8,128)(2,1)S(1)}, bf16[256,512]{1,0:T(8,128)(2,1)S(1)}, u32[]{:S(2)}, u32[]{:S(2)}) collective-permute-start(bf16[256,512]{1,0:T(8,128)(2,1)S(1)} %maximum_select_fusion.6.own), channel_id=1, source_target_pairs={{0,4},{4,0},{1,5},{5,1},{2,6},{6,2},{3,7},{7,3},{8,12},{12,8},{9,1... | collective-permute-start | bytes 786440 | tf_op jit(solution)/shard_map/ppermute | solution.py:122
  619.4 63.1 %collective-permute-start.54 = (bf16[512,1024]{1,0:T(8,128)(2,1)S(1)}, bf16[512,1024]{1,0:T(8,128)(2,1)}, u32[]{:S(2)}, u32[]{:S(2)}) collective-permute-start(bf16[512,1024]{1,0:T(8,128)(2,1)S(1)} %maximum_select_fusion.1.own), channel_id=1, source_target_pairs={{0,4},{4,0},{1,5},{5,1},{2,6},{6,2},{3,7},{7,3},{8,12},{12,8},{9,1... | collective-permute-start | bytes 3145736 | tf_op jit(solution)/shard_map/ppermute | solution.py:122
  620.2 76.3 %collective-permute-start.47 = (bf16[256,2048]{1,0:T(8,128)(2,1)S(1)}, bf16[256,2048]{1,0:T(8,128)(2,1)}, u32[]{:S(2)}, u32[]{:S(2)}) collective-permute-start(bf16[256,2048]{1,0:T(8,128)(2,1)S(1)} %maximum_select_fusion.own), channel_id=1, source_target_pairs={{0,4},{4,0},{1,5},{5,1},{2,6},{6,2},{3,7},{7,3},{8,12},{12,8},{9,1... | collective-permute-start | bytes 3145736 | tf_op jit(solution)/shard_map/ppermute | solution.py:122
  627.3 94.3 %collective-permute-start.32 = (bf16[256,1536]{1,0:T(8,128)(2,1)S(1)}, bf16[256,1536]{1,0:T(8,128)(2,1)}, u32[]{:S(2)}, u32[]{:S(2)}) collective-permute-start(bf16[256,1536]{1,0:T(8,128)(2,1)S(1)} %maximum_select_fusion.2.own), channel_id=1, source_target_pairs={{0,4},{4,0},{1,5},{5,1},{2,6},{6,2},{3,7},{7,3},{8,12},{12,8},{9,1... | collective-permute-start | bytes 2359304 | tf_op jit(solution)/shard_map/ppermute | solution.py:122
  (40 other events, 852.3 us)
Sparse Core Ops, SparseCore 0:
  314.1 28.1 reduce-scatter.6
  363.2 44.2 reduce-scatter.4
  410.7 52.6 reduce-scatter.10
  466.9 52.6 reduce-scatter.8

commit v2 on v0

v2 whole, which is shorter than its diff:
```python
import functools

import jax
import jax.numpy as jnp
from jax import lax
from jax.experimental import pallas as pl
from jax.experimental.pallas import tpu as pltpu
from jax.sharding import Mesh
from jax.sharding import PartitionSpec as P

HEADS = 16
EPS = 1e-05
FILL = -1e30
BETA_ONE = 0.9
BETA_TWO = 0.999
RATE = 0.001
ADAM_EPS = 1e-08
STEPS = 100.0
VMEM_MB = 60

f32 = jnp.float32
bf16 = jnp.bfloat16
ANY = pl.BlockSpec(memory_space=pl.ANY)


def params(limit=VMEM_MB):
    return pltpu.CompilerParams(vmem_limit_bytes=limit << 20)


def cost(flops, nbytes, trans=0):
    return pl.CostEstimate(flops=int(flops), bytes_accessed=int(nbytes), transcendentals=int(trans))


def sds(shape, dtype):
    return jax.ShapeDtypeStruct(shape, dtype)


def dot_nn(a, b):
    return jnp.dot(a, b, preferred_element_type=f32)


def dot_nt(a, b):
    return lax.dot_general(a, b, (((1,), (1,)), ((), ())), preferred_element_type=f32)


def dot_tn(a, b):
    return lax.dot_general(a, b, (((0,), (0,)), ((), ())), preferred_element_type=f32)


def pick(flag, a, b):
    return jnp.where(flag, a, b)


MESH = pl.DeviceIdType.MESH


def peer(*axes):
    return {a: 1 - lax.axis_index(a) for a in axes}


def greet(peers):
    barrier = pltpu.get_barrier_semaphore()
    for p in peers:
        pl.semaphore_signal(barrier, inc=1, device_id=p, device_id_type=MESH)
    pl.semaphore_wait(barrier, len(peers))


def member():
    return lax.axis_index("y") * 2 + lax.axis_index("x")


class Gather:
    COUNT = 9

    def __init__(self, own, oth, send, recv, base):
        rows = own.shape[0] // 4
        half = rows // 2
        x, y = lax.axis_index("x"), lax.axis_index("y")
        share = [y * 2 + x, y * 2 + 1 - x, (1 - y) * 2 + x, (1 - y) * 2 + 1 - x]

        def at(ref, k, off, count):
            return ref.at[pl.ds(pl.multiple_of(share[k] * rows + off, 8), count), :]

        def move(i, k, off, count, dst, to):
            return pltpu.make_async_remote_copy(
                src_ref=at(own, k, off, count), dst_ref=at(dst, k, off, count),
                send_sem=send.at[base + i], recv_sem=recv.at[base + i], device_id=peer(to), device_id_type=MESH,
            )

        self.moves = [
            move(0, 0, 0, rows, own, "x"),
            move(1, 0, 0, rows, own, "y"),
            move(2, 0, 0, rows, oth, "core"),
            move(3, 1, 0, half, own, "y"),
            move(4, 2, half, half, own, "x"),
            move(5, 1, 0, rows, oth, "core"),
            move(6, 2, 0, rows, oth, "core"),
            move(7, 3, 0, half, oth, "core"),
            move(8, 3, half, half, oth, "core"),
        ]

    def begin(self):
        for i in (0, 1, 2):
            self.moves[i].start()

    def relay(self):
        self.moves[0].wait_recv()
        self.moves[3].start()
        self.moves[5].start()
        self.moves[1].wait_recv()
        self.moves[4].start()
        self.moves[6].start()

    def finish(self):
        self.moves[3].wait_recv()
        self.moves[7].start()
        self.moves[4].wait_recv()
        self.moves[8].start()
        for i in (2, 5, 6, 7, 8):
            self.moves[i].wait_recv()
        for m in self.moves:
            m.wait_send()


def hand_over(src, dst, send, recv):
    return pltpu.make_async_remote_copy(
        src_ref=src, dst_ref=dst, send_sem=send, recv_sem=recv, device_id=peer("core"), device_id_type=MESH
    )


class Fold:
    def __init__(self, pieces, source, mine, inbox, cross, stage, total, theirs, send, recv, base):
        self.pieces = pieces
        z = lax.axis_index("z")
        self.end = (z == 0) | (z == 3)
        self.mid = (z == 1) | (z == 2)
        near, far = self.peers()
        rows = mine.shape[0] // pieces
        self.mine, self.inbox, self.across, self.stage, self.total = mine, inbox, cross, stage, total
        self.rows = [pl.ds(s * rows, rows) for s in range(pieces)]

        def move(kind, src, dst, to):
            i = base + kind
            return pltpu.make_async_remote_copy(
                src_ref=src, dst_ref=dst, send_sem=send.at[i], recv_sem=recv.at[i], device_id=to, device_id_type=MESH
            )

        self.fold = [move(4 * s, source.at[r, :], inbox.at[s], near) for s, r in enumerate(self.rows)]
        self.cross = [move(4 * s + 1, stage.at[s], cross.at[s], far) for s, r in enumerate(self.rows)]
        self.unfold = [move(4 * s + 2, total.at[r, :], total.at[r, :], near) for s, r in enumerate(self.rows)]
        self.core = [move(4 * s + 3, total.at[r, :], theirs.at[r, :], peer("core")) for s, r in enumerate(self.rows)]

    @staticmethod
    def peers():
        z = lax.axis_index("z")
        return [{"z": z + 1 - 2 * (z % 2)}, {"z": 3 - z}]

    def begin(self, s=None):
        @pl.when(self.end)
        def _():
            for m in self.fold if s is None else [self.fold[s]]:
                m.start()

    def inner(self, s):
        @pl.when(self.mid)
        def _():
            self.fold[s].wait_recv()
            both = self.mine[self.rows[s], :].astype(f32) + self.inbox[s].astype(f32)
            self.stage[s] = both.astype(bf16)
            self.cross[s].start()

    def outer(self, s):
        @pl.when(self.mid)
        def _():
            self.cross[s].wait_recv()
            both = self.stage[s].astype(f32) + self.across[s].astype(f32)
            self.total[self.rows[s], :] = both.astype(bf16)
            self.unfold[s].start()
            self.core[s].start()

    def land(self, s):
        @pl.when(self.end)
        def _():
            self.unfold[s].wait_recv()
            self.core[s].start()

    def tick(self, k):
        if 0 <= k < self.pieces:
            self.inner(k)
        if 0 <= k - 1 < self.pieces:
            self.outer(k - 1)
        if 0 <= k - 2 < self.pieces:
            self.land(k - 2)

    def finish(self):
        @pl.when(self.end)
        def _():
            for m in self.fold:
                m.wait_send()

        @pl.when(self.mid)
        def _():
            for m in self.cross + self.unfold:
                m.wait_send()

        for m in self.core:
            m.wait()


def fold_scratch(rows, cols, pieces):
    block = pltpu.VMEM((pieces, rows // pieces, cols), bf16)
    whole = pltpu.VMEM((rows, cols), bf16)
    return [whole, block, block, block, whole, whole]


class Scatter:
    COUNT = 6

    def __init__(self, pieces, grads, held, far, near, mid, total, send, recv, base):
        self.pieces = pieces
        share_rows = grads.shape[0] // 4
        rows = share_rows // pieces
        half = rows // 2
        x, y = lax.axis_index("x"), lax.axis_index("y")
        me, over_x, over_y, both = y * 2 + x, y * 2 + 1 - x, (1 - y) * 2 + x, (1 - y) * 2 + 1 - x
        self.held, self.far, self.near, self.mid, self.total = held, far, near, mid, total
        self.half = half

        def at(share, s, part):
            return pl.ds(pl.multiple_of(share * share_rows + s * rows + part * half, half), half)

        def move(i, src, dst, to):
            return pltpu.make_async_remote_copy(
                src_ref=src, dst_ref=dst, send_sem=send.at[base + i], recv_sem=recv.at[base + i],
                device_id=peer(to), device_id_type=MESH,
            )

        self.first, self.second, self.keep = [], [], []
        for s in range(pieces):
            b = 6 * s
            self.first.append([
                move(b, grads.at[at(over_x, s, 0), :], far.at[s, 0], "x"),
                move(b + 1, grads.at[at(both, s, 0), :], far.at[s, 1], "x"),
                move(b + 2, grads.at[at(over_y, s, 1), :], far.at[s, 2], "y"),
                move(b + 3, grads.at[at(both, s, 1), :], far.at[s, 3], "y"),
            ])
            self.second.append([
                move(b + 4, mid.at[s, 1], near.at[s, 0], "y"),
                move(b + 5, mid.at[s, 3], near.at[s, 1], "x"),
            ])
            self.keep.append([at(me, s, 0), at(over_y, s, 0), at(me, s, 1), at(over_x, s, 1)])

    def begin(self, s):
        for m in self.first[s]:
            m.start()

    def turn(self, s):
        for k in (1, 0, 3, 2):
            self.first[s][k].wait_recv()
            both = self.held[self.keep[s][k], :].astype(f32) + self.far[s, k].astype(f32)
            self.mid[s, k] = both.astype(bf16)
            if k == 1:
                self.second[s][0].start()
            if k == 3:
                self.second[s][1].start()

    def close(self, s):
        for part in range(2):
            self.second[s][part].wait_recv()
            both = self.mid[s, 2 * part].astype(f32) + self.near[s, part].astype(f32)
            self.total[pl.ds((2 * s + part) * self.half, self.half), :] = both.astype(bf16)

    def finish(self):
        for s in range(self.pieces):
            for m in self.first[s] + self.second[s]:
                m.wait_send()


def scatter_scratch(rows, cols, pieces):
    half = rows // 4 // pieces // 2
    four = pltpu.VMEM((pieces, 4, half, cols), bf16)
    return [pltpu.VMEM((rows, cols), bf16), four, pltpu.VMEM((pieces, 2, half, cols), bf16), four]


def swap_core(v):
    return lax.ppermute(v, "core", [(0, 1), (1, 0)])


def comm_params(cid, limit=VMEM_MB):
    if cid is None:
        return params(limit)
    return pltpu.CompilerParams(vmem_limit_bytes=limit << 20, collective_id=cid, has_side_effects=True)


def dma(count):
    return pltpu.SemaphoreType.DMA((count,))


def gain_row(norms, r, d):
    nb = d // 128
    return jnp.concatenate([norms[r * nb + i : r * nb + i + 1, :] for i in range(nb)], axis=1)


def layer_norm_parts(v):
    centre = v - jnp.mean(v, axis=-1, keepdims=True)
    r = lax.rsqrt(jnp.mean(centre * centre, axis=-1, keepdims=True) + EPS)
    return centre * r, r


def layer_norm_back(v, gain, dz):
    xhat, r = layer_norm_parts(v)
    dg = jnp.sum(dz * xhat, axis=0, keepdims=True)
    db = jnp.sum(dz, axis=0, keepdims=True)
    t = dz * gain
    dv = r * (t - jnp.mean(t, axis=-1, keepdims=True) - xhat * jnp.mean(t * xhat, axis=-1, keepdims=True))
    return dv, dg, db


def unpack_kernel(dims, m_qkv, m_out, m_norm, own_qkv, own_out, norm):
    n, d = dims
    first = lax.axis_index("core") == 0
    nb = d // 128
    half = nb // 2
    rows = own_qkv.shape[0]

    def put(ref, own, dst, lo, stride):
        a = ref[pl.ds(lo, rows, stride=stride), :]
        b = ref[pl.ds(lo + half, rows, stride=stride), :]
        own[:, dst : dst + 128] = pick(first, a, b).astype(bf16)

    for part in range(3):
        for w in range(half):
            put(m_qkv, own_qkv, (part * half + w) * 128, part * nb + w, 3 * nb)
    for w in range(half):
        put(m_out, own_out, w * 128, w, nb)
    norm[...] = m_norm[...].astype(bf16).astype(f32)


def group_index(n):
    return lax.axis_index(("y", "x"))


def unpack_first(lanes, n, d, ff):
    rows = d // n
    nb = d // 128
    r1, r2, r3, r4 = rows * 3 * nb, rows * nb, rows * ff // 128, ff // n * nb
    steps = 4 if n == 4 else 2
    sr = rows // steps
    me = lambda: group_index(n)
    return pl.pallas_call(
        functools.partial(unpack_kernel, (n, d)),
        grid=(steps,),
        out_shape=[sds((d, 3 * d // 2), bf16), sds((d, d // 2), bf16), sds((8, 128), f32)],
        in_specs=[
            pl.BlockSpec((r1 // steps, 128), lambda i: (i, 0)),
            pl.BlockSpec((r2 // steps, 128), lambda i: (r1 // (r2 // steps) + i, 0)),
            pl.BlockSpec((8, 128), lambda i: ((r1 + r2 + r3 + r4) // 8, 0)),
        ],
        out_specs=[
            pl.BlockSpec((sr, 3 * d // 2), lambda i: (me() * steps + i, 0)),
            pl.BlockSpec((sr, d // 2), lambda i: (me() * steps + i, 0)),
            pl.BlockSpec((8, 128), lambda i: (0, 0)),
        ],
        compiler_params=params(),
        name="unpack",
    )(lanes, lanes, lanes)


UNPACK_STEPS = 8


def qkv_kernel(cfg, tok, norm_share, m_in, m_back, w_own_in, w_oth_in, o_own_in, o_oth_in, *refs):
    n, d, comm = cfg
    (a_out, qkv, own_in, own_bk, w_own, w_oth, o_own, o_oth, norms_out, norms, w, lsem, send, recv) = refs
    if not comm:
        w_own, w_oth = w_own_in, w_oth_in
    step = pl.program_id(0)
    nb = d // 128
    half = 3 * d // 2

    if comm:
        me = member()
        near = [peer("x"), peer("y"), peer("x", "y")]
        mine = pl.ds(pl.multiple_of(me * 8, 8), 8)
        notes = [
            pltpu.make_async_remote_copy(
                src_ref=norm_share, dst_ref=norms.at[mine, :], send_sem=send.at[18 + i], recv_sem=recv.at[18 + i],
                device_id=p, device_id_type=MESH,
            )
            for i, p in enumerate(near)
        ]
        first = Gather(w_own, w_oth, send, recv, 0)
        second = Gather(o_own, o_oth, send, recv, 9)

        @pl.when(step == 0)
        def _():
            greet(near + [peer("core")])
            for m in notes:
                m.start()
            first.begin()
            norms[mine, :] = norm_share[...]

    @pl.when(step < UNPACK_STEPS)
    def _():
        core = lax.axis_index("core") == 0
        rows = own_in.shape[0]
        hs = own_in.shape[1] // n
        for j in range(n):
            for q in range(hs // 128):
                lo = (2 * hs * j) // 128 + q
                stride = m_in.shape[0] // rows
                a = m_in[pl.ds(lo, rows, stride=stride), :]
                b = m_in[pl.ds(lo + hs // 128, rows, stride=stride), :]
                at = hs * j + q * 128
                own_in[:, at : at + 128] = pick(core, a, b).astype(bf16)
        for q in range(nb):
            own_bk[:, q * 128 : (q + 1) * 128] = m_back[pl.ds(q, own_bk.shape[0], stride=nb), :].astype(bf16)

    @pl.when(step == UNPACK_STEPS)
    def _():
        if comm:
            for m in notes:
                m.wait()
            first.relay()
            second.begin()
            first.finish()
            norms_out[...] = norms[...]
        else:
            norms[...] = norm_share[...]
            norms_out[...] = norms[...]
        cps = [
            pltpu.make_async_copy(w_own, w.at[:, pl.ds(0, half)], lsem.at[0]),
            pltpu.make_async_copy(w_oth, w.at[:, pl.ds(half, half)], lsem.at[1]),
        ]
        for cp in cps:
            cp.start()
        for cp in cps:
            cp.wait()

    @pl.when(step >= UNPACK_STEPS)
    def _():
        xhat, _ = layer_norm_parts(tok[...].astype(f32))
        a = (xhat * gain_row(norms, 0, d) + gain_row(norms, 1, d)).astype(bf16)
        a_out[...] = a
        acc = dot_nn(a, w[...])
        scale = (d // HEADS) ** (-0.5)
        q = d // 2
        for o in (0, half):
            qkv[:, o : o + q] = (acc[:, o : o + q].astype(bf16).astype(f32) * scale).astype(bf16)
            qkv[:, o + q : o + half] = acc[:, o + q : o + half].astype(bf16)

    if comm:

        @pl.when(step == UNPACK_STEPS + 2)
        def _():
            second.relay()

        @pl.when(step == pl.num_programs(0) - 1)
        def _():
            second.finish()


def project_qkv(lanes, tok, norm_share, w, o, n, ff, comm, tm=256):
    t, d = tok.shape
    rows = d // n
    nb = d // 128
    hs = ff // n // 2
    r_in, r_bk = rows * ff // 128, ff // n * nb
    at_in, at_bk = rows * 4 * nb, rows * 4 * nb + r_in
    b_in, b_bk = r_in // UNPACK_STEPS, hs * nb // UNPACK_STEPS
    assert at_in % b_in == 0 and at_bk % b_bk == 0
    up = lambda i: jnp.minimum(i, UNPACK_STEPS - 1)
    tk = lambda i: jnp.maximum(i - UNPACK_STEPS, 0)
    me = lambda: group_index(n)
    blk = lambda wd: pl.BlockSpec((tm, wd), lambda i: (tk(i), 0))
    whole = lambda a: pl.BlockSpec(a.shape, lambda i: (0, 0))
    half = 3 * d // 2
    w_oth = [] if comm else [w[1], o[1]]
    shapes = [sds((t, d), bf16), sds((t, 3 * d), bf16), sds((d, ff // 2), bf16), sds((ff // 2, d), bf16),
              sds((d, half), bf16), sds((d, half), bf16), sds((d, d // 2), bf16), sds((d, d // 2), bf16), sds((4 * nb, 128), f32)]
    if not comm:
        w_args = [w[0], w[1], o[0], o[1]]
    else:
        w_args = [w, norm_share, o, norm_share]
    outs = pl.pallas_call(
        functools.partial(qkv_kernel, (n, d, comm)),
        grid=(UNPACK_STEPS + t // tm,),
        out_shape=shapes,
        in_specs=[
            blk(d), whole(norm_share),
            pl.BlockSpec((b_in, 128), lambda i: (at_in // b_in + up(i), 0)),
            pl.BlockSpec((b_bk, 128), lambda i: (at_bk // b_bk + lax.axis_index("core") * UNPACK_STEPS + up(i), 0)),
            ANY, ANY, ANY, ANY,
        ],
        out_specs=[
            blk(d), blk(3 * d),
            pl.BlockSpec((rows // UNPACK_STEPS, ff // 2), lambda i: (me() * UNPACK_STEPS + up(i), 0)),
            pl.BlockSpec((hs // UNPACK_STEPS, d), lambda i: (me() * UNPACK_STEPS + up(i), 0)),
            ANY, ANY, ANY, ANY, pl.BlockSpec((4 * nb, 128), lambda i: (0, 0)),
        ],
        scratch_shapes=[pltpu.VMEM((4 * nb, 128), f32), pltpu.VMEM((d, 3 * d), bf16), dma(2), dma(21), dma(21)],
        input_output_aliases={4: 4, 6: 6},
        compiler_params=comm_params(1 if comm else None),
        cost_estimate=cost(2 * t * d * 3 * d, 40e6),
        name="qkv",
    )(tok, norm_share, lanes, lanes, *w_args)
    if comm:
        return outs
    return [*outs[:4], w[0], w[1], o[0], o[1], outs[8]]


QB = 256


def fill_bias(bias, doc_row, doc_col):
    t = bias.shape[0]
    for r in range(0, t, QB):
        key = r + lax.broadcasted_iota(jnp.int32, (QB, t), 0)
        query = lax.broadcasted_iota(jnp.int32, (QB, t), 1)
        ok = (doc_col[r : r + QB, :] == doc_row[...]) & (key <= query)
        bias[r : r + QB, :] = jnp.where(ok, 0.0, FILL)


def head_lanes(v, h, hd):
    lane = lax.broadcasted_iota(jnp.int32, v.shape, 1)
    return jnp.where((lane >= h * hd) & (lane < (h + 1) * hd), v, jnp.zeros_like(v))


def attend_kernel(cfg, q, k, v, doc_row, doc_col, w_own_in, a_one, d_out, out, lse, w_own, w_oth, a_p, d_p, bias, send, recv):
    hd, comm = cfg
    step = pl.program_id(0)
    last = pl.num_programs(0) - 1
    if comm:
        gather = Gather(w_own, w_oth, send, recv, 0)
        swaps = [hand_over(a_one, a_p, send.at[9], recv.at[9]), hand_over(d_out, d_p, send.at[10], recv.at[10])]

        @pl.when(step == 0)
        def _():
            greet([peer("x"), peer("y"), peer("core")])
            gather.begin()
            for s in swaps:
                s.start()

        @pl.when(step == 5)
        def _():
            gather.relay()

    @pl.when(step == 0)
    def _():
        fill_bias(bias, doc_row, doc_col)

    t = q.shape[0]
    vt = v[...].T
    per = 128 // hd
    qs = [head_lanes(q[...], h, hd) for h in range(per)]
    for i in range(t // QB):
        n = (i + 1) * QB
        cols = slice(i * QB, n)
        outs = []
        for h in range(per):
            s = dot_nt(k[:n, :], qs[h][cols, :]) + bias[:n, cols]
            top = jnp.max(s, axis=0, keepdims=True)
            e = jnp.exp(s - top)
            total = jnp.sum(e, axis=0, keepdims=True)
            lse[0, h : h + 1, cols] = top + jnp.log(total)
            o = dot_nn(vt[h * hd : (h + 1) * hd, :n], e.astype(bf16))
            outs.append(o / total)
        out[cols, :] = jnp.concatenate(outs, axis=0).T.astype(bf16)

    if comm:

        @pl.when(step == last)
        def _():
            gather.finish()
            for s in swaps:
                s.wait()


def head_column(d, part):
    pairs = d // 256
    return lambda p: (0, (p // pairs) * 3 * pairs + part * pairs + p % pairs)


def attend(qkv, doc_row, doc_col, w_own, a_one, d_out, d, comm):
    t = qkv.shape[0]
    pairs = d // 128
    hd = d // HEADS
    per = 128 // hd
    col = lambda part: pl.BlockSpec((t, 128), head_column(d, part))
    outs = pl.pallas_call(
        functools.partial(attend_kernel, (hd, comm)),
        grid=(pairs,),
        out_shape=[sds((t, d), bf16), sds((pairs, per, t), f32), sds(w_own.shape, bf16), sds(w_own.shape, bf16),
                   sds((t, d), bf16), sds((t, d), bf16)],
        in_specs=[col(0), col(1), col(2), pl.BlockSpec((1, t), lambda p: (0, 0)), pl.BlockSpec((t, 1), lambda p: (0, 0)),
                  ANY, ANY, ANY],
        out_specs=[pl.BlockSpec((t, 128), lambda p: (0, p)), pl.BlockSpec((1, per, t), lambda p: (p, 0, 0)), ANY, ANY, ANY, ANY],
        scratch_shapes=[pltpu.VMEM((t, t), f32), dma(11), dma(11)],
        input_output_aliases={5: 2},
        compiler_params=comm_params(2 if comm else None),
        cost_estimate=cost(8 * t * t * d, 10e6, t * t * HEADS),
        name="attend",
    )(qkv, qkv, qkv, doc_row, doc_col, w_own, a_one, d_out)
    if comm:
        return outs
    full, oth = spread(w_own)
    return outs[0], outs[1], full, oth, swap_core(a_one), swap_core(d_out)


def spread(own):
    n = lax.axis_size("y") * lax.axis_size("x")
    rows = own.shape[0] // n
    mine = lax.dynamic_slice_in_dim(own, lax.axis_index(("y", "x")) * rows, rows, 0)
    full = lax.all_gather(mine, ("y", "x"), axis=0, tiled=True)
    return full, swap_core(full)


def attend_back_kernel(cfg, q, k, v, dout, att, lse, doc_row, doc_col, part_sum, dq, dk, dv, sent, red, red_p, *refs):
    hd, comm, deep = cfg
    bias, dk_acc, dv_acc, stage, lsem, send, recv = refs[:7]
    step = pl.program_id(0)
    pairs = q_pairs(stage)

    def hand(p, part):
        wide = 128 * pairs
        cols = pl.ds(pl.multiple_of(part * wide + p * 128, 128), 128)
        i = p * 3 + part
        return hand_over(stage.at[i], sent.at[:, cols], send.at[i], recv.at[i])

    if comm:

        if deep:
            fold = Fold(PIECES, part_sum, refs[7], *refs[8:13], send, recv, 3 * pairs)

        @pl.when(step == 0)
        def _():
            greet([peer("core")] + (Fold.peers() if deep else []))
            if deep:
                load = pltpu.make_async_copy(part_sum, refs[7], lsem.at[0])
                load.start()
                fold.begin()
                load.wait()

        @pl.when((step > 0) & (step <= pairs))
        def _():
            for part in range(3):
                hand(step - 1, part).start()

    @pl.when(step == 0)
    def _():
        fill_bias(bias, doc_row, doc_col)

    t = q.shape[0]
    per = 128 // hd
    scale = hd ** (-0.5)
    kt = k[...].T
    prod = (dout[...].astype(f32) * att[...].astype(f32)).T
    inner = [jnp.sum(prod[h * hd : (h + 1) * hd, :], axis=0, keepdims=True) for h in range(per)]
    qs = [head_lanes(q[...], h, hd) for h in range(per)]
    ds_ = [head_lanes(dout[...], h, hd) for h in range(per)]
    dk_acc[...] = jnp.zeros_like(dk_acc)
    dv_acc[...] = jnp.zeros_like(dv_acc)
    for i in range(t // QB):
        if deep and i % 2 == 0:
            for at in range(2 * pairs):
                beat = 2 * at + i // 2 - 3
                if 0 <= beat < PIECES + 2:

                    @pl.when(step == at)
                    def _():
                        fold.tick(beat)

        n = (i + 1) * QB
        cols = slice(i * QB, n)
        dqs = []
        for h in range(per):
            qh, dh = qs[h][cols, :], ds_[h][cols, :]
            s = dot_nt(k[:n, :], qh) + bias[:n, cols]
            p = jnp.exp(s - lse[0, h : h + 1, cols])
            dp = dot_nt(v[:n, :], dh)
            g = (p * (dp - inner[h][:, cols])).astype(bf16)
            dv_acc[:n, :] += dot_nn(p.astype(bf16), dh)
            dk_acc[:n, :] += dot_nn(g, qh)
            dqs.append(dot_nn(kt[h * hd : (h + 1) * hd, :n], g))
        dq[cols, :] = (jnp.concatenate(dqs, axis=0).T * scale).astype(bf16)
    dk[...] = dk_acc[...].astype(bf16)
    dv[...] = dv_acc[...].astype(bf16)

    if comm:

        @pl.when(step < pairs)
        def _():
            stage[step * 3] = dq[...]
            stage[step * 3 + 1] = dk[...]
            stage[step * 3 + 2] = dv[...]

        @pl.when(step == 2 * pairs - 1)
        def _():
            for p in range(pairs):
                for part in range(3):
                    hand(p, part).wait()
            if deep:
                fold.finish()
                put_away(refs[11], red, refs[12], red_p, lsem)


def q_pairs(stage):
    return stage.shape[0] // 3


def put_away(total, red, theirs, red_p, lsem):
    cps = [pltpu.make_async_copy(total, red, lsem.at[0]), pltpu.make_async_copy(theirs, red_p, lsem.at[1])]
    for cp in cps:
        cp.start()
    for cp in cps:
        cp.wait()


PIECES = 8


def attend_back(qkv, dout, att, lse, doc_row, doc_col, part_sum, d, comm, deep):
    t = qkv.shape[0]
    pairs = d // 128
    half = pairs // 2
    hd = d // HEADS
    per = 128 // hd
    turn = lambda p: (p + half) % pairs
    col = lambda part: pl.BlockSpec((t, 128), lambda p: head_column(d, part)(turn(p)))
    one = pl.BlockSpec((t, 128), lambda p: (0, turn(p)))
    outs = pl.pallas_call(
        functools.partial(attend_back_kernel, (hd, comm, deep)),
        grid=(pairs,),
        out_shape=[sds((t, d), bf16)] * 3 + [sds((t, 3 * d // 2), bf16)] + [sds(part_sum.shape, bf16)] * 2,
        in_specs=[col(0), col(1), col(2), one, one, pl.BlockSpec((1, per, t), lambda p: (turn(p), 0, 0)),
                  pl.BlockSpec((1, t), lambda p: (0, 0)), pl.BlockSpec((t, 1), lambda p: (0, 0)), ANY],
        out_specs=[one, one, one, ANY, ANY, ANY],
        scratch_shapes=[pltpu.VMEM((t, t), f32), pltpu.VMEM((t, 128), f32), pltpu.VMEM((t, 128), f32),
                        pltpu.VMEM((3 * half, t, 128), bf16), dma(2), dma(3 * half + 4 * PIECES), dma(3 * half + 4 * PIECES)]
        + (fold_scratch(*part_sum.shape, PIECES) if deep else []),
        compiler_params=comm_params(6 if comm else None),
        cost_estimate=cost(20 * t * t * d, 16e6, t * t * HEADS),
        name="attend_back",
    )(qkv, qkv, qkv, dout, att, lse, doc_row, doc_col, part_sum)
    sent = outs[3] if comm else swap_core(jnp.concatenate([g[:, d // 2 :] for g in outs[:3]], axis=1))
    return outs[0], outs[1], outs[2], sent, both_halves(part_sum, outs[4], outs[5], comm and deep)


def both_halves(part_sum, red, red_p, done):
    if done:
        return red, red_p
    full = lax.psum(part_sum.astype(f32), "z").astype(bf16)
    return full, swap_core(full)


def middle_kernel(cfg, att_rows, tok, norms, o_own, o_oth, w_own, w_oth, att_all, bk_own_in, *refs):
    d, tm, blk, comm = cfg
    (resid, a_two_out, hidden, slope, bk_own, bk_oth, hid_p, att_p, w, a_two, stage, lsem, send, recv) = refs
    step = pl.program_id(0)
    last = pl.num_programs(0) - 1
    t = a_two.shape[0]
    pro = t // tm
    half = d // 2
    wide = hid_p.shape[1]
    nb = wide // blk
    core = lax.axis_index("core")

    def hand(j):
        cols = pl.ds(pl.multiple_of(j * blk, blk), blk)
        return hand_over(stage.at[j], hid_p.at[:, cols], send.at[10 + j], recv.at[10 + j])

    if comm:
        gather = Gather(bk_own, bk_oth, send, recv, 0)
        swap = hand_over(att_all, att_p, send.at[9], recv.at[9])

        @pl.when(step == 0)
        def _():
            greet([peer("x"), peer("y"), peer("core")])
            gather.begin()
            swap.start()

        @pl.when(step == pro + nb + 1)
        def _():
            gather.relay()

        @pl.when((step > pro) & (step <= pro + nb))
        def _():
            hand(step - pro - 1).start()

    @pl.when(step == 0)
    def _():
        lo = pl.multiple_of(core * half, half)
        hi = pl.multiple_of((1 - core) * half, half)
        cps = [
            pltpu.make_async_copy(o_own, w.at[:, pl.ds(lo, half)], lsem.at[0]),
            pltpu.make_async_copy(o_oth, w.at[:, pl.ds(hi, half)], lsem.at[1]),
        ]
        for cp in cps:
            cp.start()
        for cp in cps:
            cp.wait()

    @pl.when(step < pro)
    def _():
        lo = pl.multiple_of(core * half, half)
        hi = pl.multiple_of((1 - core) * half, half)
        y = dot_nn(att_rows[:, :half], w[pl.ds(lo, half), :]) + dot_nn(att_rows[:, half:], w[pl.ds(hi, half), :])
        r = tok[...].astype(f32) + y
        resid[...] = r
        xhat, _ = layer_norm_parts(r)
        a = (xhat * gain_row(norms, 2, d) + gain_row(norms, 3, d)).astype(bf16)
        a_two_out[...] = a
        a_two[pl.ds(pl.multiple_of(step * tm, tm), tm), :] = a

    def unit(w_blk):
        pre = dot_nn(a_two[...], w_blk)
        cdf = 0.5 + 0.5 * lax.erf(pre * (0.5**0.5))
        pdf = jnp.exp(-0.5 * pre * pre) * 0.3989422804014327
        h = (pre * cdf).astype(bf16)
        hidden[...] = h
        slope[...] = (cdf + pre * pdf).astype(bf16)
        return h

    @pl.when((step >= pro) & (step < pro + nb))
    def _():
        h = unit(w_oth[...])
        if comm:
            stage[step - pro] = h

    @pl.when(step >= pro + nb)
    def _():
        unit(w_own[...])

    if comm:

        @pl.when(step == last)
        def _():
            gather.finish()
            swap.wait()
            for j in range(nb):
                hand(j).wait()


def middle(att, tok, norms, o_own, o_oth, w_own, w_oth, bk_own, comm, tm=256, blk=512):
    t, d = tok.shape
    wide = w_own.shape[1]
    pro, nb = t // tm, wide // blk
    rowi = lambda i: jnp.minimum(i, pro - 1)
    oth = lambda i: jnp.clip(i - pro, 0, nb - 1)
    own = lambda i: jnp.clip(i - pro - nb, 0, nb - 1)
    both = lambda i: jnp.where(i < pro + nb, nb + oth(i), own(i))
    rows = lambda wd: pl.BlockSpec((tm, wd), lambda i: (rowi(i), 0))
    outs = pl.pallas_call(
        functools.partial(middle_kernel, (d, tm, blk, comm)),
        grid=(pro + 2 * nb,),
        out_shape=[sds((t, d), f32), sds((t, d), bf16), sds((t, 2 * wide), bf16), sds((t, 2 * wide), bf16),
                   sds(bk_own.shape, bf16), sds(bk_own.shape, bf16), sds((t, wide), bf16), sds((t, d), bf16)],
        in_specs=[rows(d), rows(d), pl.BlockSpec(norms.shape, lambda i: (0, 0)), ANY, ANY,
                  pl.BlockSpec((d, blk), lambda i: (0, own(i))), pl.BlockSpec((d, blk), lambda i: (0, oth(i))), ANY, ANY],
        out_specs=[rows(d), rows(d), pl.BlockSpec((t, blk), lambda i: (0, both(i))), pl.BlockSpec((t, blk), lambda i: (0, both(i))),
                   ANY, ANY, ANY, ANY],
        scratch_shapes=[pltpu.VMEM((d, d), bf16), pltpu.VMEM((t, d), bf16), pltpu.VMEM((nb, t, blk), bf16), dma(2), dma(10 + nb), dma(10 + nb)],
        input_output_aliases={8: 4},
        compiler_params=comm_params(3 if comm else None),
        cost_estimate=cost(2 * t * d * d + 4 * t * d * wide, 44e6, 4 * t * wide),
        name="middle",
    )(att, tok, norms, o_own, o_oth, w_own, w_oth, att, bk_own)
    if comm:
        return outs
    full, other = spread(bk_own)
    return [*outs[:4], full, other, swap_core(outs[2][:, wide:]), swap_core(att)]


def pre_grad_kernel(comm, d_out, slope, w_own, w_oth, a_two, d_pre, sent, a_p, stage, send, recv):
    step = pl.program_id(0)
    nb = pl.num_programs(0) // 2
    blk = slope.shape[1]

    def hand(j):
        cols = pl.ds(pl.multiple_of(j * blk, blk), blk)
        return hand_over(stage.at[j], sent.at[:, cols], send.at[1 + j], recv.at[1 + j])

    if comm:
        swap = hand_over(a_two, a_p, send.at[0], recv.at[0])

        @pl.when(step == 0)
        def _():
            greet([peer("core")])
            swap.start()

        @pl.when((step > 0) & (step <= nb))
        def _():
            hand(step - 1).start()

    @pl.when(step < nb)
    def _():
        g = (dot_nt(d_out[...], w_oth[...]) * slope[...].astype(f32)).astype(bf16)
        d_pre[...] = g
        if comm:
            stage[step] = g

    @pl.when(step >= nb)
    def _():
        d_pre[...] = (dot_nt(d_out[...], w_own[...]) * slope[...].astype(f32)).astype(bf16)

    if comm:

        @pl.when(step == 2 * nb - 1)
        def _():
            swap.wait()
            for j in range(nb):
                hand(j).wait()


def pre_grad(d_out, slope, own, oth, a_two, comm, blk=512):
    t, d = d_out.shape
    half = own.shape[0]
    nb = half // blk
    col = pl.BlockSpec((t, blk), lambda i: (0, (i + nb) % (2 * nb)))
    outs = pl.pallas_call(
        functools.partial(pre_grad_kernel, comm),
        grid=(2 * nb,),
        out_shape=[sds((t, 2 * half), bf16), sds((t, half), bf16), sds((t, d), bf16)],
        in_specs=[pl.BlockSpec((t, d), lambda i: (0, 0)), col,
                  pl.BlockSpec((blk, d), lambda i: (jnp.maximum(i - nb, 0), 0)),
                  pl.BlockSpec((blk, d), lambda i: (jnp.minimum(i, nb - 1), 0)), ANY],
        out_specs=[col, ANY, ANY],
        scratch_shapes=[pltpu.VMEM((nb, t, blk), bf16), dma(1 + nb), dma(1 + nb)],
        compiler_params=comm_params(4 if comm else None),
        cost_estimate=cost(4 * t * d * half, 28e6),
        name="pre_grad",
    )(d_out, slope, own, oth, a_two)
    if comm:
        return outs
    return outs[0], swap_core(outs[0][:, half:]), swap_core(a_two)


def two_grad_kernel(comm, d_pre, resid, d_out, norms, w_own, w_oth, o_own, o_oth, *refs):
    d_resid, low, d_att, dg, db, sent, w, wo, stage, lsem, send, recv = refs
    step = pl.program_id(0)
    tm, d = resid.shape
    half = d // 2
    wide = w_own.shape[1]
    core = lax.axis_index("core")
    here = pl.ds(pl.multiple_of(step * tm, tm), tm)

    def hand():
        return hand_over(stage.at[here, :], sent.at[here, :], send.at[step], recv.at[step])

    @pl.when(step == 0)
    def _():
        if comm:
            greet([peer("core")])
        lo = pl.multiple_of(core * half, half)
        hi = pl.multiple_of((1 - core) * half, half)
        cps = [
            pltpu.make_async_copy(w_own, w.at[:, pl.ds(0, wide)], lsem.at[0]),
            pltpu.make_async_copy(w_oth, w.at[:, pl.ds(wide, wide)], lsem.at[1]),
            pltpu.make_async_copy(o_own, wo.at[:, pl.ds(lo, half)], lsem.at[2]),
            pltpu.make_async_copy(o_oth, wo.at[:, pl.ds(hi, half)], lsem.at[3]),
        ]
        for cp in cps:
            cp.start()
        for cp in cps:
            cp.wait()
        dg[...] = jnp.zeros_like(dg)
        db[...] = jnp.zeros_like(db)

    dz = dot_nt(d_pre[...], w[...])
    dv, g, b = layer_norm_back(resid[...], gain_row(norms, 2, d), dz)
    dg[...] += g
    db[...] += b
    dr = d_out[...].astype(f32) + dv
    d_resid[...] = dr
    dl = dr.astype(bf16)
    low[...] = dl
    stage[here, :] = pick(core == 0, dl[:, half:], dl[:, :half])
    lo = pl.multiple_of(core * half, half)
    hi = pl.multiple_of((1 - core) * half, half)
    d_att[:, :half] = dot_nt(dl, wo[pl.ds(lo, half), :]).astype(bf16)
    d_att[:, half:] = dot_nt(dl, wo[pl.ds(hi, half), :]).astype(bf16)
    if comm:
        hand().start()

        @pl.when(step == pl.num_programs(0) - 1)
        def _():
            for s in range(stage.shape[0] // tm):
                rows = pl.ds(s * tm, tm)
                hand_over(stage.at[rows, :], sent.at[rows, :], send.at[s], recv.at[s]).wait()


def two_grad(d_pre, resid, d_out, norms, w_own, w_oth, o_own, o_oth, comm, tm=256):
    t, wide = d_pre.shape
    d = resid.shape[1]
    blk = lambda w: pl.BlockSpec((tm, w), lambda i: (i, 0))
    row = pl.BlockSpec((1, d), lambda i: (0, 0))
    outs = pl.pallas_call(
        functools.partial(two_grad_kernel, comm),
        grid=(t // tm,),
        out_shape=[sds((t, d), f32), sds((t, d), bf16), sds((t, d), bf16), sds((1, d), f32), sds((1, d), f32), sds((t, d // 2), bf16)],
        in_specs=[blk(wide), blk(d), blk(d), pl.BlockSpec(norms.shape, lambda i: (0, 0)), ANY, ANY, ANY, ANY],
        out_specs=[blk(d), blk(d), blk(d), row, row, ANY],
        scratch_shapes=[pltpu.VMEM((d, wide), bf16), pltpu.VMEM((d, d), bf16), pltpu.VMEM((t, d // 2), bf16),
                        dma(4), dma(t // tm), dma(t // tm)],
        compiler_params=comm_params(5 if comm else None),
        cost_estimate=cost(2 * t * d * (wide + d), 34e6),
        name="two_grad",
    )(d_pre, resid, d_out, norms, w_own, w_oth, o_own, o_oth)
    if comm:
        return outs
    core = lax.axis_index("core")
    other = lax.dynamic_slice_in_dim(outs[1], (1 - core) * (d // 2), d // 2, 1)
    return [*outs[:5], swap_core(other)]


LEAD = 2


def last_kernel(cfg, dq, dk, dv, tok, d_resid, norms, h_own, h_oth, resid, doc, two_norm, w_own, w_oth, b_own, b_oth, part_in, grads, *refs):
    d, comm = cfg
    out, mixed, red_in, red_in_p, red_at, red_at_p, sums, w, wb, parts, lsem = refs[:11]
    step = pl.program_id(0)
    last = pl.num_programs(0) - 1
    pro = last // 2
    half = 3 * d // 2
    q = d // 2
    hb = b_own.shape[0]
    nb = d // 128
    late = [
        pltpu.make_async_copy(b_own, wb.at[pl.ds(0, hb), :], lsem.at[2]),
        pltpu.make_async_copy(b_oth, wb.at[pl.ds(hb, hb), :], lsem.at[3]),
    ]
    if comm:
        send, recv, fi, sc, fa, vec, box = refs[11], refs[12], refs[13:19], refs[19:23], refs[23:29], refs[29], refs[30]
        fold_in = Fold(PIECES, part_in, fi[0], *fi[1:6], send, recv, 0)
        scat = Scatter(PIECES, grads, sc[0], sc[1], sc[2], sc[3], fa[0], send, recv, 4 * PIECES)
        fold_at = Fold(PIECES, fa[0], fa[0], *fa[1:6], send, recv, 10 * PIECES)
        base = 14 * PIECES

        def note(i, src, dst, to):
            return pltpu.make_async_remote_copy(
                src_ref=src, dst_ref=dst, send_sem=send.at[base + i], recv_sem=recv.at[base + i], device_id=to, device_id_type=MESH
            )

        near, far = Fold.peers()
        notes = [
            note(0, vec.at[0], box.at[0], peer("x")),
            note(1, vec.at[1], box.at[1], peer("y")),
            note(2, vec.at[2], box.at[2], peer("core")),
            note(3, vec.at[3], box.at[3], near),
            note(4, vec.at[4], box.at[4], far),
            note(5, vec.at[5], vec.at[5], near),
        ]

        def tick(k):
            if LEAD <= k + LEAD - 1 < PIECES:
                scat.begin(k + LEAD - 1)
            if 0 <= k - 1 < PIECES:
                scat.turn(k - 1)
            if 0 <= k - 2 < PIECES:
                scat.close(k - 2)
                fold_at.begin(k - 2)
            fold_in.tick(k - 1)
            fold_at.tick(k - 3)

        def norm_sum(k):
            if k < 3:
                notes[k].wait_recv()
                vec[k + 1] = vec[k] + box[k]
                if k < 2:
                    notes[k + 1].start()
                else:
                    pl.when(fold_in.end)(notes[3].start)
            elif k < 5:

                @pl.when(fold_in.mid)
                def _():
                    notes[k].wait_recv()
                    vec[k + 1] = vec[k] + box[k]
                    notes[k + 1].start()

            else:
                pl.when(fold_in.end)(notes[5].wait_recv)

    @pl.when(step == 0)
    def _():
        cps = [
            pltpu.make_async_copy(w_own, w.at[:, pl.ds(0, half)], lsem.at[0]),
            pltpu.make_async_copy(w_oth, w.at[:, pl.ds(half, half)], lsem.at[1]),
        ]
        for cp in cps:
            cp.start()
        if comm:
            loads = [pltpu.make_async_copy(part_in, fi[0], lsem.at[4]), pltpu.make_async_copy(grads, sc[0], lsem.at[5])]
            for cp in loads:
                cp.start()
            greet([peer("core"), peer("x"), peer("y")] + Fold.peers())
            for s in range(LEAD):
                scat.begin(s)
            fold_in.begin()
            for cp in loads:
                cp.wait()
        for cp in cps:
            cp.wait()
        for cp in late:
            cp.start()
        parts[0 : 2 * nb, :] = jnp.zeros((2 * nb, 128), f32)
        parts[2 * nb :, :] = two_norm[...]

    if comm:
        for k in range(1, last):

            @pl.when(step == k)
            def _():
                tick(k)

    @pl.when(step < pro)
    def _():
        both = jnp.concatenate([g[:, :q] for g in (dq, dk, dv)] + [g[:, q:] for g in (dq, dk, dv)], axis=1)
        dz = dot_nt(both, w[...])
        grad, g, b = layer_norm_back(tok[...].astype(f32), gain_row(norms, 0, d), dz)
        parts[0:nb, :] += flat_row(g)
        parts[nb : 2 * nb, :] += flat_row(b)
        out[...] = (d_resid[...] + grad).astype(bf16)

    @pl.when(step == pro)
    def _():
        for cp in late:
            cp.wait()
        if comm:
            vec[0] = parts[...]
            notes[0].start()

    @pl.when((step >= pro) & (step < last))
    def _():
        y = dot_nn(h_own[...], wb[:hb, :]) + dot_nn(h_oth[...], wb[hb:, :]) + resid[...]
        mixed[...] = jnp.where(doc[...] >= 0, y, 0.0).astype(bf16)

    @pl.when(step == last)
    def _():
        if comm:
            for k in range(2 * pro, PIECES + 6):
                tick(k)
                if k - 2 * pro < 6:
                    norm_sum(k - 2 * pro)
            fold_in.finish()
            scat.finish()
            fold_at.finish()
            for i in (0, 1, 2):
                notes[i].wait_send()
            pl.when(fold_in.end)(notes[3].wait_send)

            @pl.when(fold_in.mid)
            def _():
                notes[4].wait_send()
                notes[5].wait_send()

            sums[...] = vec[5]
            put_away(fi[4], red_in, fi[5], red_in_p, lsem)
            put_away(fa[4], red_at, fa[5], red_at_p, lsem)
        else:
            sums[...] = parts[...]


def flat_row(v):
    return jnp.concatenate([v[:, i * 128 : (i + 1) * 128] for i in range(v.shape[1] // 128)], axis=0)


def last_grad(grads3, tok, d_resid, norms, hidden, resid, doc_col, two_norm, own, oth, b_own, b_oth, part_in, grads, comm, tm=256):
    t, d = tok.shape
    pro = t // tm
    half = b_own.shape[0]
    one = lambda w, c=0: pl.BlockSpec((tm, w), lambda i: (jnp.minimum(i, pro - 1), c))
    two = lambda w, c=0: pl.BlockSpec((tm, w), lambda i: (jnp.clip(i - pro, 0, pro - 1), c))
    whole = lambda a: pl.BlockSpec(a.shape, lambda i: (0, 0))
    nv = 4 * d // 128
    share = (grads.shape[0] // 4, grads.shape[1])
    slots = 14 * PIECES + 6
    extra = []
    if comm:
        extra = [dma(slots), dma(slots)] + fold_scratch(*part_in.shape, PIECES) + scatter_scratch(*grads.shape, PIECES)
        extra += fold_scratch(*share, PIECES) + [pltpu.VMEM((6, nv, 128), f32), pltpu.VMEM((5, nv, 128), f32)]
    return pl.pallas_call(
        functools.partial(last_kernel, (d, comm)),
        grid=(2 * pro + 1,),
        out_shape=[sds((t, d), bf16), sds((t, d), bf16)] + [sds(part_in.shape, bf16)] * 2 + [sds(share, bf16)] * 2 + [sds((nv, 128), f32)],
        in_specs=[one(d)] * 5 + [whole(norms), two(half), two(half, 1), two(d), two(1), whole(two_norm)] + [ANY] * 6,
        out_specs=[one(d), two(d), ANY, ANY, ANY, ANY, pl.BlockSpec((nv, 128), lambda i: (0, 0))],
        scratch_shapes=[pltpu.VMEM((d, 3 * d), bf16), pltpu.VMEM((2 * half, d), bf16), pltpu.VMEM((nv, 128), f32), dma(6)] + extra,
        compiler_params=comm_params(7 if comm else None, 62),
        cost_estimate=cost(6 * t * d * d + 4 * t * d * half, 45e6),
        name="last_grad",
    )(*grads3, tok, d_resid, norms, hidden, hidden, resid, doc_col, two_norm, own, oth, b_own, b_oth, part_in, grads)


def pair_kernel(nb, a_mine, a_theirs, *refs):
    mine, theirs, out = refs[:nb], refs[nb], refs[nb + 1]
    wide = mine[0].shape[1]
    for j in range(nb):
        cols = slice(j * wide, (j + 1) * wide)
        acc = dot_tn(a_mine[...], mine[j][...]) + dot_tn(a_theirs[...], theirs[:, cols])
        out[:, cols] = acc.astype(bf16)


def pair_grad(a_mine, m, a_theirs, mine, wide, theirs, name, tm=256):
    t = a_mine.shape[0]
    nb = len(mine)
    a_spec = pl.BlockSpec((t, tm), lambda i: (0, i))
    b_spec = pl.BlockSpec((t, wide), lambda i: (0, 0))
    return pl.pallas_call(
        functools.partial(pair_kernel, nb),
        grid=(m // tm,),
        out_shape=sds((m, nb * wide), bf16),
        in_specs=[a_spec, a_spec] + [b_spec] * nb + [pl.BlockSpec((t, nb * wide), lambda i: (0, 0))],
        out_specs=pl.BlockSpec((tm, nb * wide), lambda i: (i, 0)),
        compiler_params=params(),
        cost_estimate=cost(4 * t * m * wide * nb, 14e6),
        name=name,
    )(a_mine, a_theirs, *mine, theirs)


def attention_grad_kernel(a, a_p, g1, g2, g3, theirs, att, att_p, low, low_p, out):
    wide = g1.shape[1]
    for j, g in enumerate((g1, g2, g3)):
        cols = slice(j * wide, (j + 1) * wide)
        out[:, cols] = (dot_tn(a[...], g[...]) + dot_tn(a_p[...], theirs[:, cols])).astype(bf16)
    out[:, 3 * wide :] = (dot_tn(att[...], low[...]) + dot_tn(att_p[...], low_p[...])).astype(bf16)


def attention_grads(a_one, a_one_p, mine, theirs, att, att_p, low, low_p, tm=256):
    t, d = a_one.shape
    half = d // 2
    nh = half // tm
    core = lambda: lax.axis_index("core")
    col = lambda f: pl.BlockSpec((t, tm), lambda i: (0, f(i)))
    held = lambda wd, f: pl.BlockSpec((t, wd), lambda i: (0, f()))
    own = lambda i: (i + core() * nh) % (2 * nh)
    theirs_at = lambda i: (i + (1 - core()) * nh) % (2 * nh)
    zero = lambda: 0
    return pl.pallas_call(
        attention_grad_kernel,
        grid=(d // tm,),
        out_shape=sds((d, 2 * d), bf16),
        in_specs=[col(lambda i: i), col(lambda i: i)] + [held(half, zero)] * 3 + [held(3 * half, zero)]
        + [col(own), col(theirs_at), held(half, core), held(half, zero)],
        out_specs=pl.BlockSpec((tm, 2 * d), lambda i: (i, 0)),
        compiler_params=params(),
        cost_estimate=cost(8 * t * d * d, 20e6),
        name="attention_grads",
    )(a_one, a_one_p, *mine, theirs, att, att_p, low, low_p)


def adam_update(g, m1, m2, wg, st, mn):
    first = BETA_ONE * m1[...] + (1.0 - BETA_ONE) * g
    second_hat = (BETA_TWO / (1.0 - BETA_TWO**STEPS)) * m2[...] + ((1.0 - BETA_TWO) / (1.0 - BETA_TWO**STEPS)) * g * g
    wg[...] = g
    st[...] = (-RATE / (1.0 - BETA_ONE**STEPS)) * first / (jnp.sqrt(second_hat) + ADAM_EPS)
    mn[...] = first


def flatten_columns(flat, own, oth, take, rows, stride, places, inv_root):
    first = lax.axis_index("core") == 0
    for col, lo, hi in places:
        a = own[take, col : col + 128].astype(f32) * inv_root
        b = oth[take, col : col + 128].astype(f32) * inv_root
        flat[pl.ds(lo, rows, stride=stride), :] = pick(first, a, b)
        flat[pl.ds(hi, rows, stride=stride), :] = pick(first, b, a)


def adam_kernel(plan, inv_root, own, oth, m1, m2, *refs):
    wg, st, mn, flat = refs[-4:]
    rows, stride, places = plan
    flatten_columns(flat, own, oth, slice(None), rows, stride, places, inv_root)
    adam_update(flat[...], m1, m2, wg, st, mn)


def adam_columns(own, oth, at, wide, m1, m2, prev, inv_root, first_row, rows, places):
    count = own.shape[0]
    nb = 2 * wide // 128
    blk = rows * nb
    assert first_row % blk == 0
    base = first_row // blk
    half = pl.BlockSpec((rows, wide), lambda i: (i, at))
    flat = pl.BlockSpec((blk, 128), lambda i: (base + i, 0))
    kernel = functools.partial(adam_kernel, (rows, nb, places), inv_root)
    return adam_call(kernel, (count // rows,), own, oth, m1, m2, prev, half, flat, blk, "adam")


def adam_call(kernel, grid, own, oth, m1, m2, prev, half, flat, blk, name):
    return pl.pallas_call(
        kernel,
        grid=grid,
        out_shape=[sds(m1.shape, f32)] * 3,
        in_specs=[half, half, flat, flat] + [ANY] * len(prev),
        out_specs=[flat] * 3,
        scratch_shapes=[pltpu.VMEM((blk, 128), f32)],
        input_output_aliases={4 + i: i for i in range(len(prev))},
        compiler_params=params(),
        cost_estimate=cost(0, own.size * 2 * 22),
        name=name,
    )(own, oth, m1, m2, *prev)


def adam_rows_kernel(inv_root, own, oth, m1, m2, *refs):
    wg, st, mn, flat = refs[-4:]
    g = pick(pl.program_id(0) == lax.axis_index("core"), own[...], oth[...]).astype(f32) * inv_root
    rows, width = g.shape
    nb = width // 128
    for w in range(nb):
        flat[pl.ds(w, rows, stride=nb), :] = g[:, w * 128 : (w + 1) * 128]
    adam_update(flat[...], m1, m2, wg, st, mn)


def adam_rows_halves(own, oth, m1, m2, prev, inv_root, first_row):
    count, width = own.shape
    rows = count // 4
    blk = rows * width // 128
    base = first_row // blk
    half = pl.BlockSpec((rows, width), lambda h, i: (i, 0))
    flat = pl.BlockSpec((blk, 128), lambda h, i: (base + h * 4 + i, 0))
    kernel = functools.partial(adam_rows_kernel, inv_root)
    return adam_call(kernel, (2, 4), own, oth, m1, m2, prev, half, flat, blk, "adam_rows")


def adam_tail_kernel(g, m1, m2, p1, p2, p3, wg, st, mn):
    adam_update(g[...], m1, m2, wg, st, mn)


def adam_tail(g, m1, m2, prev, first_row):
    rows = 8
    assert first_row % rows == 0 and g.shape[0] <= rows
    g = jnp.pad(g, ((0, rows - g.shape[0]), (0, 0)))
    flat = pl.BlockSpec((rows, 128), lambda i: (first_row // rows, 0))
    return pl.pallas_call(
        adam_tail_kernel,
        grid=(1,),
        out_shape=[sds(m1.shape, f32)] * 3,
        in_specs=[pl.BlockSpec((rows, 128), lambda i: (0, 0)), flat, flat] + [ANY] * 3,
        out_specs=[flat] * 3,
        input_output_aliases={3: 0, 4: 1, 5: 2},
        name="adam_norms",
    )(g, m1, m2, *prev)


def after(x, *deps):
    return lax.optimization_barrier((x, deps))[0]


def body(n, nz, tokens, cotangent, doc_ids, master, moment_one, moment_two):
    t, d = tokens.shape
    ff = (master.shape[0] * n - 4 * d) // (2 * d) - 2 * d
    me = lax.axis_index(("y", "x"))
    rows = d // n
    comm = n == 4

    lanes = master.reshape(-1, 128)
    w, o, norm_share = unpack_first(lanes, n, d, ff)
    doc_row = doc_ids.reshape(1, t)
    doc_col = doc_ids.reshape(t, 1)
    d_out = jnp.where(doc_col >= 0, cotangent, jnp.zeros((), bf16))
    if not comm:
        w, o = spread(w), spread(o)
        norm_share = lax.all_gather(master[-(4 * d // n) :].astype(bf16), ("y", "x"), axis=0, tiled=True)
        norm_share = norm_share.astype(f32).reshape(-1, 128)
    a_one, qkv, in_own, bk_own, w_own, w_oth, o_own, o_oth, norms = project_qkv(lanes, tokens, norm_share, w, o, n, ff, comm)
    att, lse, in_own, in_oth, a_one_p, d_out_p = attend(qkv, doc_row, doc_col, in_own, a_one, d_out, d, comm)
    resid, a_two, hidden, slope, bk_own, bk_oth, hid_p, att_p = middle(
        att, tokens, norms, o_own, o_oth, in_own, in_oth, bk_own, comm
    )
    scatter = lambda g: lax.psum_scatter(g, ("y", "x"), scatter_dimension=0, tiled=True)
    g_back = pair_grad(hidden, ff // 2, hid_p, [d_out], d, d_out_p, "grad_back")
    grad_back = scatter(g_back)
    d_pre, dp_p, a_two_p = pre_grad(after(d_out, g_back), slope, bk_own, bk_oth, a_two, comm)
    g_in = pair_grad(a_two, d, a_two_p, [d_pre], ff // 2, dp_p, "grad_in")
    grad_in = scatter(g_in)
    d_resid, low, d_att, gain_two, bias_two, low_p = two_grad(
        after(d_pre, g_in), resid, d_out, norms, in_own, in_oth, o_own, o_oth, comm
    )
    deep = nz == 4
    dq, dk, dv, dqkv_p, red_back = attend_back(
        qkv, d_att, att, lse, doc_row, doc_col, grad_back, d, comm, deep
    )
    g_at = attention_grads(a_one, a_one_p, [dq, dk, dv], dqkv_p, att, att_p, low, low_p)
    two_norm = jnp.concatenate([gain_two, bias_two]).reshape(-1, 128)
    full = comm and deep
    input_grad, mixed, red_in, red_in_p, red_at, red_at_p, sums = last_grad(
        [after(dq, g_at), dk, dv], tokens, d_resid, norms, hidden, resid, doc_col, two_norm, w_own, w_oth, bk_own, bk_oth,
        grad_in, g_at, full,
    )
    if not full:
        red_in, red_in_p = both_halves(grad_in, None, None, False)
        red_at, red_at_p = both_halves(scatter(g_at), None, None, False)
        sums = lax.psum(sums, ("z", "core", "y", "x"))

    inv_root = float(t * n * nz * 2) ** (-0.5)
    m1, m2 = moment_one.reshape(-1, 128), moment_two.reshape(-1, 128)
    nb = d // 128
    half = nb // 2
    hs = ff // n // 2
    r_qkv, r_out, r_in = rows * 3 * nb, rows * nb, rows * ff // 128
    back_at = r_qkv + r_out + r_in
    outs = adam_rows_halves(*red_back, m1, m2, [], inv_root, back_at)
    places = [(hs * j + q * 128, (2 * hs * j) // 128 + q, (2 * hs * j + hs) // 128 + q) for j in range(n) for q in range(hs // 128)]
    outs = adam_columns(red_in, red_in_p, 0, ff // 2, m1, m2, outs, inv_root, r_qkv + r_out, rows // 8, places)
    places = [((p * half + w) * 128, p * nb + w, p * nb + w + half) for p in range(3) for w in range(half)]
    outs = adam_columns(red_at, red_at_p, 0, 3 * d // 2, m1, m2, outs, inv_root, 0, rows // 8, places)
    places = [(w * 128, w, w + half) for w in range(half)]
    outs = adam_columns(red_at, red_at_p, 3, d // 2, m1, m2, outs, inv_root, r_qkv, rows // 2, places)
    per = 4 * nb // n
    norm_part = lax.dynamic_slice_in_dim(sums, group_index(n) * per, per, 0) * inv_root
    outs = adam_tail(norm_part, m1, m2, outs, back_at + ff // n * nb)
    weight_grad, step, moment = [o.reshape(-1) for o in outs]
    return mixed, input_grad, weight_grad, step, moment


def solution(mesh):
    dp, n = mesh.shape["dp"], mesh.shape["group"]
    fine = Mesh(mesh.devices.reshape(dp // 2, 2, n // 2, 2), ("z", "core", "y", "x"))
    tok = ("z", "core", "y", "x")
    flat = P(("y", "x"))
    in_specs = (P(tok, None), P(tok, None), P(tok), flat, flat, flat)
    out_specs = (P(tok, None), P(tok, None), flat, flat, flat)
    return jax.shard_map(
        functools.partial(body, n, dp // 2), mesh=fine, in_specs=in_specs, out_specs=out_specs, check_vma=False
    )
```

time: 1900 us -> 448 us (0.24)
  waiting for transfers between devices: 1110 us -> 0.04 us
  Pallas kernels: 0 us -> 421 us
  matrix products: 394 us -> 0 us
  local copies, waits for them, and re-layouts: 176 us -> 6.02 us
  other arithmetic: 139 us -> 4.2 us
  blocking collectives: 41.7 us -> 0 us
    unnamed x7 -> x2, waiting for transfers between devices: 856 us -> 0.03 us
    pallas_call x0 -> x16, Pallas kernels: none -> 421 us  [the longest x1 85.8 us: last_grad(): pl.pallas_call(functools.partial(last_kernel, (d, comm)), grid=(2 * pro +...]
    dot_general x26 -> x0, matrix products: 394 us -> none  [the longest x4 62 us: one_block(): jnp.einsum('qhd,khd->hqk', query_blk, keys_all, preferred_element_type=jn...]
    psum x1 -> x0, waiting for transfers between devices: 175 us -> none  [body(): summed = lax.psum((owned[0], owned[1], owned[2], owned[3], owned[4]), 'dp')]
    unnamed x143 -> x8, local copies, waits for them, and re-layouts: 90.5 us -> 3.71 us
    all_gather x4 -> x0, waiting for transfers between devices: 79.4 us -> none  [the longest x1 68.5 us: body(): lax.all_gather(pieces[0], 'group', axis=0, tiled=True)]
    convert_element_type x6 -> x0, other arithmetic: 65.8 us -> none  [the longest x2 55.6 us: one_block(): score_grad = (prob_full * (prob_grad - inner)).astype(jnp.bfloat16)]
    reduce_sum x9 -> x0, other arithmetic: 44.3 us -> none  [the longest x2 31.2 us: one_block(): totals = jnp.sum(exp_scores, axis=-1, keepdims=True)]
  transfers between devices with their start and end apart: 6 -> 2, of which waited for: 4 -> 0; matrix products, arithmetic and copies ran while one was open for 14% -> 0% of each run, Pallas kernels for 0% -> 29%
where the time goes in v2:
time: 448 us; the launch traced here: 446 us
  Pallas kernels  421 us (94%)
  between operations  14.1 us (3%)
  local copies, waits for them, and re-layouts  6.02 us (1%)
    pallas_call x1, Pallas kernels, last_grad(): pl.pallas_call(functools.partial(last_kernel, (d, comm)), grid=(2 * pro +...  85.8 us
    pallas_call x1, Pallas kernels, attend_back(): pl.pallas_call(functools.partial(attend_back_kernel, (hd, comm, deep)), g...  57.9 us
    pallas_call x1, Pallas kernels, project_qkv(): pl.pallas_call(functools.partial(qkv_kernel, (n, d, comm)), grid=(UNPACK_...  55.3 us
    pallas_call x1, Pallas kernels, middle(): pl.pallas_call(functools.partial(middle_kernel, (d, tm, blk, comm)), grid...  45.5 us
    pallas_call x1, Pallas kernels, attend(): pl.pallas_call(functools.partial(attend_kernel, (hd, comm)), grid=(pairs,...  44.2 us
    pallas_call x4, Pallas kernels, adam_call(): pl.pallas_call(kernel, grid=grid, out_shape=[sds(m1.shape, f32)] * 3, in_...  41.1 us
    pallas_call x2, Pallas kernels, pair_grad(): pl.pallas_call(functools.partial(pair_kernel, nb), grid=(m // tm,), out_s...  28.7 us
    pallas_call x1, Pallas kernels, two_grad(): pl.pallas_call(functools.partial(two_grad_kernel, comm), grid=(t // tm,),...  24.3 us
  transfers between devices with their start and end apart: 2, of which 0 were waited for; matrix products, arithmetic and copies ran while one was open for 0% of the time, Pallas kernels for 29%

profile of v2, /device:TPU:0, one launch (start us, length us, event | category | flops | bytes accessed | tf_op | source)
XLA Modules:
  0.0 445.9 jit_solution(6084483265417541339)
XLA Ops:
  7.2 0.0 reduce-scatter.3.cloned.1.call-start
  7.2 0.7 broadcast_compare_fusion
  7.9 1.7 copy.27.doc_col.doc
  9.6 0.0 copy-start
  9.6 4.4 unpack.1
  14.0 0.0 copy-done
  14.0 1.5 broadcast_select_fusion.d_out.refs_0_
  15.6 55.3 %qkv.1 = (bf16[1024,1024]{1,0:T(8,128)(2,1)}, bf16[1024,3072]{1,0:T(8,128)(2,1)}, bf16[1024,2048]{1,0:T(8,128)(2,1)}, bf16[2048,1024]{1,0:T(8,128)(2,1)}, bf16[1...) custom-call(bf16[1024,1024]{1,0:T(8,128)(2,1)} %tok.5, ...), custom_call_target="tpu_custom_call", output_to_operand_aliasing={{4}: (4, {}), {6}: (6, {})} | custom-call | flops 6442450944 | bytes 40000000 | tf_op jit(solution)/shard_map/qkv/pallas_call | solution.py:485
  70.9 44.2 %attend.1 = (bf16[1024,1024]{1,0:T(8,128)(2,1)}, f32[8,2,1024]{2,1,0:T(2,128)}, bf16[1024,2048]{1,0:T(8,128)(2,1)}, bf16[1024,2048]{1,0:T(8,128)(2,1)}, bf16[102...) custom-call(bf16[1024,3072]{1,0:T(8,128)(2,1)} %get-tuple-element.74.q.k.v, ...), custom_call_target="tpu_custom_call", output_to_operand_aliasing={{2}: (5, {})} | custom-call | flops 8589934592 | bytes 10000000 | tf_op jit(solution)/shard_map/attend/pallas_call | solution.py:590
  115.1 45.5 %middle.1 = (f32[1024,1024]{1,0:T(8,128)}, bf16[1024,1024]{1,0:T(8,128)(2,1)}, bf16[1024,4096]{1,0:T(8,128)(2,1)}, bf16[1024,4096]{1,0:T(8,128)(2,1)}, bf16[2048...) custom-call(bf16[1024,1024]{1,0:T(8,128)(2,1)} %get-tuple-element.77, ...), custom_call_target="tpu_custom_call", output_to_operand_aliasing={{4}: (8, {})} | custom-call | flops 10737418240 | bytes 44000000 | tf_op jit(solution)/shard_map/middle/pallas_call | solution.py:853
  160.6 14.1 %grad_back.1 = bf16[2048,1024]{1,0:T(8,128)(2,1)} custom-call(bf16[1024,4096]{1,0:T(8,128)(2,1)} %get-tuple-element.84.a_mine.h_own.h_oth, bf16[1024,2048]{1,0:T(8,128)(2,1)} %get-tuple-element.85.a_theirs, bf16[1024,1024]{1,0:T(8,128)(2,1)} %broadcast_select_fusion.d_out.refs_0_, bf16[1024,1024]{1,0:T(8,128)(2,1)} %get-tuple-element.86.refs_1_), custom_call_target="tpu_custom_call" | custom-call | flops 8589934592 | bytes 14000000 | tf_op jit(solution)/shard_map/grad_back/pallas_call | solution.py:1210
  174.7 0.0 reduce-scatter.3.cloned.1.call-update
  174.7 0.0 reduce-scatter.5.cloned.1.call-start
  174.8 17.4 %pre_grad.1 = (bf16[1024,4096]{1,0:T(8,128)(2,1)}, bf16[1024,2048]{1,0:T(8,128)(2,1)}, bf16[1024,1024]{1,0:T(8,128)(2,1)}) custom-call(bf16[1024,1024]{1,0:T(8,128)(2,1)} %broadcast_select_fusion.d_out.refs_0_, bf16[1024,4096]{1,0:T(8,128)(2,1)} %get-tuple-element.88.slope, bf16[2048,1024]{1,0:T(8,128)(2,1)} %get-tuple-element.89.w_own.b_own, ...), custom_call_target="tpu_custom_call" | custom-call | flops 8589934592 | bytes 28000000 | tf_op jit(solution)/shard_map/pre_grad/pallas_call | solution.py:920
  192.2 14.6 %grad_in.1 = bf16[1024,2048]{1,0:T(8,128)(2,1)} custom-call(bf16[1024,1024]{1,0:T(8,128)(2,1)} %get-tuple-element.91.a_two.a_mine, bf16[1024,1024]{1,0:T(8,128)(2,1)} %get-tuple-element.93.a_theirs, bf16[1024,4096]{1,0:T(8,128)(2,1)} %get-tuple-element.95.refs_0_.d_pre, bf16[1024,2048]{1,0:T(8,128)(2,1)} %get-tuple-element.94.refs_1_), custom_call_target="tpu_custom_call" | custom-call | flops 8589934592 | bytes 14000000 | tf_op jit(solution)/shard_map/grad_in/pallas_call | solution.py:1210
  206.8 0.0 reduce-scatter.5.cloned.1.call-update
  206.8 24.3 %two_grad.1 = (f32[1024,1024]{1,0:T(8,128)}, bf16[1024,1024]{1,0:T(8,128)(2,1)}, bf16[1024,1024]{1,0:T(8,128)(2,1)}, f32[1,1024]{1,0:T(1,128)}, f32[1,1024]{1,0:T(1,128)}, /*index=5*/bf16[1024,512]{1,0:T(8,128)(2,1)}) custom-call(bf16[1024,4096]{1,0:T(8,128)(2,1)} %get-tuple-element.95.refs_0_.d_pre, f32[1024,1024]{1,0:T(8,128)} %get-tuple-element.96.resid, ...), custom_call_target="tpu_custom_call" | custom-call | flops 10737418240 | bytes 34000000 | tf_op jit(solution)/shard_map/two_grad/pallas_call | solution.py:997
  231.1 0.7 pad_maximum_fusion
  231.8 0.6 reshape.42.two_norm
  232.4 0.0 reduce-scatter.3.cloned.1.call-done.part_sum
  232.4 57.9 %attend_back.1 = (bf16[1024,1024]{1,0:T(8,128)(2,1)}, bf16[1024,1024]{1,0:T(8,128)(2,1)}, bf16[1024,1024]{1,0:T(8,128)(2,1)}, bf16[1024,1536]{1,0:T(8,128)(2,1)}...) custom-call(bf16[1024,3072]{1,0:T(8,128)(2,1)} %get-tuple-element.74.q.k.v, ...), custom_call_target="tpu_custom_call" | custom-call | flops 21474836480 | bytes 16000000 | tf_op jit(solution)/shard_map/attend_back/pallas_call | solution.py:731
  290.3 15.4 %attention_grads.1.grads = bf16[1024,2048]{1,0:T(8,128)(2,1)} custom-call(bf16[1024,1024]{1,0:T(8,128)(2,1)} %get-tuple-element.76.a_one.a, bf16[1024,1024]{1,0:T(8,128)(2,1)} %get-tuple-element.100.a_p, bf16[1024,1024]{1,0:T(8,128)(2,1)} %get-tuple-element.107.g1.dq, bf16[1024,1024]{1,0:T(8,128)(2,1)} %get-tuple-element.101.g2.dk, ...), custom_call_target="tpu_custom_call" | custom-call | flops 8589934592 | bytes 20000000 | tf_op jit(solution)/shard_map/attention_grads/pallas_call | solution.py:1240
  305.7 0.0 reduce-scatter.5.cloned.1.call-done.part_in
  305.7 85.8 %last_grad.1 = (bf16[1024,1024]{1,0:T(8,128)(2,1)}, bf16[1024,1024]{1,0:T(8,128)(2,1)}, bf16[256,2048]{1,0:T(8,128)(2,1)}, bf16[256,2048]{1,0:T(8,128)(2,1)}, bf...) custom-call(bf16[1024,1024]{1,0:T(8,128)(2,1)} %get-tuple-element.107.g1.dq, ...), custom_call_target="tpu_custom_call" | custom-call | flops 15032385536 | bytes 45000000 | tf_op jit(solution)/shard_map/last_grad/pallas_call | solution.py:1183
  391.5 1.3 dynamic-slice_multiply_fusion.g
  392.8 13.3 %adam_rows.1 = (f32[24584,128]{1,0:T(8,128)}, f32[24584,128]{1,0:T(8,128)}, f32[24584,128]{1,0:T(8,128)}) custom-call(bf16[512,1024]{1,0:T(8,128)(2,1)} %get-tuple-element.120.own, bf16[512,1024]{1,0:T(8,128)(2,1)} %get-tuple-element.121.oth, f32[24584,128]{1,0:T(8,128)} %bitcast.8, f32[24584,128]{1,0:T(8,128)} %bitcast.13), custom_call_target="tpu_custom_call" | custom-call | bytes 23068672 | tf_op jit(solution)/shard_map/adam_rows/pallas_call | solution.py:1290
  406.0 13.2 %adam.3 = (f32[24584,128]{1,0:T(8,128)}, f32[24584,128]{1,0:T(8,128)}, f32[24584,128]{1,0:T(8,128)}) custom-call(bf16[256,2048]{1,0:T(8,128)(2,1)} %get-tuple-element.118.own, bf16[256,2048]{1,0:T(8,128)(2,1)} %get-tuple-element.119.oth, f32[24584,128]{1,0:T(8,128)} %bitcast.9, ...), custom_call_target="tpu_custom_call", output_to_operand_aliasing={{0}: (4, {}), {1}: (5, {}), {2}: (6, {})} | custom-call | bytes 23068672 | tf_op jit(solution)/shard_map/adam/pallas_call | solution.py:1290
  419.2 10.7 %adam.4 = (f32[24584,128]{1,0:T(8,128)}, f32[24584,128]{1,0:T(8,128)}, f32[24584,128]{1,0:T(8,128)}) custom-call(bf16[256,2048]{1,0:T(8,128)(2,1)} %get-tuple-element.116.own, bf16[256,2048]{1,0:T(8,128)(2,1)} %get-tuple-element.117.oth, f32[24584,128]{1,0:T(8,128)} %bitcast.10, ...), custom_call_target="tpu_custom_call", output_to_operand_aliasing={{0}: (4, {}), {1}: (5, {}), {2}: (6, {})} | custom-call | bytes 23068672 | tf_op jit(solution)/shard_map/adam/pallas_call | solution.py:1290
  429.9 3.9 adam.5
  433.8 0.0 copy-start.2
  433.8 1.5 adam_norms.1
  435.3 0.0 copy-start.1
  435.3 0.1 copy-done.2
  435.5 1.3 copy.48
  436.8 0.9 copy-done.1
  437.7 1.3 copy.49
Async XLA Ops:
  7.2 225.2 %reduce-scatter.3.cloned.1.call-start = ((), (), s32[]{:S(2)}) async-start(), calls=%async_computation.2 | async-start | bytes 5242880 | tf_op jit(solution)/shard_map/reduce_scatter | solution.py:1370
  9.6 4.4 copy-start
  174.7 131.0 %reduce-scatter.5.cloned.1.call-start = ((), (), s32[]{:S(2)}) async-start(), calls=%async_computation.3 | async-start | bytes 5242880 | tf_op jit(solution)/shard_map/reduce_scatter | solution.py:1370
  433.8 1.6 copy-start.2
  435.3 2.4 copy-start.1
Sparse Core Ops, SparseCore 0:
  174.9 53.0 reduce-scatter.2
  231.7 52.7 reduce-scatter.4
